TPU v7x, 32 devices: a whole 2x2x4 slice. The times are simulated.
32 devices in a mesh: wide: 8 (over y, x, core), narrow: 4 (over z).
Axes of the slice: x: 2, y: 2, z: 4, core: 2. Of those that a mesh axis runs over, the one named last changes fastest.
Arguments:
- tokens: bfloat16 [32768, 1024], P(('wide', 'narrow')), may hold values from -6 to 6
- cotangent: bfloat16 [32768, 1024], P(('wide', 'narrow')), may hold values from -6 to 6
- gain_mix: bfloat16 [1024], P(('wide', 'narrow')), may hold values from 0.099609375 to 1.8984375
- in_weight: bfloat16 [1024, 3072], P(('wide', 'narrow')), may hold values from -0.1875 to 0.1875
- conv_taps: bfloat16 [3, 1024], P(None, ('wide', 'narrow')), may hold values from -3 to 3
- out_weight: bfloat16 [1024, 1024], P(('wide', 'narrow')), may hold values from -0.1875 to 0.1875
- gain_ffn: bfloat16 [1024], P(('wide', 'narrow')), may hold values from 0.099609375 to 1.8984375
- gate_weight: bfloat16 [1024, 4608], P(('wide', 'narrow')), may hold values from -0.1875 to 0.1875
- up_weight: bfloat16 [1024, 4608], P(('wide', 'narrow')), may hold values from -0.1875 to 0.1875
- down_weight: bfloat16 [4608, 1024], P(('wide', 'narrow')), may hold values from -0.1875 to 0.1875
- doc_lengths: int32 [8, 16], replicated, may hold values from 1 to 2048, as said below
- valid_count: int32 [8], replicated, may hold values from 3584 to 4096
Outputs:
- output: float32 [32768, 1024], P(('wide', 'narrow'))
- grad_tokens: float32 [32768, 1024], P(('wide', 'narrow'))
- grad_gain_mix: float32 [1024], P(('wide', 'narrow'))
- grad_in_weight: float32 [1024, 3072], P(('wide', 'narrow'))
- grad_conv_taps: float32 [3, 1024], P(None, ('wide', 'narrow'))
- grad_out_weight: float32 [1024, 1024], P(('wide', 'narrow'))
- grad_gain_ffn: float32 [1024], P(('wide', 'narrow'))
- grad_gate_weight: float32 [1024, 4608], P(('wide', 'narrow'))
- grad_up_weight: float32 [1024, 4608], P(('wide', 'narrow'))
- grad_down_weight: float32 [4608, 1024], P(('wide', 'narrow'))
Inputs may be any that keep to these rules, and one draw needn't show every extreme that they name: Each row of doc_lengths fills its packed row of 4096 tokens exactly; the longest document of every row has exactly 2048 tokens; no document starts at a place p > 0 with p % 1024 < 2.
All inputs are finite; a program needn't handle non-finite values.
Results may differ from a plain program's by a relative error of at most 0.0084.
Values may be sent and summed in bfloat16 or wider, within the bound.
A program may use at most 320 MiB of HBM per device.

v0:
```python
import jax
import jax.numpy as jnp
from jax import lax
from jax.sharding import PartitionSpec as P

ROW_LEN = 4096


epsilon = 1e-05


def passed_along(array, axis, by):
    size = lax.axis_size(axis)
    pairs = [(i, i + by) for i in range(size) if 0 <= i + by < size]
    return lax.ppermute(array, axis, pairs)


def rms_forward(values, gain_vec):
    inv_rms = lax.rsqrt(jnp.mean(values * values, axis=1, keepdims=True) + epsilon)
    return (values * inv_rms * gain_vec[None, :], inv_rms)


def rms_backward(values, inv_rms, gain_vec, grad_normed):
    weighted = grad_normed * gain_vec[None, :]
    features = values.shape[1]
    total_dot = jnp.sum(weighted * values, axis=1, keepdims=True)
    grad_values = inv_rms * weighted - values * (inv_rms * inv_rms * inv_rms) * total_dot / features
    grad_gain = jnp.sum(grad_normed * values * inv_rms, axis=0)
    return (grad_values, grad_gain)


def outer_sum(left, right):
    return lax.dot_general(
        left, right, (((0,), (0,)), ((), ())), preferred_element_type=jnp.float32
    )


def back_product(grad_low, weight_mat):
    return lax.dot_general(
        grad_low, weight_mat, (((1,), (1,)), ((), ())), preferred_element_type=jnp.float32
    )


def doc_masks(doc_lengths, valid_count, first_pos, tok_count):
    packed_row = first_pos // ROW_LEN
    lengths = lax.dynamic_index_in_dim(doc_lengths, packed_row, 0, keepdims=False)
    limit_count = lax.dynamic_index_in_dim(valid_count, packed_row, 0, keepdims=False)
    offsets = jnp.cumsum(lengths) - lengths
    places = first_pos % ROW_LEN + jnp.arange(tok_count, dtype=jnp.int32)
    begins = jnp.any(offsets[None, :] == places[:, None], axis=1)
    before = jnp.any(offsets[None, :] == places[:, None] - 1, axis=1)
    keep_one = jnp.where(begins, 0.0, 1.0).astype(jnp.float32)
    keep_two = jnp.where(begins | before, 0.0, 1.0).astype(jnp.float32)
    live_mask = jnp.where(places < limit_count, 1.0, 0.0).astype(jnp.float32)
    return (keep_one[:, None], keep_two[:, None], live_mask[:, None])


def shards(
    tokens,
    cotangent,
    gain_mix,
    in_weight,
    conv_taps,
    out_weight,
    gain_ffn,
    gate_weight,
    up_weight,
    down_weight,
    doc_lengths,
    valid_count,
):
    tok_count = tokens.shape[0]
    first_pos = lax.axis_index(("wide", "narrow")) * tok_count
    keep_one, keep_two, live_mask = doc_masks(doc_lengths, valid_count, first_pos, tok_count)
    full_gm, w_in, full_taps, w_out, full_gf, w_gate, w_up, w_down = (
        lax.all_gather(gain_mix, ("wide", "narrow"), axis=0, tiled=True),
        lax.all_gather(in_weight, ("wide", "narrow"), axis=0, tiled=True),
        lax.all_gather(conv_taps, ("wide", "narrow"), axis=1, tiled=True),
        lax.all_gather(out_weight, ("wide", "narrow"), axis=0, tiled=True),
        lax.all_gather(gain_ffn, ("wide", "narrow"), axis=0, tiled=True),
        lax.all_gather(gate_weight, ("wide", "narrow"), axis=0, tiled=True),
        lax.all_gather(up_weight, ("wide", "narrow"), axis=0, tiled=True),
        lax.all_gather(down_weight, ("wide", "narrow"), axis=0, tiled=True),
    )
    mix_gain = full_gm.astype(jnp.float32)
    ffn_gain = full_gf.astype(jnp.float32)
    taps = full_taps.astype(jnp.float32)
    features = tokens.shape[1]
    tok_float = tokens.astype(jnp.float32)
    normed_mix, inv_mix = rms_forward(tok_float, mix_gain)
    normed_low = normed_mix.astype(jnp.bfloat16)
    projected = jnp.dot(normed_low, w_in, preferred_element_type=jnp.float32)
    b_part = projected[:, :features]
    c_part = projected[:, features : 2 * features]
    x_part = projected[:, 2 * features :]
    gated = b_part * x_part
    edge_rows = passed_along(gated[-2:], "narrow", 1)
    extended = jnp.concatenate([edge_rows, gated], axis=0)
    lag_one = keep_one * extended[1:-1]
    lag_two = keep_two * extended[:-2]
    conv_out = taps[2][None, :] * gated + taps[1][None, :] * lag_one + taps[0][None, :] * lag_two
    mixed_low = (c_part * conv_out).astype(jnp.bfloat16)
    hidden_res = tok_float + jnp.dot(mixed_low, w_out, preferred_element_type=jnp.float32)
    normed_ffn, inv_ffn = rms_forward(hidden_res, ffn_gain)
    ffn_low = normed_ffn.astype(jnp.bfloat16)
    gate_val = jnp.dot(ffn_low, w_gate, preferred_element_type=jnp.float32)
    up_val = jnp.dot(ffn_low, w_up, preferred_element_type=jnp.float32)
    sigmoid_gate = jax.nn.sigmoid(gate_val)
    silu_val = gate_val * sigmoid_gate
    act_low = (silu_val * up_val).astype(jnp.bfloat16)
    ffn_out = jnp.dot(act_low, w_down, preferred_element_type=jnp.float32)
    output = live_mask * (hidden_res + ffn_out)
    again_gm, w_in, again_taps, w_out, again_gf, w_gate, w_up, w_down = (
        lax.all_gather(gain_mix, ("wide", "narrow"), axis=0, tiled=True),
        lax.all_gather(in_weight, ("wide", "narrow"), axis=0, tiled=True),
        lax.all_gather(conv_taps, ("wide", "narrow"), axis=1, tiled=True),
        lax.all_gather(out_weight, ("wide", "narrow"), axis=0, tiled=True),
        lax.all_gather(gain_ffn, ("wide", "narrow"), axis=0, tiled=True),
        lax.all_gather(gate_weight, ("wide", "narrow"), axis=0, tiled=True),
        lax.all_gather(up_weight, ("wide", "narrow"), axis=0, tiled=True),
        lax.all_gather(down_weight, ("wide", "narrow"), axis=0, tiled=True),
    )
    mix_gain = again_gm.astype(jnp.float32)
    ffn_gain = again_gf.astype(jnp.float32)
    taps = again_taps.astype(jnp.float32)
    grad_res = live_mask * cotangent.astype(jnp.float32)
    grad_ffn_low = grad_res.astype(jnp.bfloat16)
    grad_down = outer_sum(act_low, grad_ffn_low)
    grad_act = back_product(grad_ffn_low, w_down)
    grad_gate_low = (
        grad_act * up_val * sigmoid_gate * (1.0 + gate_val * (1.0 - sigmoid_gate))
    ).astype(jnp.bfloat16)
    grad_up_low = (grad_act * silu_val).astype(jnp.bfloat16)
    grad_gate = outer_sum(ffn_low, grad_gate_low)
    grad_up = outer_sum(ffn_low, grad_up_low)
    grad_nffn = back_product(grad_gate_low, w_gate) + back_product(grad_up_low, w_up)
    grad_hnorm, grad_gf = rms_backward(hidden_res, inv_ffn, ffn_gain, grad_nffn)
    grad_hidden = grad_res + grad_hnorm
    grad_mix_low = grad_hidden.astype(jnp.bfloat16)
    grad_out = outer_sum(mixed_low, grad_mix_low)
    grad_mixed = back_product(grad_mix_low, w_out)
    grad_c = grad_mixed * conv_out
    grad_conv = grad_mixed * c_part
    grad_taps = jnp.stack(
        [
            jnp.sum(grad_conv * lag_two, axis=0),
            jnp.sum(grad_conv * lag_one, axis=0),
            jnp.sum(grad_conv * gated, axis=0),
        ],
        axis=0,
    )
    lag_grad_one = taps[1][None, :] * keep_one * grad_conv
    lag_grad_two = taps[0][None, :] * keep_two * grad_conv
    grad_ext = (
        jnp.pad(taps[2][None, :] * grad_conv, ((2, 0), (0, 0)))
        + jnp.pad(lag_grad_one, ((1, 1), (0, 0)))
        + jnp.pad(lag_grad_two, ((0, 2), (0, 0)))
    )
    from_right = passed_along(grad_ext[:2], "narrow", -1)
    grad_gated = jnp.concatenate([grad_ext[2:-2], grad_ext[-2:] + from_right], axis=0)
    grad_b = grad_gated * x_part
    grad_x = grad_gated * b_part
    grad_proj_low = jnp.concatenate([grad_b, grad_c, grad_x], axis=1).astype(jnp.bfloat16)
    grad_in = outer_sum(normed_low, grad_proj_low)
    grad_nmix = back_product(grad_proj_low, w_in)
    grad_tnorm, grad_gm = rms_backward(tok_float, inv_mix, mix_gain, grad_nmix)
    grad_tokens = grad_hidden + grad_tnorm
    sum_gm, sum_in, sum_taps, sum_out, sum_gf, sum_gate, sum_up, sum_down = (
        lax.psum_scatter(grad_gm, ("wide", "narrow"), scatter_dimension=0, tiled=True),
        lax.psum_scatter(grad_in, ("wide", "narrow"), scatter_dimension=0, tiled=True),
        lax.psum_scatter(grad_taps, ("wide", "narrow"), scatter_dimension=1, tiled=True),
        lax.psum_scatter(grad_out, ("wide", "narrow"), scatter_dimension=0, tiled=True),
        lax.psum_scatter(grad_gf, ("wide", "narrow"), scatter_dimension=0, tiled=True),
        lax.psum_scatter(grad_gate, ("wide", "narrow"), scatter_dimension=0, tiled=True),
        lax.psum_scatter(grad_up, ("wide", "narrow"), scatter_dimension=0, tiled=True),
        lax.psum_scatter(grad_down, ("wide", "narrow"), scatter_dimension=0, tiled=True),
    )
    return (
        output,
        grad_tokens,
        sum_gm,
        sum_in,
        sum_taps,
        sum_out,
        sum_gf,
        sum_gate,
        sum_up,
        sum_down,
    )


def solution(mesh):
    placed = (
        P(("wide", "narrow"), None),
        P(("wide", "narrow"), None),
        P(("wide", "narrow")),
        P(("wide", "narrow"), None),
        P(None, ("wide", "narrow")),
        P(("wide", "narrow"), None),
        P(("wide", "narrow")),
        P(("wide", "narrow"), None),
        P(("wide", "narrow"), None),
        P(("wide", "narrow"), None),
        P(),
        P(),
    )
    return jax.shard_map(
        shards,
        mesh=mesh,
        in_specs=placed,
        out_specs=(
            P(("wide", "narrow"), None),
            P(("wide", "narrow"), None),
            P(("wide", "narrow")),
            P(("wide", "narrow"), None),
            P(None, ("wide", "narrow")),
            P(("wide", "narrow"), None),
            P(("wide", "narrow")),
            P(("wide", "narrow"), None),
            P(("wide", "narrow"), None),
            P(("wide", "narrow"), None),
        ),
        check_vma=False,
    )
```

profile of v0, /device:TPU:0, one launch (start us, length us, event | category | flops | bytes accessed | tf_op | source)
XLA Modules:
  0.0 1554.4 jit_solution(15098074451749255470)
XLA Ops:
  13.2 42.2 %all-reduce.8 = (bf16[1024]{0:T(1024)(128)(2,1)S(1)}, bf16[1024]{0:T(1024)(128)(2,1)S(1)}) all-reduce(bf16[1024]{0:T(1024)(128)(2,1)S(1)} %dynamic-update-slice, bf16[1024]{0:T(1024)(128)(2,1)S(1)} %dynamic-update-slice.1), channel_id=1, replica_groups=mesh['wide'=8,'narrow'=4] {'wide','narrow'}, use_global_device_ids=true, to_apply=%add.3 | all-reduce | flops 2048 | bytes 8192
  55.4 2.9 copy.61
  58.3 66.5 %all-gather = bf16[32,32,3]{1,2,0:T(4,128)(2,1)S(1)} all-gather(bf16[1,32,3]{1,2,0:T(4,128)(2,1)S(1)} %bitcast.51), channel_id=1, replica_groups=mesh['wide'=8,'narrow'=4] {'wide','narrow'}, dimensions={0}, use_global_device_ids=true | all-gather | bytes 6336 | tf_op jit(solution)/shard_map/all_gather | solution.py:78
  127.5 9.2 fusion.26
  136.7 1.4 slice_multiply_fusion
  138.1 3.6 copy-done
  141.7 2.0 copy-done.1
  143.7 2.1 collective-permute-start
  146.5 4.0 copy.64
  150.5 9.4 multiply_convert_fusion.7
  159.9 4.8 multiply_reduce_fusion.5
  164.7 1.9 copy-done.6
  167.1 58.0 %all-gather.11.cloned.1.call-done = bf16[1024,4608]{1,0:T(8,128)(2,1)} async-done(((bf16[32,4608]{1,0:T(8,128)(2,1)}), bf16[1024,4608]{1,0:T(8,128)(2,1)}) %all-gather.11.cloned.1.call-update) | async-done | bytes 9437200 | tf_op jit(solution)/shard_map/all_gather | solution.py:81
  225.1 16.3 %fusion.32 = f32[1024,4608]{1,0:T(8,128)} fusion(bf16[1024,1024]{0,1:T(8,128)(2,1)S(1)} %multiply_convert_fusion.6, bf16[1024,4608]{1,0:T(8,128)(2,1)} %all-gather.11.cloned.1.call-done), kind=kOutput, calls=%fused_computation.81 | convolution fusion | flops 9663676416 | bytes 30408704 | tf_op jit(solution)/shard_map/dot_general | solution.py:106
  241.4 67.0 %all-gather.13.cloned.1.call-done = bf16[1024,4608]{1,0:T(8,128)(2,1)} async-done(((bf16[32,4608]{1,0:T(8,128)(2,1)}), bf16[1024,4608]{1,0:T(8,128)(2,1)}) %all-gather.13.cloned.1.call-update) | async-done | bytes 9437200 | tf_op jit(solution)/shard_map/all_gather | solution.py:82
  308.4 17.4 %fusion.33 = f32[1024,4608]{1,0:T(8,128)} fusion(bf16[1024,1024]{0,1:T(8,128)(2,1)} %copy-done.11, bf16[1024,4608]{1,0:T(8,128)(2,1)} %all-gather.13.cloned.1.call-done), kind=kOutput, calls=%fused_computation.82 | convolution fusion | flops 9663676416 | bytes 30408704 | tf_op jit(solution)/shard_map/dot_general | solution.py:107
  325.8 65.9 %all-gather.15.cloned.1.call-done = bf16[4608,1024]{1,0:T(8,128)(2,1)} async-done(((bf16[144,1024]{1,0:T(8,128)(2,1)}), bf16[4608,1024]{1,0:T(8,128)(2,1)}) %all-gather.15.cloned.1.call-update) | async-done | bytes 9437200 | tf_op jit(solution)/shard_map/all_gather | solution.py:83
  391.7 31.3 %multiply_convert_fusion = (bf16[1024,4608]{1,0:T(8,128)(2,1)}, bf16[1024,4608]{1,0:T(8,128)(2,1)}, bf16[1024,4608]{1,0:T(8,128)(2,1)}) fusion(f32[1024,4608]{1,0:T(8,128)} %fusion.32, f32[1024,4608]{1,0:T(8,128)} %fusion.33, bf16[4608,1024]{1,0:T(8,128)(2,1)} %all-gather.15.cloned.1.call-done, bf16[1024,1024]{0,1:T(8,128)(2,1)S(1)} %copy-done.9, ...), kind=kOutput, calls=%fused_computation | convolution fusion | flops 9737601024 | bytes 77598720 | tf_op jit(solution)/shard_map/dot_general | solution.py:39
  423.0 14.4 fusion.34
  437.4 16.5 %multiply_reduce_fusion = (f32[1024]{0:T(1024)}, f32[1024]{0:T(1024)S(1)}, f32[1024,1024]{0,1:T(8,128)S(1)}) fusion(f32[1024,1024]{0,1:T(8,128)S(1)} %copy-done.7, f32[1024]{0:T(1024)S(1)} %get-tuple-element.91, f32[1024]{0:T(1024)S(1)} %convert_element_type.54, f32[1024,1024]{0,1:T(8,128)S(1)} %fusion.34, bf16[1024,4608]{1,0:T(8,128)(2,1)} %get-tuple-element.76, ...), kind=kOutput, calls=%fused_computation.30 | convolution fusion | flops 9671014400 | bytes 31473664 | tf_op jit(solution)/shard_map/dot_general | solution.py:39
  453.9 1.4 subtract_add_fusion
  455.5 2.4 fusion.23
  457.9 1.3 copy-done.2
  459.2 1.3 copy-done.5
  460.5 6.0 multiply_reduce_fusion.3
  467.6 6.6 fusion.21
  475.0 2.8 broadcast_multiply_fusion
  477.8 1.5 collective-permute-start.1
  479.4 2.0 pad_add_fusion
  481.9 1.5 collective-permute-done.1
  483.5 4.5 multiply_convert_fusion.5
  488.0 1.3 copy-done.13
  490.0 10.0 fusion.15
  500.1 16.8 %fusion.35 = f32[1024,4608]{1,0:T(8,128)} fusion(bf16[1024,1024]{0,1:T(8,128)(2,1)} %copy-done.11, bf16[1024,4608]{1,0:T(8,128)(2,1)} %get-tuple-element.77), kind=kOutput, calls=%fused_computation.84 | convolution fusion | flops 9663676416 | bytes 30408704 | tf_op jit(solution)/shard_map/dot_general | solution.py:33
  517.0 16.7 %fusion.36 = f32[1024,4608]{1,0:T(8,128)} fusion(bf16[1024,1024]{0,1:T(8,128)(2,1)} %copy-done.11, bf16[1024,4608]{1,0:T(8,128)(2,1)} %get-tuple-element.76), kind=kOutput, calls=%fused_computation.85 | convolution fusion | flops 9663676416 | bytes 30408704 | tf_op jit(solution)/shard_map/dot_general | solution.py:33
  534.2 16.9 %fusion.17 = f32[4608,1024]{1,0:T(8,128)} fusion(bf16[1024,4608]{1,0:T(8,128)(2,1)} %get-tuple-element.78, bf16[1024,1024]{0,1:T(8,128)(2,1)} %copy.64, f32[1024]{0:T(1024)S(1)} %compare_select_fusion), kind=kOutput, calls=%fused_computation.54 | convolution fusion | flops 9666822144 | bytes 30412800 | tf_op jit(solution)/shard_map/dot_general | solution.py:33
  551.1 17.3 %add_multiply_fusion = f32[1024,1024]{0,1:T(8,128)} fusion(f32[1024,1024]{0,1:T(8,128)} %copy-done.6, f32[1024]{0:T(1024)S(1)} %compare_select_fusion, bf16[1024,4608]{1,0:T(8,128)(2,1)} %get-tuple-element.78, bf16[4608,1024]{1,0:T(8,128)(2,1)} %all-gather.15.cloned.1.call-done), kind=kOutput, calls=%fused_computation.43 | convolution fusion | flops 9665773568 | bytes 27267072 | tf_op jit(solution)/shard_map/dot_general | solution.py:111
  568.4 5.4 copy.69
  573.8 12.8 fusion.12
  586.5 39.3 %all-reduce.7 = (f32[1024]{0:T(1024)S(1)}, f32[1024]{0:T(1024)S(1)}) all-reduce(f32[1024]{0:T(1024)S(1)} %get-tuple-element.65, f32[1024]{0:T(1024)S(1)} %copy-done.26), channel_id=2, replica_groups=mesh['wide'=8,'narrow'=4] {'wide','narrow'}, use_global_device_ids=true, to_apply=%region_8.9.clone | all-reduce | flops 2048 | bytes 16384
  627.0 6.7 fusion.9
  633.7 5.4 copy.70
  639.1 1.4 copy.76
  640.5 107.8 %reduce-scatter.11.cloned.1.call-done = f32[32,1024]{1,0:T(8,128)} async-done(((f32[1024,1024]{1,0:T(8,128)}), f32[32,1024]{1,0:T(8,128)}) %reduce-scatter.11.cloned.1.call-update) | async-done | bytes 131088 | tf_op jit(solution)/shard_map/reduce_scatter | solution.py:172
  748.2 161.6 %reduce-scatter.9.cloned.1.call-done = f32[32,3072]{1,0:T(8,128)} async-done(((f32[1024,3072]{1,0:T(8,128)}), f32[32,3072]{1,0:T(8,128)}) %reduce-scatter.9.cloned.1.call-update) | async-done | bytes 393232 | tf_op jit(solution)/shard_map/reduce_scatter | solution.py:170
  909.8 212.8 %reduce-scatter.13.cloned.1.call-done = f32[32,4608]{1,0:T(8,128)} async-done(((f32[1024,4608]{1,0:T(8,128)}), f32[32,4608]{1,0:T(8,128)}) %reduce-scatter.13.cloned.1.call-update) | async-done | bytes 589840 | tf_op jit(solution)/shard_map/reduce_scatter | solution.py:174
  1122.6 212.4 %reduce-scatter.15.cloned.1.call-done = f32[32,4608]{1,0:T(8,128)} async-done(((f32[1024,4608]{1,0:T(8,128)}), f32[32,4608]{1,0:T(8,128)}) %reduce-scatter.15.cloned.1.call-update) | async-done | bytes 589840 | tf_op jit(solution)/shard_map/reduce_scatter | solution.py:175
  1335.0 212.6 %reduce-scatter.17.cloned.1.call-done = f32[144,1024]{1,0:T(8,128)} async-done(((f32[4608,1024]{1,0:T(8,128)}), f32[144,1024]{1,0:T(8,128)}) %reduce-scatter.17.cloned.1.call-update) | async-done | bytes 589840 | tf_op jit(solution)/shard_map/reduce_scatter | solution.py:176
  (109 shorter events, 14.7 us)
Async XLA Ops:
  7.2 51.1 %copy-start.27 = (bf16[3,32]{1,0:T(4,128)(2,1)S(1)}, bf16[3,32]{1,0:T(4,128)(2,1)}, u32[]{:S(2)}) copy-start(bf16[3,32]{1,0:T(4,128)(2,1)} %param.16) | copy-start | bytes 580
  7.2 117.7 %copy-start.29 = (s32[8]{0:T(128)S(1)}, s32[8]{0:T(128)}, u32[]{:S(2)}) copy-start(s32[8]{0:T(128)} %param.23) | copy-start | bytes 100
  7.2 120.3 %all-gather.7.cloned.1.call-start = ((), (), s32[]{:S(2)}) async-start(), calls=%async_computation.6 | async-start | bytes 6488064 | tf_op jit(solution)/shard_map/all_gather | solution.py:77
  7.9 151.9 %all-gather.9.cloned.1.call-start = ((), (), s32[]{:S(2)}) async-start(), calls=%async_computation.7 | async-start | bytes 2162688 | tf_op jit(solution)/shard_map/all_gather | solution.py:79
  8.7 216.4 %all-gather.11.cloned.1.call-start = ((), (), s32[]{:S(2)}) async-start(), calls=%async_computation.8 | async-start | bytes 9732096 | tf_op jit(solution)/shard_map/all_gather | solution.py:81
  9.4 299.0 %all-gather.13.cloned.1.call-start = ((), (), s32[]{:S(2)}) async-start(), calls=%async_computation.9 | async-start | bytes 9732096 | tf_op jit(solution)/shard_map/all_gather | solution.py:82
  10.0 381.7 %all-gather.15.cloned.1.call-start = ((), (), s32[]{:S(2)}) async-start(), calls=%async_computation.10 | async-start | bytes 9732096 | tf_op jit(solution)/shard_map/all_gather | solution.py:83
  10.6 628.5 %reduce-scatter.19.cloned.1.call-start = ((), (), s32[]{:S(2)}) async-start(), calls=%async_computation.16 | async-start | bytes 540672
  55.4 81.3 %copy-start.24 = (f32[1024]{0:T(1024)}, f32[1024]{0:T(1024)S(1)}, u32[]{:S(2)}) copy-start(f32[1024]{0:T(1024)S(1)} %convert_element_type.50) | copy-start | bytes 12292
  58.3 101.6 %copy-start.3 = (bf16[1024,1024]{0,1:T(8,128)(2,1)}, bf16[1024,1024]{0,1:T(8,128)(2,1)S(1)}, u32[]{:S(2)}) copy-start(bf16[1024,1024]{0,1:T(8,128)(2,1)S(1)} %copy.61) | copy-start | bytes 6291460
  127.4 9.3 copy-start.22
  127.4 23.1 %copy-start.15 = (f32[1,1024]{1,0:T(1,128)}, f32[1,1024]{1,0:T(1,128)S(1)}, u32[]{:S(2)}) copy-start(f32[1,1024]{1,0:T(1,128)S(1)} %get-tuple-element.85) | copy-start | bytes 12292
  127.4 23.0 %copy-start.17 = (f32[1,1024]{1,0:T(1,128)}, f32[1,1024]{1,0:T(1,128)S(1)}, u32[]{:S(2)}) copy-start(f32[1,1024]{1,0:T(1,128)S(1)} %get-tuple-element.86) | copy-start | bytes 12292
  127.4 23.0 %copy-start.19 = (f32[1,1024]{1,0:T(1,128)}, f32[1,1024]{1,0:T(1,128)S(1)}, u32[]{:S(2)}) copy-start(f32[1,1024]{1,0:T(1,128)S(1)} %get-tuple-element.87) | copy-start | bytes 12292
  136.7 5.0 copy-start
  141.7 2.0 copy-start.1
  143.7 6.8 collective-permute-start
  164.7 1.9 copy-start.6
  167.1 58.0 %copy-start.11 = (bf16[1024,1024]{0,1:T(8,128)(2,1)}, bf16[1024,1024]{0,1:T(8,128)(2,1)S(1)}, u32[]{:S(2)}) copy-start(bf16[1024,1024]{0,1:T(8,128)(2,1)S(1)} %multiply_convert_fusion.6) | copy-start | bytes 6291460
  241.4 150.3 %copy-start.9 = (bf16[1024,1024]{0,1:T(8,128)(2,1)S(1)}, bf16[1024,1024]{0,1:T(8,128)(2,1)}, u32[]{:S(2)}) copy-start(bf16[1024,1024]{0,1:T(8,128)(2,1)} %copy.64) | copy-start | bytes 6291460
  423.0 14.4 copy-start.7
  453.9 1.6 copy-start.28
  455.5 2.4 copy-start.8
  455.5 3.7 copy-start.2
  455.5 5.0 copy-start.5
  460.5 7.2 copy-start.12
  467.6 280.6 %reduce-scatter.11.cloned.1.call-start = ((), (), s32[]{:S(2)}) async-start(), calls=%async_computation.12 | async-start | bytes 4325376 | tf_op jit(solution)/shard_map/reduce_scatter | solution.py:172
  474.3 0.7 copy-start.16
  474.3 0.7 copy-start.18
  474.3 0.7 copy-start.20
  474.3 435.5 %reduce-scatter.9.cloned.1.call-start = ((), (), s32[]{:S(2)}) async-start(), calls=%async_computation.11 | async-start | bytes 12976128 | tf_op jit(solution)/shard_map/reduce_scatter | solution.py:170
  477.8 5.6 collective-permute-start.1
  483.4 6.6 copy-start.4
  483.4 6.6 copy-start.10
  483.5 6.6 copy-start.23
  483.5 6.5 copy-start.25
  488.0 1.3 copy-start.13
  488.0 2.0 copy-start.14
  500.0 622.6 %reduce-scatter.13.cloned.1.call-start = ((), (), s32[]{:S(2)}) async-start(), calls=%async_computation.13 | async-start | bytes 19464192 | tf_op jit(solution)/shard_map/reduce_scatter | solution.py:174
  516.9 818.1 %reduce-scatter.15.cloned.1.call-start = ((), (), s32[]{:S(2)}) async-start(), calls=%async_computation.14 | async-start | bytes 19464192 | tf_op jit(solution)/shard_map/reduce_scatter | solution.py:175
  533.7 1013.9 %reduce-scatter.17.cloned.1.call-start = ((), (), s32[]{:S(2)}) async-start(), calls=%async_computation.15 | async-start | bytes 19464192 | tf_op jit(solution)/shard_map/reduce_scatter | solution.py:176
  573.8 12.8 copy-start.26
  573.8 53.3 %copy-start.21 = (f32[1024]{0:T(1024)S(1)}, f32[1024]{0:T(1024)}, u32[]{:S(2)}) copy-start(f32[1024]{0:T(1024)} %get-tuple-element.88) | copy-start | bytes 12292
Sparse Core Ops, SparseCore 0:
  10.9 72.4 all-gather.6
  86.3 54.9 all-gather.8
  144.1 80.8 all-gather.10
  227.7 80.6 all-gather.12
  311.1 80.6 all-gather.14
  467.7 132.8 reduce-scatter.18
  603.5 144.6 reduce-scatter.10
  755.8 153.9 reduce-scatter.8
  916.8 205.7 reduce-scatter.12
  1129.4 205.5 reduce-scatter.14
  1342.0 205.5 reduce-scatter.16
where the time goes:
time: 1560 us; the launch traced here: 1550 us
  waiting for transfers between devices  1100 us (71%)
  matrix products  209 us (13%)
  blocking collectives  148 us (9%)
  local copies, waits for them, and re-layouts  37.7 us (2%)
  other arithmetic  37.4 us (2%)
    reduce_scatter x1, waiting for transfers between devices, shards(): lax.psum_scatter(grad_gate, ('wide', 'narrow'), scatter_dimension=0, tile...  213 us
    reduce_scatter x1, waiting for transfers between devices, shards(): lax.psum_scatter(grad_down, ('wide', 'narrow'), scatter_dimension=0, tile...  213 us
    reduce_scatter x1, waiting for transfers between devices, shards(): lax.psum_scatter(grad_up, ('wide', 'narrow'), scatter_dimension=0, tiled=...  212 us
    reduce_scatter x1, waiting for transfers between devices, shards(): lax.psum_scatter(grad_in, ('wide', 'narrow'), scatter_dimension=0, tiled=...  162 us
    reduce_scatter x1, waiting for transfers between devices, shards(): lax.psum_scatter(grad_out, ('wide', 'narrow'), scatter_dimension=0, tiled...  108 us
    unnamed x2, blocking collectives  81.5 us
    dot_general x5, matrix products, back_product(): lax.dot_general(grad_low, weight_mat, (((1,), (1,)), ((), ())), preferred...  77.3 us
    dot_general x5, matrix products, outer_sum(): lax.dot_general(left, right, (((0,), (0,)), ((), ())), preferred_element_...  67.1 us
  transfers between devices with their start and end apart: 13, of which 9 were waited for; matrix products, arithmetic and copies ran while one was open for 13% of the time, Pallas kernels for 0%

commit v1 on v0

--- a/solution.py
+++ b/solution.py
@@ -1,12 +1,529 @@
+import functools
+
 import jax
 import jax.numpy as jnp
 from jax import lax
+from jax.experimental import pallas as pl
+from jax.experimental.pallas import tpu as pltpu
 from jax.sharding import PartitionSpec as P
 
 ROW_LEN = 4096
-
-
 epsilon = 1e-05
+F32 = jnp.float32
+BF = jnp.bfloat16
+MESH = pl.DeviceIdType.MESH
+ANY = pl.BlockSpec(memory_space=pl.ANY)
+VM = pl.BlockSpec(memory_space=pltpu.VMEM)
+
+
+def dg(a, b, ca, cb):
+    return lax.dot_general(a, b, (((ca,), (cb,)), ((), ())), preferred_element_type=F32)
+
+
+class Place:
+    def __init__(self):
+        w = lax.axis_index("wide")
+        z = lax.axis_index("narrow")
+        c = lax.rem(w, 2)
+        x = lax.rem(w // 2, 2)
+        y = w // 4
+        self.w, self.z, self.c, self.x, self.y = w, z, c, x, y
+        self.core = (w + 1 - 2 * c, z)
+        self.xn = (w + 2 - 4 * x, z)
+        self.yn = (w + 4 - 8 * y, z)
+        self.zs = [(w, lax.rem(z + k, 4)) for k in (1, 2, 3)]
+        self.zto = [lax.rem(z + k, 4) for k in (1, 2, 3)]
+        self.zfrom = [lax.rem(z + 4 - k, 4) for k in (1, 2, 3)]
+
+        def base(yy, xx, cc):
+            return 16 * yy + 8 * xx + 4 * cc
+
+        self.own, self.xb = base(y, x, c), base(y, 1 - x, c)
+        self.yb, self.db = base(1 - y, x, c), base(1 - y, 1 - x, c)
+        self.sown, self.sxb = base(y, x, 1 - c), base(y, 1 - x, 1 - c)
+        self.syb, self.sdb = base(1 - y, x, 1 - c), base(1 - y, 1 - x, 1 - c)
+        self.me = self.own + z
+
+    def greet(self):
+        bar = pltpu.get_barrier_semaphore()
+        peers = [self.core, self.xn, self.yn] + self.zs
+        for p in peers:
+            pl.semaphore_signal(bar, inc=1, device_id=p, device_id_type=MESH)
+        pl.semaphore_wait(bar, len(peers))
+
+
+def remote(src, dst, ss, rs, dev):
+    return pltpu.make_async_remote_copy(
+        src_ref=src, dst_ref=dst, send_sem=ss, recv_sem=rs, device_id=dev, device_id_type=MESH
+    )
+
+
+class Gather:
+    def __init__(self, pc, shard, full, ss, rs):
+        self.pc, self.shard, self.full, self.ss, self.rs = pc, shard, full, ss, rs
+
+    def zc(self, k):
+        return remote(self.shard(), self.full(self.pc.me, 1), self.ss.at[k], self.rs.at[k], self.pc.zs[k])
+
+    def zr(self, k):
+        v = self.full(self.pc.own + self.pc.zfrom[k], 1)
+        return remote(v, v, self.ss.at[k], self.rs.at[k], self.pc.zs[k])
+
+    def loc(self):
+        return pltpu.make_async_copy(self.shard(), self.full(self.pc.me, 1), self.ss.at[11])
+
+    def cp(self, k, b, n, dev):
+        v = self.full(b, n)
+        return remote(v, v, self.ss.at[k], self.rs.at[k], dev)
+
+    def s0(self):
+        self.loc().start()
+        for k in range(3):
+            self.zc(k).start()
+
+    def s1(self):
+        p = self.pc
+        self.loc().wait()
+        for k in range(3):
+            self.zr(k).wait_recv()
+        self.cp(3, p.own, 4, p.xn).start()
+        self.cp(4, p.own, 4, p.yn).start()
+        self.cp(5, p.own, 4, p.core).start()
+
+    def s2(self):
+        p = self.pc
+        self.cp(3, p.xb, 4, p.xn).wait_recv()
+        self.cp(6, p.xb, 2, p.yn).start()
+        self.cp(7, p.xb, 4, p.core).start()
+        self.cp(4, p.yb, 4, p.yn).wait_recv()
+        self.cp(8, p.yb + 2, 2, p.xn).start()
+        self.cp(9, p.yb, 4, p.core).start()
+
+    def s3(self):
+        p = self.pc
+        self.cp(6, p.db, 2, p.yn).wait_recv()
+        self.cp(8, p.db + 2, 2, p.xn).wait_recv()
+        self.cp(10, p.db, 4, p.core).start()
+
+    def s4(self):
+        p = self.pc
+        for k, b in ((5, p.sown), (7, p.sxb), (9, p.syb), (10, p.sdb)):
+            self.cp(k, b, 4, p.core).wait_recv()
+
+    def fin(self):
+        p = self.pc
+        for k in range(3):
+            self.zc(k).wait_send()
+        for k, b, n in (
+            (3, p.own, 4), (4, p.own, 4), (5, p.own, 4), (6, p.xb, 2),
+            (7, p.xb, 4), (8, p.yb + 2, 2), (9, p.yb, 4), (10, p.db, 4),
+        ):
+            self.cp(k, b, n, p.core).wait_send()
+
+
+NG = 12
+
+
+class Scatter:
+    def __init__(self, pc, bufs, h, out):
+        self.pc, self.h, self.out = pc, h, out
+        (self.part, self.l0, self.ldx, self.ldy, self.lx, self.ly, self.lz,
+         self.sd, self.sx, self.sy, self.so, self.sz, self.ob, self.ss, self.rs, self.os) = bufs
+
+    def hr(self):
+        return pl.ds(0, self.h)
+
+    def c0(self, j, s):
+        p = self.pc
+        return remote(self.part.at[s, :, :, :, 1 - p.c, :, self.hr()], self.l0.at[j, :, :, :, :, self.hr()],
+                      self.ss.at[j, 0], self.rs.at[j, 0], p.core)
+
+    def cdx(self, j, s):
+        return remote(self.sd.at[s, :, pl.ds(0, 2), self.hr()], self.ldx.at[j, :, :, self.hr()],
+                      self.ss.at[j, 1], self.rs.at[j, 1], self.pc.xn)
+
+    def cdy(self, j, s):
+        return remote(self.sd.at[s, :, pl.ds(2, 2), self.hr()], self.ldy.at[j, :, :, self.hr()],
+                      self.ss.at[j, 2], self.rs.at[j, 2], self.pc.yn)
+
+    def cx(self, j, s):
+        return remote(self.sx.at[s, :, :, self.hr()], self.lx.at[j, :, :, self.hr()],
+                      self.ss.at[j, 3], self.rs.at[j, 3], self.pc.xn)
+
+    def cy(self, j, s):
+        return remote(self.sy.at[s, :, :, self.hr()], self.ly.at[j, :, :, self.hr()],
+                      self.ss.at[j, 4], self.rs.at[j, 4], self.pc.yn)
+
+    def cz(self, j, s, k):
+        return remote(self.sz.at[s, :, self.pc.zto[k], self.hr()], self.lz.at[j, k, :, self.hr()],
+                      self.ss.at[j, 5 + k], self.rs.at[j, 5 + k], self.pc.zs[k])
+
+    def r0(self, j, s):
+        self.c0(j, s).start()
+
+    def q(self, j, s, a, yy, xx):
+        hr = self.hr()
+        return (self.part[s, a, yy, xx, self.pc.c, :, hr].astype(F32)
+                + self.l0[j, a, yy, xx, :, hr].astype(F32))
+
+    def r1(self, j, s):
+        p, hr = self.pc, self.hr()
+        self.c0(j, s).wait()
+        for a in range(2):
+            self.sd[s, a, :, hr] = self.q(j, s, a, 1 - p.y, 1 - p.x).astype(BF)
+        self.cdx(j, s).start()
+        self.cdy(j, s).start()
+        for a in range(2):
+            self.sx[s, a, :, hr] = self.q(j, s, a, p.y, 1 - p.x).astype(BF)
+            self.sy[s, a, :, hr] = self.q(j, s, a, 1 - p.y, p.x).astype(BF)
+            self.so[s, a, :, hr] = self.q(j, s, a, p.y, p.x)
+
+    def r2(self, j, s):
+        hr = self.hr()
+        lo, hi = pl.ds(0, 2), pl.ds(2, 2)
+        self.cdx(j, s).wait()
+        for a in range(2):
+            self.sy[s, a, lo, hr] = (self.sy[s, a, lo, hr].astype(F32) + self.ldx[j, a, :, hr].astype(F32)).astype(BF)
+        self.cy(j, s).start()
+        self.cdy(j, s).wait()
+        for a in range(2):
+            self.sx[s, a, hi, hr] = (self.sx[s, a, hi, hr].astype(F32) + self.ldy[j, a, :, hr].astype(F32)).astype(BF)
+        self.cx(j, s).start()
+
+    def r3(self, j, s):
+        hr = self.hr()
+        self.cy(j, s).wait()
+        self.cx(j, s).wait()
+        for a in range(2):
+            t = self.so[s, a, :, hr] + self.lx[j, a, :, hr].astype(F32) + self.ly[j, a, :, hr].astype(F32)
+            self.so[s, a, :, hr] = t
+            self.sz[s, a, :, hr] = t.astype(BF)
+        for k in range(3):
+            self.cz(j, s, k).start()
+
+    def r4(self, j, s):
+        hr = self.hr()
+        for k in range(3):
+            self.cz(j, s, k).wait()
+        for a in range(2):
+            t = self.so[s, a, self.pc.z, hr]
+            for k in range(3):
+                t = t + self.lz[j, k, a, hr].astype(F32)
+            self.ob[s, a, hr] = t
+        for o in self.out(j, s, self.ob, self.os):
+            o.start()
+
+    def drain(self, j, s):
+        for o in self.out(j, s, self.ob, self.os):
+            o.wait()
+
+
+def scatter_scratch(n, h, w):
+    return [
+        pltpu.VMEM((2, 2, 2, 2, 2, 4, h, w), BF),
+        pltpu.VMEM((n, 2, 2, 2, 4, h, w), BF),
+        pltpu.VMEM((n, 2, 2, h, w), BF),
+        pltpu.VMEM((n, 2, 2, h, w), BF),
+        pltpu.VMEM((n, 2, 4, h, w), BF),
+        pltpu.VMEM((n, 2, 4, h, w), BF),
+        pltpu.VMEM((n, 3, 2, h, w), BF),
+        pltpu.VMEM((2, 2, 4, h, w), BF),
+        pltpu.VMEM((2, 2, 4, h, w), BF),
+        pltpu.VMEM((2, 2, 4, h, w), BF),
+        pltpu.VMEM((2, 2, 4, h, w), F32),
+        pltpu.VMEM((2, 2, 4, h, w), BF),
+        pltpu.VMEM((2, 2, h, w), F32),
+        pltpu.SemaphoreType.DMA((n, 8)),
+        pltpu.SemaphoreType.DMA((n, 8)),
+        pltpu.SemaphoreType.DMA((2, 2)),
+    ]
+
+
+NSC = 16
+
+
+def gather_kernel(units, nin, *refs):
+    ins, outs = refs[:nin], refs[nin : 2 * nin]
+    ss, rs = refs[2 * nin :]
+    pc = Place()
+    pc.greet()
+
+    def make(u):
+        a, (r0, rn), (c0, cn) = units[u]
+        nd = len(ins[a].shape)
+        mid = (slice(None),) * (nd - 3)
+        tail = mid + (pl.ds(r0, rn), pl.ds(c0, cn))
+        return Gather(pc, lambda: ins[a].at[(slice(None),) + tail],
+                      lambda b, n: outs[a].at[(pl.ds(b, n),) + tail], ss.at[u], rs.at[u])
+
+    us = [make(u) for u in range(len(units))]
+    n, ahead = len(us), 4
+    for t in range(-ahead, n + 4):
+        if 0 <= t + ahead < n:
+            us[t + ahead].s0()
+        if 0 <= t < n:
+            us[t].s1()
+        if 0 <= t - 1 < n:
+            us[t - 1].s2()
+        if 0 <= t - 2 < n:
+            us[t - 2].s3()
+        if 0 <= t - 3 < n:
+            us[t - 3].s4()
+    for u in us:
+        u.fin()
+
+
+def gather_call(shards, units, cid):
+    n = len(shards)
+    sh = [s[None] for s in shards]
+    return pl.pallas_call(
+        functools.partial(gather_kernel, units, n),
+        out_shape=[jax.ShapeDtypeStruct((32,) + s.shape, s.dtype) for s in shards],
+        in_specs=[ANY] * n,
+        out_specs=[ANY] * n,
+        scratch_shapes=[pltpu.SemaphoreType.DMA((len(units), NG)), pltpu.SemaphoreType.DMA((len(units), NG))],
+        name="gather_first",
+        compiler_params=pltpu.CompilerParams(collective_id=cid, has_side_effects=True),
+    )(*sh)
+
+
+def ffn_kernel(ready, gu_ref, wgu_in, wd_ref, nf_ref, gf_ref, hid_ref,
+               o_ref, gn_ref, ggate_ref, gup_ref, gdown_ref, wgu_ref,
+               gw, uw, dw, act, gg, gu, nt, b3, insem, b3sem, hsem, gss, grs, *sc):
+    pc = Place()
+    f = gw.shape[-1]
+    tok, dim = nf_ref.shape
+    n = gu_ref.shape[-1] // f
+    tm = td = 512
+    pc.greet()
+
+    def cols(j):
+        return pl.ds(pl.multiple_of(j * f, f), f)
+
+    def unit(j):
+        return Gather(pc, lambda: gu_ref.at[:, :, :, cols(j)],
+                      lambda b, m: wgu_ref.at[pl.ds(b, m), :, :, cols(j)], gss.at[j], grs.at[j])
+
+    def out(j, s, ob, osem):
+        return [pltpu.make_async_copy(ob.at[s, 0], ggate_ref.at[:, cols(j)], osem.at[s, 0]),
+                pltpu.make_async_copy(ob.at[s, 1], gup_ref.at[:, cols(j)], osem.at[s, 1])]
+
+    rs = Scatter(pc, sc, 32, out)
+    part = sc[0]
+
+    def fetch(j, s):
+        return [pltpu.make_async_copy(wgu_ref.at[:, 0, :, cols(j)], gw.at[s], insem.at[s, 0]),
+                pltpu.make_async_copy(wgu_ref.at[:, 1, :, cols(j)], uw.at[s], insem.at[s, 1]),
+                pltpu.make_async_copy(wd_ref.at[cols(j), :], dw.at[s], insem.at[s, 2])]
+
+    def put(j, s):
+        return pltpu.make_async_copy(b3.at[s], gdown_ref.at[cols(j), :], b3sem.at[s])
+
+    def on(cond, fn):
+        pl.when(cond)(fn)
+
+    hcopy = pltpu.make_async_copy(hid_ref, o_ref, hsem)
+    hcopy.start()
+    for c in fetch(0, 0):
+        c.start()
+    for j in range(ready, min(ready + 4, n)):
+        unit(j).s0()
+    gn_ref[...] = jnp.zeros_like(gn_ref)
+    for i in range(4):
+        nt[:, i * 256 : (i + 1) * 256] = nf_ref[i * 256 : (i + 1) * 256, :].T
+    hcopy.wait()
+
+    def body(j, carry):
+        s = lax.rem(j, 2)
+
+        def stage(fn, k, lo=0):
+            @pl.when(jnp.logical_and(j + k >= lo, j + k < n))
+            def _():
+                fn(j + k)
+
+        stage(lambda u: [c.wait() for c in fetch(u, s)], 0)
+
+        def tile(i):
+            r = pl.ds(i * tm, tm)
+            x = nf_ref[r, :]
+            g_w, u_w = gw[s].reshape(dim, f), uw[s].reshape(dim, f)
+            g = dg(x, g_w, 1, 0)
+            u = dg(x, u_w, 1, 0)
+            ga = dg(gf_ref[r, :], dw[s], 1, 1)
+            sg = jax.nn.sigmoid(g)
+            si = g * sg
+            a = (si * u).astype(BF)
+            act[r, :] = a
+            ggv = (ga * u * sg * (1.0 + g * (1.0 - sg))).astype(BF)
+            guv = (ga * si).astype(BF)
+            gg[r, :] = ggv
+            gu[r, :] = guv
+            o_ref[r, :] += dg(a, dw[s], 1, 0)
+            gn_ref[r, :] += dg(ggv, g_w, 1, 1) + dg(guv, u_w, 1, 1)
+
+        on(j < n, lambda: tile(0))
+        stage(lambda u: rs.r2(u, 1 - s), -1)
+        stage(lambda u: unit(u).s2(), 2, ready)
+        on(j < n, lambda: tile(1))
+        stage(lambda u: rs.r4(u, s), -2)
+        stage(lambda u: unit(u).s1(), 3, ready + 1)
+        stage(lambda u: unit(u).s0(), 4, ready + 4)
+
+        @pl.when(j < n)
+        def _():
+            for i in range(dim // td):
+                x = nt[i * td : (i + 1) * td, :]
+                part[s, 0, i] = dg(x, gg[...], 1, 0).astype(BF).reshape(2, 2, 4, 32, f)
+                part[s, 1, i] = dg(x, gu[...], 1, 0).astype(BF).reshape(2, 2, 4, 32, f)
+            rs.r0(j, s)
+
+        stage(lambda u: unit(u).s3(), 2, ready)
+        stage(lambda u: unit(u).s4(), 1, ready)
+        stage(lambda u: [c.start() for c in fetch(u, 1 - s)], 1)
+
+        @pl.when(j < n)
+        def _():
+            on(j >= 2, lambda: put(j - 2, s).wait())
+            for i in range(f // 256):
+                b3[s, i * 256 : (i + 1) * 256, :] = dg(act[:, i * 256 : (i + 1) * 256].T, gf_ref[...], 1, 0).astype(BF)
+            put(j, s).start()
+            rs.r1(j, s)
+
+        stage(lambda u: rs.r3(u, 1 - s), -1)
+        stage(lambda u: rs.drain(u, s), -2)
+        return carry
+
+    unit(ready).s1()
+    lax.fori_loop(0, n + 2, body, 0)
+    for j in (n - 2, n - 1):
+        put(j, j % 2).wait()
+
+    def last(j, carry):
+        unit(j).fin()
+        return carry
+
+    lax.fori_loop(ready, n, last, 0)
+
+
+def ffn_call(ready, gu, wgu, wd, nf, gf, hid, cid):
+    tok, dim = nf.shape
+    ff = wd.shape[0]
+    f = 512
+    n = ff // f
+    return pl.pallas_call(
+        functools.partial(ffn_kernel, ready),
+        out_shape=[
+            jax.ShapeDtypeStruct((tok, dim), F32),
+            jax.ShapeDtypeStruct((tok, dim), F32),
+            jax.ShapeDtypeStruct((32, ff), F32),
+            jax.ShapeDtypeStruct((32, ff), F32),
+            jax.ShapeDtypeStruct((ff, dim), BF),
+            jax.ShapeDtypeStruct(wgu.shape, BF),
+        ],
+        in_specs=[ANY, ANY, ANY, VM, VM, ANY],
+        out_specs=[VM, VM, ANY, ANY, ANY, ANY],
+        input_output_aliases={1: 5},
+        scratch_shapes=[
+            pltpu.VMEM((2, 32, 32, f), BF),
+            pltpu.VMEM((2, 32, 32, f), BF),
+            pltpu.VMEM((2, f, dim), BF),
+            pltpu.VMEM((tok, f), BF),
+            pltpu.VMEM((tok, f), BF),
+            pltpu.VMEM((tok, f), BF),
+            pltpu.VMEM((dim, tok), BF),
+            pltpu.VMEM((2, f, dim), BF),
+            pltpu.SemaphoreType.DMA((2, 3)),
+            pltpu.SemaphoreType.DMA((2,)),
+            pltpu.SemaphoreType.DMA,
+            pltpu.SemaphoreType.DMA((n, NG)),
+            pltpu.SemaphoreType.DMA((n, NG)),
+        ] + scatter_scratch(n, 32, f),
+        name="ffn",
+        compiler_params=pltpu.CompilerParams(
+            collective_id=cid, has_side_effects=True, vmem_limit_bytes=60 * 2**20
+        ),
+    )(gu, wgu, wd, nf, gf, hid)
+
+
+def reduce_kernel(gd_ref, go_ref, gi_ref, sm_ref, od_ref, oo_ref, oi_ref, osm_ref, lsem, gss, grs, *sc):
+    pc = Place()
+    pc.greet()
+    small = Gather(pc, lambda: sm_ref, lambda b, m: osm_ref.at[pl.ds(b, m)], gss, grs)
+    small.s0()
+    part = sc[0]
+    units = [(gd_ref, od_ref, 48, 48 * i, 0) for i in range(3)] + [(go_ref, oo_ref, 32, 0, 0)]
+    units += [(gi_ref, oi_ref, 32, 0, 1024 * i) for i in range(3)]
+    n = len(units)
+
+    def load(u):
+        src, _, h, r0, c0 = units[u]
+        s = u % 2
+        return [pltpu.make_async_copy(src.at[:, :, :, :, pl.ds(r0, h), pl.ds(c0 + 512 * a, 512)],
+                                      part.at[s, a, :, :, :, :, pl.ds(0, h)], lsem.at[s, a]) for a in range(2)]
+
+    def eng(u):
+        _, dst, h, r0, c0 = units[u]
+
+        def out(j, s, ob, osem):
+            return [pltpu.make_async_copy(ob.at[s, a, pl.ds(0, h)],
+                                          dst.at[pl.ds(r0, h), pl.ds(c0 + 512 * a, 512)], osem.at[s, a]) for a in range(2)]
+
+        return Scatter(pc, sc, h, out)
+
+    es = [eng(u) for u in range(n)]
+    for c in load(0):
+        c.start()
+    for t in range(n + 4):
+        if t < n:
+            for c in load(t):
+                c.wait()
+            es[t].r0(t, t % 2)
+        if 0 <= t - 2 < n:
+            es[t - 2].r2(t - 2, t % 2)
+        if 0 <= t - 3 < n:
+            es[t - 3].r4(t - 3, (t - 3) % 2)
+        if 0 <= t - 1 < n:
+            es[t - 1].r1(t - 1, (t - 1) % 2)
+        if t + 1 < n:
+            for c in load(t + 1):
+                c.start()
+        if 0 <= t - 2 < n:
+            es[t - 2].r3(t - 2, t % 2)
+        if 0 <= t - 3 < n:
+            es[t - 3].drain(t - 3, (t - 3) % 2)
+        if t == 1:
+            small.s1()
+        if t == 2:
+            small.s2()
+        if t == 3:
+            small.s3()
+    small.s4()
+    small.fin()
+
+
+def reduce_call(gd, go, gi, sm, cid):
+    n = 7
+    view = lambda a: a.reshape(2, 2, 2, 4, a.shape[0] // 32, a.shape[1])
+    return pl.pallas_call(
+        reduce_kernel,
+        out_shape=[
+            jax.ShapeDtypeStruct((gd.shape[0] // 32, gd.shape[1]), F32),
+            jax.ShapeDtypeStruct((go.shape[0] // 32, go.shape[1]), F32),
+            jax.ShapeDtypeStruct((gi.shape[0] // 32, gi.shape[1]), F32),
+            jax.ShapeDtypeStruct((32,) + sm.shape, F32),
+        ],
+        in_specs=[ANY] * 4,
+        out_specs=[ANY] * 4,
+        scratch_shapes=[
+            pltpu.SemaphoreType.DMA((2, 2)),
+            pltpu.SemaphoreType.DMA((NG,)),
+            pltpu.SemaphoreType.DMA((NG,)),
+        ] + scatter_scratch(n, 48, 512),
+        name="reduce_last",
+        compiler_params=pltpu.CompilerParams(
+            collective_id=cid, has_side_effects=True, vmem_limit_bytes=60 * 2**20
+        ),
+    )(view(gd), view(go), view(gi), sm[None])
 
 
 def passed_along(array, axis, by):
@@ -55,7 +572,7 @@
     return (keep_one[:, None], keep_two[:, None], live_mask[:, None])
 
 
-def shards(
+def shards_plain(
     tokens,
     cotangent,
     gain_mix,
@@ -189,36 +706,95 @@
     )
 
 
+def shards(
+    tokens, cotangent, gain_mix, in_weight, conv_taps, out_weight, gain_ffn,
+    gate_weight, up_weight, down_weight, doc_lengths, valid_count,
+):
+    tok_count, features = tokens.shape
+    first_pos = lax.axis_index(("wide", "narrow")) * tok_count
+    keep_one, keep_two, live_mask = doc_masks(doc_lengths, valid_count, first_pos, tok_count)
+    own = gain_mix.shape[0]
+    vecs = jnp.concatenate([gain_mix[None], gain_ffn[None], conv_taps], axis=0)
+    vecs = jnp.pad(vecs, ((0, 11), (0, 128 - own)))
+    gu_shard = jnp.stack([gate_weight, up_weight])
+    units = [(4, (0, 16), (0, 128))]
+    units += [(0, (0, 32), (1024 * i, 1024)) for i in range(3)] + [(1, (0, 32), (0, 1024))]
+    units += [(2, (0, 32), (0, 1024)), (2, (32, 32), (0, 1024)), (2, (64, 32), (0, 1024)), (2, (96, 48), (0, 1024))]
+    units += [(3, (0, 32), (512 * i, 512)) for i in range(2)]
+    w_in, w_out, w_down, w_gu, all_vecs = gather_call(
+        [in_weight, out_weight, down_weight, gu_shard, vecs], units, 1
+    )
+    w_in = w_in.reshape(features, -1)
+    w_out = w_out.reshape(features, features)
+    w_down = w_down.reshape(-1, features)
+    vec = all_vecs[:, :5, :own].transpose(1, 0, 2).reshape(5, features).astype(F32)
+    mix_gain, ffn_gain, taps = vec[0], vec[1], vec[2:]
+    tok_float = tokens.astype(F32)
+    normed_mix, inv_mix = rms_forward(tok_float, mix_gain)
+    normed_low = normed_mix.astype(BF)
+    projected = jnp.dot(normed_low, w_in, preferred_element_type=F32)
+    b_part = projected[:, :features]
+    c_part = projected[:, features : 2 * features]
+    x_part = projected[:, 2 * features :]
+    gated = b_part * x_part
+    edge_rows = passed_along(gated[-2:], "narrow", 1)
+    extended = jnp.concatenate([edge_rows, gated], axis=0)
+    lag_one = keep_one * extended[1:-1]
+    lag_two = keep_two * extended[:-2]
+    conv_out = taps[2][None, :] * gated + taps[1][None, :] * lag_one + taps[0][None, :] * lag_two
+    mixed_low = (c_part * conv_out).astype(BF)
+    hidden_res = tok_float + jnp.dot(mixed_low, w_out, preferred_element_type=F32)
+    normed_ffn, inv_ffn = rms_forward(hidden_res, ffn_gain)
+    ffn_low = normed_ffn.astype(BF)
+    grad_res = live_mask * cotangent.astype(F32)
+    grad_ffn_low = grad_res.astype(BF)
+    summed, grad_nffn, sum_gate, sum_up, grad_down, _ = ffn_call(
+        2, gu_shard[None], w_gu, w_down, ffn_low, grad_ffn_low, hidden_res, 2
+    )
+    output = live_mask * summed
+    grad_hnorm, grad_gf = rms_backward(hidden_res, inv_ffn, ffn_gain, grad_nffn)
+    grad_hidden = grad_res + grad_hnorm
+    grad_mix_low = grad_hidden.astype(BF)
+    grad_out = outer_sum(mixed_low, grad_mix_low).astype(BF)
+    grad_mixed = back_product(grad_mix_low, w_out)
+    grad_c = grad_mixed * conv_out
+    grad_conv = grad_mixed * c_part
+    grad_taps = [
+        jnp.sum(grad_conv * lag_two, axis=0),
+        jnp.sum(grad_conv * lag_one, axis=0),
+        jnp.sum(grad_conv * gated, axis=0),
+    ]
+    lag_grad_one = taps[1][None, :] * keep_one * grad_conv
+    lag_grad_two = taps[0][None, :] * keep_two * grad_conv
+    grad_ext = (
+        jnp.pad(taps[2][None, :] * grad_conv, ((2, 0), (0, 0)))
+        + jnp.pad(lag_grad_one, ((1, 1), (0, 0)))
+        + jnp.pad(lag_grad_two, ((0, 2), (0, 0)))
+    )
+    from_right = passed_along(grad_ext[:2], "narrow", -1)
+    grad_gated = jnp.concatenate([grad_ext[2:-2], grad_ext[-2:] + from_right], axis=0)
+    grad_b = grad_gated * x_part
+    grad_x = grad_gated * b_part
+    grad_proj_low = jnp.concatenate([grad_b, grad_c, grad_x], axis=1).astype(BF)
+    grad_in = outer_sum(normed_low, grad_proj_low).astype(BF)
+    grad_nmix = back_product(grad_proj_low, w_in)
+    grad_tnorm, grad_gm = rms_backward(tok_float, inv_mix, mix_gain, grad_nmix)
+    grad_tokens = grad_hidden + grad_tnorm
+    zero = jnp.zeros_like(grad_gm)
+    small = jnp.stack([grad_gm, grad_gf] + grad_taps + [zero] * 3)
+    sum_down, sum_out, sum_in, all_small = reduce_call(grad_down, grad_out, grad_in, small, 3)
+    mine = lax.dynamic_slice_in_dim(jnp.sum(all_small, axis=0), lax.axis_index(("wide", "narrow")) * own, own, 1)
+    return (output, grad_tokens, mine[0], sum_in, mine[2:5], sum_out, mine[1], sum_gate, sum_up, sum_down)
+
+
 def solution(mesh):
-    placed = (
-        P(("wide", "narrow"), None),
-        P(("wide", "narrow"), None),
-        P(("wide", "narrow")),
-        P(("wide", "narrow"), None),
-        P(None, ("wide", "narrow")),
-        P(("wide", "narrow"), None),
-        P(("wide", "narrow")),
-        P(("wide", "narrow"), None),
-        P(("wide", "narrow"), None),
-        P(("wide", "narrow"), None),
-        P(),
-        P(),
-    )
+    both = ("wide", "narrow")
+    rows, vec, flat = P(both, None), P(both), P(None, both)
+    step = shards if (mesh.shape["wide"], mesh.shape["narrow"]) == (8, 4) else shards_plain
     return jax.shard_map(
-        shards,
+        step,
         mesh=mesh,
-        in_specs=placed,
-        out_specs=(
-            P(("wide", "narrow"), None),
-            P(("wide", "narrow"), None),
-            P(("wide", "narrow")),
-            P(("wide", "narrow"), None),
-            P(None, ("wide", "narrow")),
-            P(("wide", "narrow"), None),
-            P(("wide", "narrow")),
-            P(("wide", "narrow"), None),
-            P(("wide", "narrow"), None),
-            P(("wide", "narrow"), None),
-        ),
+        in_specs=(rows, rows, vec, rows, flat, rows, vec, rows, rows, rows, P(), P()),
+        out_specs=(rows, rows, vec, rows, flat, rows, vec, rows, rows, rows),
         check_vma=False,
     )

time: 1560 us -> 528 us (0.34)
  waiting for transfers between devices: 1100 us -> 1.71 us
  Pallas kernels: 0 us -> 396 us
  matrix products: 209 us -> 41.2 us
  blocking collectives: 148 us -> 0 us
  local copies, waits for them, and re-layouts: 37.7 us -> 17 us
  other arithmetic: 37.4 us -> 54.2 us
    reduce_scatter x5 -> x0, waiting for transfers between devices: 907 us -> none  [the longest x1 213 us: shards(): lax.psum_scatter(grad_gate, ('wide', 'narrow'), scatter_dimension=0, tile...]
    pallas_call x0 -> x3, Pallas kernels: none -> 396 us  [the longest x1 186 us: ffn_call(): pl.pallas_call(functools.partial(ffn_kernel, ready), out_shape=[jax.Shape...]
    all_gather x5 -> x0, waiting for transfers between devices: 191 us -> none  [the longest x1 67 us: shards(): lax.all_gather(up_weight, ('wide', 'narrow'), axis=0, tiled=True)]
    unnamed x2 -> x0, blocking collectives: 81.5 us -> none
    all_gather x1 -> x0, blocking collectives: 66.5 us -> none  [shards(): lax.all_gather(conv_taps, ('wide', 'narrow'), axis=1, tiled=True)]
    dot_general x5 -> x2, matrix products: 77.3 us -> 16.2 us  [back_product(): lax.dot_general(grad_low, weight_mat, (((1,), (1,)), ((), ())), preferred...]
    dot_general x5 -> x2, matrix products: 65 us -> 11.4 us  [the longest x1 8.88 us: shards(): projected = jnp.dot(normed_low, w_in, preferred_element_type=F32)]
    dot_general x5 -> x2, matrix products: 67.1 us -> 13.7 us  [outer_sum(): lax.dot_general(left, right, (((0,), (0,)), ((), ())), preferred_element_...]
  transfers between devices with their start and end apart: 13 -> 2, of which waited for: 9 -> 1; matrix products, arithmetic and copies ran while one was open for 13% -> 2% of each run, Pallas kernels for 0% -> 0%
where the time goes in v1:
time: 528 us; the launch traced here: 520 us
  Pallas kernels  396 us (75%)
  other arithmetic  54.2 us (10%)
  matrix products  41.2 us (8%)
  local copies, waits for them, and re-layouts  17 us (3%)
  starting transfers between devices  8.44 us (2%)
    pallas_call x1, Pallas kernels, ffn_call(): pl.pallas_call(functools.partial(ffn_kernel, ready), out_shape=[jax.Shape...  186 us
    pallas_call x1, Pallas kernels, gather_call(): pl.pallas_call(functools.partial(gather_kernel, units, n), out_shape=[jax...  110 us
    pallas_call x1, Pallas kernels, reduce_call(): pl.pallas_call(reduce_kernel, out_shape=[jax.ShapeDtypeStruct((gd.shape[0...  99.6 us
    dot_general x2, matrix products, back_product(): lax.dot_general(grad_low, weight_mat, (((1,), (1,)), ((), ())), preferred...  16.2 us
    dot_general x2, matrix products, outer_sum(): lax.dot_general(left, right, (((0,), (0,)), ((), ())), preferred_element_...  13.7 us
    unnamed x43, local copies, waits for them, and re-layouts  12.8 us
  transfers between devices with their start and end apart: 2, of which 1 were waited for; matrix products, arithmetic and copies ran while one was open for 2% of the time, Pallas kernels for 0%

profile of v1, /device:TPU:0, one launch (start us, length us, event | category | flops | bytes accessed | tf_op | source)
XLA Modules:
  0.0 519.8 jit_solution(15629330110202865876)
XLA Ops:
  0.7 2.1 maximum_bitcast_fusion.refs_3_.gu_ref
  2.7 1.3 fusion.30.refs_4_
  4.0 110.5 %gather_first.1 = (bf16[32,32,3072]{2,1,0:T(8,128)(2,1)}, bf16[32,32,1024]{2,1,0:T(8,128)(2,1)}, bf16[32,144,1024]{2,1,0:T(8,128)(2,1)}, bf16[32,2,32,4608]{3,2,1,0:T(8,128)(2,1)}, bf16[32,16,128]{2,1,0:T(8,128)(2,1)}) custom-call(bf16[1,32,3072]{2,1,0:T(8,128)(2,1)} %bitcast.45, bf16[1,32,1024]{2,1,0:T(8,128)(2,1)} %bitcast.47, ...), custom_call_target="tpu_custom_call" | custom-call | tf_op jit(solution)/shard_map/gather_first/pallas_call | solution.py:279
  114.5 0.9 convert_bitcast_fusion
  115.3 0.2 slice_reduce_fusion
  115.7 2.1 fusion.2
  117.8 8.9 %fusion.19 = f32[1024,3072]{1,0:T(8,128)S(1)} fusion(bf16[1024,3072]{1,0:T(8,128)(2,1)} %bitcast.55, bf16[1024,1024]{1,0:T(8,128)(2,1)S(1)} %copy-done.8, f32[1024]{0:T(1024)S(1)} %mul.287, f32[1024]{0:T(1024)S(1)} %get-tuple-element.64), kind=kOutput, calls=%fused_computation.52 | convolution fusion | flops 6446645248 | bytes 20979712 | tf_op jit(solution)/shard_map/dot_general | solution.py:735
  126.7 1.4 slice_multiply_fusion
  128.0 3.6 copy-done.2
  131.6 2.0 copy-done.3
  133.7 7.1 %collective-permute-start = (f32[2,1024]{1,0:T(2,128)S(1)}, f32[2,1024]{1,0:T(2,128)S(1)}, u32[]{:S(2)}, u32[]{:S(2)}) collective-permute-start(f32[2,1024]{1,0:T(2,128)S(1)} %slice.90), channel_id=1, source_target_pairs={{0,1},{1,2},{2,3},{4,5},{5,6},{6,7},{8,9},{9,10},{10,11},{12,13},{... | collective-permute-start | bytes 24584 | tf_op jit(solution)/shard_map/ppermute | solution.py:532
  140.8 0.7 constant_dynamic-slice_fusion.1
  141.5 0.2 reduce-window_clone.1
  141.7 0.7 subtract_bitcast_fusion
  142.4 0.6 dynamic_slice.11
  143.0 0.6 compare_select_fusion
  143.7 3.3 fusion.13.gf_ref
  147.0 0.1 compare_reduce_fusion
  147.4 9.3 %multiply_convert_fusion.4 = (bf16[1024,1024]{1,0:T(8,128)(2,1)S(1)}, f32[1024,1024]{1,0:T(8,128)}) fusion(f32[1024,3072]{1,0:T(8,128)} %copy-done.2, f32[1024,1024]{1,0:T(8,128)} %copy-done.3, f32[2,1024]{1,0:T(2,128)S(1)} %collective-permute-done, f32[1024]{0:T(1024)S(1)} %get-tuple-element.70, f32[1024]{0:T(1024)S(1)} %mul.299, ...), kind=kLoop, calls=%fused_computation.41 | loop fusion | flops 11534336 | bytes 14708736 | tf_op jit(solution)/shard_map/convert_element_type | solution.py:745
  156.7 2.5 multiply_reduce_fusion.5
  159.2 2.0 copy-done
  161.2 1.8 multiply_convert_fusion.3.nf_ref
  163.0 185.9 %ffn.1 = (f32[1024,1024]{1,0:T(8,128)}, f32[1024,1024]{1,0:T(8,128)}, f32[32,4608]{1,0:T(8,128)}, f32[32,4608]{1,0:T(8,128)}, bf16[4608,1024]{1,0:T(8,128)(2,1)}, /*index=5*/bf16[32,2,32,4608]{3,2,1,0:T(8,128)(2,1)}) custom-call(bf16[1,2,32,4608]{3,2,1,0:T(8,128)(2,1)} %maximum_bitcast_fusion.refs_3_.gu_ref, ...), custom_call_target="tpu_custom_call", output_to_operand_aliasing={{5}: (1, {})} | custom-call | tf_op jit(solution)/shard_map/ffn/pallas_call | solution.py:413
  348.9 4.6 multiply_reduce_fusion.3
  353.5 1.3 copy-done.6
  354.8 5.6 %subtract_add_fusion = (f32[1024,1024]{1,0:T(8,128)S(1)}, f32[1024,1024]{1,0:T(8,128)}) fusion(f32[1024,1024]{1,0:T(8,128)S(1)} %copy-done.1, bf16[1024,1024]{1,0:T(8,128)(2,1)} %param.13, f32[1024,1024]{1,0:T(8,128)S(1)} %copy-done.6, f32[1024]{0:T(1024)S(1)} %get-tuple-element.42, f32[1024]{0:T(1024)S(1)} %get-tuple-element.67, f32[1024]{0:T(1024)S(1)} %mul.308, ...), kind=kLoop, calls=%fused_computation.35 | loop fusion | flops 10485760 | bytes 23089152 | tf_op jit(solution)/shard_map/add | solution.py:756
  360.4 4.4 fusion.16
  364.8 3.8 convolution_convert_fusion.1
  368.6 5.3 %multiply_reduce_fusion.1 = (f32[1024]{0:T(1024)S(1)}, f32[1024]{0:T(1024)S(1)}, f32[1024]{0:T(1024)S(1)}, f32[1024,1024]{1,0:T(8,128)S(1)}, bf16[1024,1024]{1,0:T(8,128)(2,1)S(1)}) fusion(f32[1024,1024]{1,0:T(8,128)S(1)} %copy-done.4, f32[2,1024]{1,0:T(2,128)S(1)} %collective-permute-done, f32[1024]{0:T(1024)S(1)} %get-tuple-element.69, ...), kind=kLoop, calls=%fused_computation.27 | loop fusion | flops 13628416 | bytes 23097344 | tf_op jit(solution)/shard_map/reduce_sum | solution.py:764
  374.0 1.4 broadcast_multiply_fusion
  375.4 1.3 collective-permute-start.1
  376.7 2.0 pad_add_fusion
  378.7 0.5 slice.95
  379.2 1.7 collective-permute-done.1
  380.9 4.5 multiply_convert_fusion.2
  385.5 11.8 %fusion.11 = (f32[1024]{0:T(1024)S(1)}, f32[1024]{0:T(1024)S(1)}, f32[1024,1024]{1,0:T(8,128)}) fusion(bf16[1024,1024]{1,0:T(8,128)(2,1)S(1)} %copy-done.8, f32[1024]{0:T(1024)S(1)} %get-tuple-element.64, f32[1024]{0:T(1024)S(1)} %mul.287, bf16[1024,3072]{1,0:T(8,128)(2,1)} %bitcast.56, bf16[1024,1024]{1,0:T(8,128)(2,1)S(1)} %get-tuple-element.56, ...), kind=kOutput, calls=%fused_computation.22 | convolution fusion | flops 6468663296 | bytes 18890752 | tf_op jit(solution)/shard_map/dot_general | solution.py:556
  397.3 9.9 %convolution_convert_fusion = bf16[1024,3072]{1,0:T(8,128)(2,1)} fusion(bf16[1024,1024]{1,0:T(8,128)(2,1)S(1)} %get-tuple-element.56, bf16[1024,1024]{1,0:T(8,128)(2,1)S(1)} %get-tuple-element.57, bf16[1024,1024]{1,0:T(8,128)(2,1)S(1)} %get-tuple-element.55, bf16[1024,1024]{1,0:T(8,128)(2,1)S(1)} %copy-done.8, f32[1024]{0:T(1024)S(1)} %mul.287, ...), kind=kOutput, calls=%fused_computation.7 | convolution fusion | flops 6468665344 | bytes 14688256 | tf_op jit(solution)/shard_map/dot_general | solution.py:550
  407.2 0.7 stack.39
  407.9 99.6 %reduce_last.1 = (f32[144,1024]{1,0:T(8,128)}, f32[32,1024]{1,0:T(8,128)}, f32[32,3072]{1,0:T(8,128)}, f32[32,8,1024]{2,1,0:T(8,128)}) custom-call(bf16[2,2,2,4,144,1024]{5,4,3,2,1,0:T(8,128)(2,1)} %bitcast.39, bf16[2,2,2,4,32,1024]{5,4,3,2,1,0:T(8,128)(2,1)} %bitcast.41, bf16[2,2,2,4,32,3072]{5,4,3,2,1,0:T(8,128)(2,1)} %bitcast.40, f32[1,8,1024]{2,1,0:T(8,128)} %bitcast.46), custom_call_target="tpu_custom_call" | custom-call | tf_op jit(solution)/shard_map/reduce_last/pallas_call | solution.py:507
  507.5 1.3 reduce_sum.99
  508.9 0.6 slice.82
  509.4 0.5 slice_bitcast_fusion
  510.0 5.7 %fusion.8 = f32[1024,1024]{1,0:T(8,128)} fusion(f32[1024,1024]{1,0:T(8,128)} %copy-done.7, bf16[1024,1024]{1,0:T(8,128)(2,1)S(1)} %copy-done.8, f32[1024,1024]{1,0:T(8,128)} %get-tuple-element.73, f32[1024]{0:T(1024)S(1)} %get-tuple-element.44, f32[1024]{0:T(1024)S(1)} %get-tuple-element.63, f32[1024]{0:T(1024)S(1)} %mul.287, f32[1024]{0:T(1024)S(1)} %get-tuple-element.64), kind=kLoop, calls=%fused_computation.19 | loop fusion | flops 8388608 | bytes 14696448 | tf_op jit(solution)/shard_map/add | solution.py:782
  515.7 0.7 copy.32
  516.4 0.7 copy.33
  517.1 0.8 copy.34
  517.9 0.8 copy.35
  518.7 0.8 copy.36
  (50 shorter events, 0.6 us)
Async XLA Ops:
  0.6 117.1 %copy-start.8 = (bf16[1024,1024]{1,0:T(8,128)(2,1)S(1)}, bf16[1024,1024]{1,0:T(8,128)(2,1)}, u32[]{:S(2)}) copy-start(bf16[1024,1024]{1,0:T(8,128)(2,1)} %param.12) | copy-start | bytes 6291460
  126.6 5.0 copy-start.2
  126.7 15.8 %copy-start.18 = (s32[8]{0:T(128)S(1)}, s32[8]{0:T(128)}, u32[]{:S(2)}) copy-start(s32[8]{0:T(128)} %param.23) | copy-start | bytes 100
  131.6 2.0 copy-start.3
  133.7 13.7 %collective-permute-start = (f32[2,1024]{1,0:T(2,128)S(1)}, f32[2,1024]{1,0:T(2,128)S(1)}, u32[]{:S(2)}, u32[]{:S(2)}) collective-permute-start(f32[2,1024]{1,0:T(2,128)S(1)} %slice.90), channel_id=1, source_target_pairs={{0,1},{1,2},{2,3},{4,5},{5,6},{6,7},{8,9},{9,10},{10,11},{12,13},{... | collective-permute-start | bytes 24584 | tf_op jit(solution)/shard_map/ppermute | solution.py:532
  147.4 9.3 %copy-start.16 = (bf16[32,32,1024]{2,1,0:T(8,128)(2,1)S(1)}, bf16[32,32,1024]{2,1,0:T(8,128)(2,1)}, u32[]{:S(2)}) copy-start(bf16[32,32,1024]{2,1,0:T(8,128)(2,1)} %get-tuple-element.28) | copy-start | bytes 6291460
  156.7 2.5 copy-start.9
  159.2 2.0 copy-start
  348.8 4.6 copy-start.1
  348.9 5.9 %copy-start.6 = (f32[1024,1024]{1,0:T(8,128)S(1)}, f32[1024,1024]{1,0:T(8,128)}, u32[]{:S(2)}) copy-start(f32[1024,1024]{1,0:T(8,128)} %get-tuple-element.30) | copy-start | bytes 12582916
  354.8 5.6 %copy-start.17 = (bf16[32,32,1024]{2,1,0:T(8,128)(2,1)S(1)}, bf16[32,32,1024]{2,1,0:T(8,128)(2,1)}, u32[]{:S(2)}) copy-start(bf16[32,32,1024]{2,1,0:T(8,128)(2,1)} %get-tuple-element.28) | copy-start | bytes 6291460
  360.4 4.4 copy-start.7
  360.4 4.4 copy-start.10
  364.8 3.8 copy-start.4
  364.8 3.8 copy-start.5
  375.4 5.5 %collective-permute-start.1 = (f32[2,1024]{1,0:T(2,128)S(1)}, f32[2,1024]{1,0:T(2,128)S(1)}, u32[]{:S(2)}, u32[]{:S(2)}) collective-permute-start(f32[2,1024]{1,0:T(2,128)S(1)} %pad_add_fusion.1), channel_id=1, source_target_pairs={{1,0},{2,1},{3,2},{5,4},{6,5},{7,6},{9,8},{10,9},{11,10},{13,12},{... | collective-permute-start | bytes 24584 | tf_op jit(solution)/shard_map/ppermute | solution.py:532
  510.0 5.7 %copy-start.14 = (f32[32,3072]{1,0:T(8,128)S(1)}, f32[32,3072]{1,0:T(8,128)}, u32[]{:S(2)}) copy-start(f32[32,3072]{1,0:T(8,128)} %get-tuple-element.89) | copy-start | bytes 1179652
  510.0 6.5 %copy-start.15 = (f32[32,1024]{1,0:T(8,128)S(1)}, f32[32,1024]{1,0:T(8,128)}, u32[]{:S(2)}) copy-start(f32[32,1024]{1,0:T(8,128)} %get-tuple-element.91) | copy-start | bytes 393220
  510.0 7.1 %copy-start.12 = (f32[32,4608]{1,0:T(8,128)S(1)}, f32[32,4608]{1,0:T(8,128)}, u32[]{:S(2)}) copy-start(f32[32,4608]{1,0:T(8,128)} %get-tuple-element.93) | copy-start | bytes 1769476
  510.0 8.0 %copy-start.11 = (f32[32,4608]{1,0:T(8,128)S(1)}, f32[32,4608]{1,0:T(8,128)}, u32[]{:S(2)}) copy-start(f32[32,4608]{1,0:T(8,128)} %get-tuple-element.94) | copy-start | bytes 1769476
  510.0 8.8 %copy-start.13 = (f32[144,1024]{1,0:T(8,128)S(1)}, f32[144,1024]{1,0:T(8,128)}, u32[]{:S(2)}) copy-start(f32[144,1024]{1,0:T(8,128)} %get-tuple-element.95) | copy-start | bytes 1769476

commit v2 on v0

--- a/solution.py
+++ b/solution.py
@@ -1,12 +1,793 @@
+import functools
+
 import jax
 import jax.numpy as jnp
 from jax import lax
+from jax.experimental import pallas as pl
+from jax.experimental.pallas import tpu as pltpu
 from jax.sharding import PartitionSpec as P
 
 ROW_LEN = 4096
-
-
 epsilon = 1e-05
+F32 = jnp.float32
+BF = jnp.bfloat16
+MESH = pl.DeviceIdType.MESH
+ANY = pl.BlockSpec(memory_space=pl.ANY)
+VM = pl.BlockSpec(memory_space=pltpu.VMEM)
+
+
+def dg(a, b, ca, cb):
+    return lax.dot_general(a, b, (((ca,), (cb,)), ((), ())), preferred_element_type=F32)
+
+
+class Place:
+    def __init__(self):
+        w = lax.axis_index("wide")
+        z = lax.axis_index("narrow")
+        c = lax.rem(w, 2)
+        x = lax.rem(w // 2, 2)
+        y = w // 4
+        self.w, self.z, self.c, self.x, self.y = w, z, c, x, y
+        self.core = (w + 1 - 2 * c, z)
+        self.xn = (w + 2 - 4 * x, z)
+        self.yn = (w + 4 - 8 * y, z)
+        self.zs = [(w, lax.rem(z + k, 4)) for k in (1, 2, 3)]
+        self.zto = [lax.rem(z + k, 4) for k in (1, 2, 3)]
+        self.zfrom = [lax.rem(z + 4 - k, 4) for k in (1, 2, 3)]
+
+        def base(yy, xx, cc):
+            return 16 * yy + 8 * xx + 4 * cc
+
+        self.own, self.xb = base(y, x, c), base(y, 1 - x, c)
+        self.yb, self.db = base(1 - y, x, c), base(1 - y, 1 - x, c)
+        self.sown, self.sxb = base(y, x, 1 - c), base(y, 1 - x, 1 - c)
+        self.syb, self.sdb = base(1 - y, x, 1 - c), base(1 - y, 1 - x, 1 - c)
+        self.me = self.own + z
+
+    def greet(self):
+        bar = pltpu.get_barrier_semaphore()
+        peers = [self.core, self.xn, self.yn] + self.zs
+        for p in peers:
+            pl.semaphore_signal(bar, inc=1, device_id=p, device_id_type=MESH)
+        pl.semaphore_wait(bar, len(peers))
+
+
+def remote(src, dst, ss, rs, dev):
+    return pltpu.make_async_remote_copy(
+        src_ref=src, dst_ref=dst, send_sem=ss, recv_sem=rs, device_id=dev, device_id_type=MESH
+    )
+
+
+class Gather:
+    def __init__(self, pc, src, dst, full, ss, rs):
+        self.pc, self.src, self.dst, self.full, self.ss, self.rs = pc, src, dst, full, ss, rs
+        self.parts = range(len(src))
+
+    def zc(self, i, k):
+        q = 3 * i + k
+        return remote(self.src[i](), self.dst[i](self.pc.me, 1), self.ss.at[q], self.rs.at[q], self.pc.zs[k])
+
+    def zr(self, i, k):
+        q = 3 * i + k
+        v = self.dst[i](self.pc.own + self.pc.zfrom[k], 1)
+        return remote(v, v, self.ss.at[q], self.rs.at[q], self.pc.zs[k])
+
+    def loc(self, i):
+        return pltpu.make_async_copy(self.src[i](), self.dst[i](self.pc.me, 1), self.ss.at[14 + i])
+
+    def cp(self, k, b, n, dev):
+        v = self.full(b, n)
+        return remote(v, v, self.ss.at[k], self.rs.at[k], dev)
+
+    def s0(self):
+        for i in self.parts:
+            self.loc(i).start()
+            for k in range(3):
+                self.zc(i, k).start()
+
+    def s1(self):
+        p = self.pc
+        for i in self.parts:
+            self.loc(i).wait()
+            for k in range(3):
+                self.zr(i, k).wait_recv()
+        self.cp(6, p.own, 4, p.xn).start()
+        self.cp(7, p.own, 4, p.yn).start()
+        self.cp(8, p.own, 4, p.core).start()
+
+    def s2(self):
+        p = self.pc
+        self.cp(6, p.xb, 4, p.xn).wait_recv()
+        self.cp(9, p.xb, 2, p.yn).start()
+        self.cp(10, p.xb, 4, p.core).start()
+        self.cp(7, p.yb, 4, p.yn).wait_recv()
+        self.cp(11, p.yb + 2, 2, p.xn).start()
+        self.cp(12, p.yb, 4, p.core).start()
+
+    def s3(self):
+        p = self.pc
+        self.cp(9, p.db, 2, p.yn).wait_recv()
+        self.cp(11, p.db + 2, 2, p.xn).wait_recv()
+        self.cp(13, p.db, 4, p.core).start()
+
+    def s4(self):
+        p = self.pc
+        for k, b in ((8, p.sown), (10, p.sxb), (12, p.syb), (13, p.sdb)):
+            self.cp(k, b, 4, p.core).wait_recv()
+
+    def fin(self):
+        p = self.pc
+        for i in self.parts:
+            for k in range(3):
+                self.zc(i, k).wait_send()
+        for k, b, n in (
+            (6, p.own, 4), (7, p.own, 4), (8, p.own, 4), (9, p.xb, 2),
+            (10, p.xb, 4), (11, p.yb + 2, 2), (12, p.yb, 4), (13, p.db, 4),
+        ):
+            self.cp(k, b, n, p.core).wait_send()
+
+
+NG = 16
+NL = 4
+
+
+class Scatter:
+    def __init__(self, pc, bufs, h, out):
+        self.pc, self.h, self.out = pc, h, out
+        (self.part, self.l0, self.ldx, self.ldy, self.lx, self.ly, self.lz,
+         self.sd, self.sx, self.sy, self.so, self.sz, self.ob, self.ss, self.rs, self.os) = bufs
+
+    def hr(self):
+        return pl.ds(0, self.h)
+
+    def c0(self, j, s):
+        p = self.pc
+        return remote(self.part.at[s, :, :, :, 1 - p.c, :, self.hr()], self.l0.at[lax.rem(j, NL), :, :, :, :, self.hr()],
+                      self.ss.at[j, 0], self.rs.at[j, 0], p.core)
+
+    def cdx(self, j, s):
+        return remote(self.sd.at[s, :, pl.ds(0, 2), self.hr()], self.ldx.at[lax.rem(j, NL), :, :, self.hr()],
+                      self.ss.at[j, 1], self.rs.at[j, 1], self.pc.xn)
+
+    def cdy(self, j, s):
+        return remote(self.sd.at[s, :, pl.ds(2, 2), self.hr()], self.ldy.at[lax.rem(j, NL), :, :, self.hr()],
+                      self.ss.at[j, 2], self.rs.at[j, 2], self.pc.yn)
+
+    def cx(self, j, s):
+        return remote(self.sx.at[s, :, :, self.hr()], self.lx.at[lax.rem(j, NL), :, :, self.hr()],
+                      self.ss.at[j, 3], self.rs.at[j, 3], self.pc.xn)
+
+    def cy(self, j, s):
+        return remote(self.sy.at[s, :, :, self.hr()], self.ly.at[lax.rem(j, NL), :, :, self.hr()],
+                      self.ss.at[j, 4], self.rs.at[j, 4], self.pc.yn)
+
+    def cz(self, j, s, k):
+        return remote(self.sz.at[s, :, self.pc.zto[k], self.hr()], self.lz.at[lax.rem(j, NL), k, :, self.hr()],
+                      self.ss.at[j, 5 + k], self.rs.at[j, 5 + k], self.pc.zs[k])
+
+    def r0(self, j, s):
+        self.c0(j, s).start()
+
+    def q(self, j, s, a, yy, xx):
+        hr = self.hr()
+        return (self.part[s, a, yy, xx, self.pc.c, :, hr].astype(F32)
+                + self.l0[lax.rem(j, NL), a, yy, xx, :, hr].astype(F32))
+
+    def r1(self, j, s):
+        p, hr = self.pc, self.hr()
+        self.c0(j, s).wait()
+        for a in range(2):
+            self.sd[s, a, :, hr] = self.q(j, s, a, 1 - p.y, 1 - p.x).astype(BF)
+        self.cdx(j, s).start()
+        self.cdy(j, s).start()
+        for a in range(2):
+            self.sx[s, a, :, hr] = self.q(j, s, a, p.y, 1 - p.x).astype(BF)
+            self.sy[s, a, :, hr] = self.q(j, s, a, 1 - p.y, p.x).astype(BF)
+            self.so[s, a, :, hr] = self.q(j, s, a, p.y, p.x)
+
+    def r2(self, j, s):
+        hr = self.hr()
+        lo, hi = pl.ds(0, 2), pl.ds(2, 2)
+        self.cdx(j, s).wait()
+        for a in range(2):
+            self.sy[s, a, lo, hr] = (self.sy[s, a, lo, hr].astype(F32) + self.ldx[lax.rem(j, NL), a, :, hr].astype(F32)).astype(BF)
+        self.cy(j, s).start()
+        self.cdy(j, s).wait()
+        for a in range(2):
+            self.sx[s, a, hi, hr] = (self.sx[s, a, hi, hr].astype(F32) + self.ldy[lax.rem(j, NL), a, :, hr].astype(F32)).astype(BF)
+        self.cx(j, s).start()
+
+    def r3(self, j, s):
+        hr = self.hr()
+        self.cy(j, s).wait()
+        self.cx(j, s).wait()
+        for a in range(2):
+            t = self.so[s, a, :, hr] + self.lx[lax.rem(j, NL), a, :, hr].astype(F32) + self.ly[lax.rem(j, NL), a, :, hr].astype(F32)
+            self.so[s, a, :, hr] = t
+            self.sz[s, a, :, hr] = t.astype(BF)
+        for k in range(3):
+            self.cz(j, s, k).start()
+
+    def r4(self, j, s):
+        hr = self.hr()
+        for k in range(3):
+            self.cz(j, s, k).wait()
+        for a in range(2):
+            t = self.so[s, a, self.pc.z, hr]
+            for k in range(3):
+                t = t + self.lz[lax.rem(j, NL), k, a, hr].astype(F32)
+            self.ob[s, a, hr] = t
+        self.out(j, s, self.ob, self.os, "start")
+
+    def drain(self, j, s):
+        self.out(j, s, self.ob, self.os, "wait")
+
+
+def scatter_scratch(n, h, w):
+    return [
+        pltpu.VMEM((2, 2, 2, 2, 2, 4, h, w), BF),
+        pltpu.VMEM((NL, 2, 2, 2, 4, h, w), BF),
+        pltpu.VMEM((NL, 2, 2, h, w), BF),
+        pltpu.VMEM((NL, 2, 2, h, w), BF),
+        pltpu.VMEM((NL, 2, 4, h, w), BF),
+        pltpu.VMEM((NL, 2, 4, h, w), BF),
+        pltpu.VMEM((NL, 3, 2, h, w), BF),
+        pltpu.VMEM((2, 2, 4, h, w), BF),
+        pltpu.VMEM((2, 2, 4, h, w), BF),
+        pltpu.VMEM((2, 2, 4, h, w), BF),
+        pltpu.VMEM((2, 2, 4, h, w), F32),
+        pltpu.VMEM((2, 2, 4, h, w), BF),
+        pltpu.VMEM((2, 2, h, w), F32),
+        pltpu.SemaphoreType.DMA((n, 8)),
+        pltpu.SemaphoreType.DMA((n, 8)),
+        pltpu.SemaphoreType.DMA((2, 2)),
+    ]
+
+
+def inverse_rms(v):
+    return lax.rsqrt(jnp.mean(v * v, axis=1, keepdims=True) + epsilon)
+
+
+def block_kernel(
+    tok_ref, cot_ref, msk_ref, vec_ref, win_s, wout_s, wgate_s, wup_s, wdown_s,
+    out_ref, gtok_ref, ggate_o, gup_o, gdown_o, gout_o, gin_o, small_o,
+    win_h, wout_h, wd_h, wgu_h, vec_h, bcx_h, hid_h, mix_h, gdown_h,
+    obuf, gn, nf, gf, nm, vec, sm, halo_t, halo_g, edge_s, edge_r,
+    vsem, lsem, hsem, gss, grs, *sc,
+):
+    pc = Place()
+    tok, dim = tok_ref.shape
+    ff = wgate_s.shape[-1]
+    f = 512
+    n = ff // f
+    tt = 256
+    nt_ = tok // tt
+    part = sc[0]
+
+    def cols(j, w=f):
+        return pl.ds(pl.multiple_of(j * w, w), w)
+
+    def simple(u, src, dst, c0, w):
+        at = lambda b, m: dst.at[pl.ds(b, m), :, pl.ds(c0, w)]
+        return Gather(pc, [lambda: src.at[:, :, pl.ds(c0, w)]], [at], at, gss.at[u], grs.at[u])
+
+    def down_unit(i):
+        rows = ff // 32
+        at = lambda b, m: wd_h.at[pl.ds(pl.multiple_of(b * rows, rows), m * rows), pl.ds(256 * i, 256)]
+        return Gather(pc, [lambda: wdown_s.at[:, pl.ds(256 * i, 256)]], [at], at, gss.at[5 + i], grs.at[5 + i])
+
+    def gu_unit(j):
+        srcs = [lambda: wgate_s.at[:, :, cols(j)], lambda: wup_s.at[:, :, cols(j)]]
+        dsts = [lambda b, m: wgu_h.at[pl.ds(b, m), 0, :, cols(j)], lambda b, m: wgu_h.at[pl.ds(b, m), 1, :, cols(j)]]
+        return Gather(pc, srcs, dsts, lambda b, m: wgu_h.at[pl.ds(b, m), :, :, cols(j)], gss.at[9 + j], grs.at[9 + j])
+
+    def unit(u):
+        if u == 0:
+            return simple(0, vec_ref, vec_h, 0, 128)
+        if u < 4:
+            return simple(u, win_s, win_h, 1024 * (u - 1), 1024)
+        if u == 4:
+            return simple(4, wout_s, wout_h, 0, 1024)
+        if u < 9:
+            return down_unit(u - 5)
+        return gu_unit(u - 9)
+
+    small = Gather(pc, [lambda: sm], [lambda b, m: small_o.at[pl.ds(b, m)]], lambda b, m: small_o.at[pl.ds(b, m)],
+                   gss.at[9 + n], grs.at[9 + n])
+
+    def step(t):
+        if t + 4 < 9 + n:
+            unit(t + 4).s0()
+        unit(t).s1()
+        if t >= 1:
+            unit(t - 1).s2()
+        if t >= 2:
+            unit(t - 2).s3()
+        if t >= 3:
+            unit(t - 3).s4()
+
+    ndn = n + 4
+    gdown6 = gdown_h.reshape(2, 2, 2, 4, ff // 32, dim)
+
+    def act_on(copies, what):
+        for c in copies:
+            getattr(c, what)()
+
+    def out_gu(j, s, ob, osem, what):
+        act_on([pltpu.make_async_copy(ob.at[s, 0], ggate_o.at[:, cols(j)], osem.at[s, 0]),
+                pltpu.make_async_copy(ob.at[s, 1], gup_o.at[:, cols(j)], osem.at[s, 1])], what)
+
+    def out_rows(dst, r0, c0, h):
+        def go(j, s, ob, osem, what):
+            act_on([pltpu.make_async_copy(ob.at[s, a, pl.ds(0, h)],
+                                          dst.at[pl.ds(r0, h), pl.ds(c0 + 512 * a, 512)], osem.at[s, a])
+                    for a in range(2)], what)
+        return go
+
+    def out_down(j, s, ob, osem, what):
+        out_rows(gdown_o, pl.multiple_of((j - n) * 32, 32), 0, 32)(j, s, ob, osem, what)
+
+    def out_mixed(j, s, ob, osem, what):
+        pl.when(j < n)(lambda: out_gu(j, s, ob, osem, what))
+        pl.when(j >= n)(lambda: out_down(j, s, ob, osem, what))
+
+    eng_gu = Scatter(pc, sc, 32, out_gu)
+    eng_mid = Scatter(pc, sc, 32, out_mixed)
+    order = (1, 0, 2)
+
+    def eng(u):
+        if u < ndn:
+            return Scatter(pc, sc, 32, out_down)
+        if u == ndn:
+            return Scatter(pc, sc, 16, out_rows(gdown_o, 128, 0, 16))
+        if u == ndn + 1:
+            return Scatter(pc, sc, 32, out_rows(gout_o, 0, 0, 32))
+        return Scatter(pc, sc, 32, out_rows(gin_o, 0, 1024 * order[u - ndn - 2], 32))
+
+    pc.greet()
+    cot_copy = pltpu.make_async_copy(cot_ref, gf, hsem.at[0])
+    cot_copy.start()
+    for u in range(5):
+        unit(u).s0()
+    tail = remote(tok_ref.at[pl.ds(tok - 16, 16)], halo_t, hsem.at[1], hsem.at[2], pc.zs[0])
+    tail.start()
+    sm[...] = jnp.zeros_like(sm)
+    edge_s[...] = jnp.zeros_like(edge_s)
+    gn[...] = jnp.zeros_like(gn)
+    cot_copy.wait()
+
+    def live_rows(i, _):
+        r = cols(i, tt)
+        gf[r, :] = (gf[r, :].astype(F32) * msk_ref[r, 2:3]).astype(BF)
+        return 0
+
+    lax.fori_loop(0, nt_, live_rows, 0)
+    unit(0).s1()
+    unit(1).s1()
+    unit(0).s2()
+    unit(2).s1()
+    unit(0).s3()
+    unit(1).s2()
+    unit(0).s4()
+
+    def mixer_forward(vbuf, win, wout, st, mst, tb):
+        vcopy = pltpu.make_async_copy(vec_h, vbuf, vsem.at[0])
+        vcopy.start()
+        for u in (5, 6, 7):
+            unit(u).s0()
+        vcopy.wait()
+        for q in range(8):
+            v = vbuf[4 * q].astype(F32)
+            for k in range(1, 4):
+                v = v + vbuf[4 * q + k].astype(F32)
+            vec[:, 128 * q : 128 * q + 128] = v
+        gain = vec[0:1, :]
+
+        def normed(i, _):
+            r = cols(i, tt)
+            t = tok_ref[r, :].astype(F32)
+            nm[r, :] = (t * inverse_rms(t) * gain).astype(BF)
+            return 0
+
+        lax.fori_loop(0, nt_, normed, 0)
+        unit(3).s1()
+        unit(2).s2()
+        unit(1).s3()
+        wl = [pltpu.make_async_copy(win_h.at[:, :, pl.ds(1024 * i, 1024)], win.at[i], vsem.at[i]) for i in range(3)]
+        wl.append(pltpu.make_async_copy(wout_h, wout, vsem.at[3]))
+        for t in (4, 5, 6, 7):
+            step(t)
+            wl[t - 4].start()
+        tail.wait()
+        th = halo_t[...].astype(F32)
+        nh = (th * inverse_rms(th) * gain).astype(BF)
+        for c in wl:
+            c.wait()
+        hb = dg(nh, win[0].reshape(dim, dim), 1, 0) * dg(nh, win[2].reshape(dim, dim), 1, 0)
+        halo_g[...] = hb[8:16, :]
+        tb[0:8, :] = halo_g[...]
+
+        def stash(i, s):
+            r = cols(i, tt)
+            return [pltpu.make_async_copy(st.at[s, k], bcx_h.at[k, r], lsem.at[s, k]) for k in range(3)] + [
+                pltpu.make_async_copy(mst.at[s], mix_h.at[r], lsem.at[s, 3]),
+                pltpu.make_async_copy(obuf.at[r], hid_h.at[r], lsem.at[s, 4])]
+
+        def tile(i, _):
+            r = cols(i, tt)
+            s = lax.rem(i, 2)
+            pl.when(i >= 2)(lambda: act_on(stash(i - 2, s), "wait"))
+            x = nm[r, :]
+            bv = dg(x, win[0].reshape(dim, dim), 1, 0)
+            st[s, 0] = bv
+            xv = dg(x, win[2].reshape(dim, dim), 1, 0)
+            st[s, 2] = xv
+            tb[8 : 8 + tt, :] = bv * xv
+            cv = dg(x, win[1].reshape(dim, dim), 1, 0)
+            st[s, 1] = cv
+            k1, k2 = msk_ref[r, 0:1], msk_ref[r, 1:2]
+            conv = (vec[4:5, :] * tb[8 : 8 + tt, :] + vec[3:4, :] * (k1 * tb[7 : 7 + tt, :])
+                    + vec[2:3, :] * (k2 * tb[6 : 6 + tt, :]))
+            mixed = (cv * conv).astype(BF)
+            mst[s] = mixed
+            tb[0:8, :] = tb[tt : tt + 8, :]
+            h = tok_ref[r, :].astype(F32) + dg(mixed, wout[...].reshape(dim, dim), 1, 0)
+            obuf[r, :] = h
+            nf[r, :] = (h * inverse_rms(h) * vec[1:2, :]).astype(BF)
+            act_on(stash(i, s), "start")
+            for k in range(4):
+                pl.when(i == k)(functools.partial(step, 8 + k))
+            return 0
+
+        lax.fori_loop(0, nt_, tile, 0)
+        for i in (nt_ - 2, nt_ - 1):
+            act_on(stash(i, i % 2), "wait")
+
+    pl.run_scoped(
+        mixer_forward, pltpu.VMEM((32, 16, 128), BF), pltpu.VMEM((3, 32, 32, dim), BF), pltpu.VMEM((32, 32, dim), BF),
+        pltpu.VMEM((2, 3, tt, dim), F32), pltpu.VMEM((2, tt, dim), BF), pltpu.VMEM((tt + 8, dim), F32),
+    )
+    step(12)
+
+    def put(b3, j, s):
+        return pltpu.make_async_copy(b3.at[s], gdown_h.at[cols(j), :], vsem.at[s])
+
+    def ffn(gw, uw, dw, act, gg, gu, nt, b3):
+        tm = td = 512
+
+        def fetch(j, s):
+            return [pltpu.make_async_copy(wgu_h.at[:, 0, :, cols(j)], gw.at[s], lsem.at[s, 0]),
+                    pltpu.make_async_copy(wgu_h.at[:, 1, :, cols(j)], uw.at[s], lsem.at[s, 1]),
+                    pltpu.make_async_copy(wd_h.at[cols(j), :], dw.at[s], lsem.at[s, 2])]
+
+        act_on(fetch(0, 0), "start")
+
+        def turned(i, _):
+            nt[:, cols(i, tt)] = nf[cols(i, tt), :].T
+            return 0
+
+        lax.fori_loop(0, nt_, turned, 0)
+
+        def body(j, carry):
+            s = lax.rem(j, 2)
+
+            def stage(fn, k, lo=0):
+                pl.when(jnp.logical_and(j + k >= lo, j + k < n))(lambda: fn(j + k))
+
+            act_on(fetch(j, s), "wait")
+
+            def tile(i):
+                r = pl.ds(i * tm, tm)
+                x = nf[r, :]
+                g_w, u_w = gw[s].reshape(dim, f), uw[s].reshape(dim, f)
+                g = dg(x, g_w, 1, 0)
+                u = dg(x, u_w, 1, 0)
+                ga = dg(gf[r, :], dw[s], 1, 1)
+                sg = jax.nn.sigmoid(g)
+                si = g * sg
+                a = (si * u).astype(BF)
+                act[r, :] = a
+                ggv = (ga * u * sg * (1.0 + g * (1.0 - sg))).astype(BF)
+                guv = (ga * si).astype(BF)
+                gg[r, :] = ggv
+                gu[r, :] = guv
+                obuf[r, :] += dg(a, dw[s], 1, 0)
+                gn[r, :] += dg(ggv, g_w, 1, 1) + dg(guv, u_w, 1, 1)
+
+            tile(0)
+            stage(lambda u: eng_gu.r2(u, 1 - s), -1)
+            stage(lambda u: gu_unit(u).s2(), 2, 3)
+            tile(1)
+            stage(lambda u: eng_gu.r4(u, s), -2)
+            stage(lambda u: gu_unit(u).s1(), 3, 4)
+            stage(lambda u: gu_unit(u).s0(), 8, 8)
+            for i in range(dim // td):
+                x = nt[i * td : (i + 1) * td, :]
+                part[s, 0, i] = dg(x, gg[...], 1, 0).astype(BF).reshape(2, 2, 4, 32, f)
+                part[s, 1, i] = dg(x, gu[...], 1, 0).astype(BF).reshape(2, 2, 4, 32, f)
+            eng_gu.r0(j, s)
+            stage(lambda u: gu_unit(u).s3(), 2, 2)
+            stage(lambda u: gu_unit(u).s4(), 1, 1)
+            stage(lambda u: act_on(fetch(u, 1 - s), "start"), 1)
+            pl.when(j >= 2)(lambda: put(b3, j - 2, s).wait())
+            for i in range(f // 256):
+                b3[s, i * 256 : (i + 1) * 256, :] = dg(act[:, i * 256 : (i + 1) * 256].T, gf[...], 1, 0).astype(BF)
+            put(b3, j, s).start()
+            eng_gu.r1(j, s)
+            stage(lambda u: eng_gu.r3(u, 1 - s), -1)
+            stage(lambda u: eng_gu.drain(u, s), -2)
+            return carry
+
+        lax.fori_loop(0, n, body, 0)
+        for j in (n - 2, n - 1):
+            put(b3, j, j % 2).wait()
+
+    pl.run_scoped(
+        ffn, pltpu.VMEM((2, 32, 32, f), BF), pltpu.VMEM((2, 32, 32, f), BF), pltpu.VMEM((2, f, dim), BF),
+        pltpu.VMEM((tok, f), BF), pltpu.VMEM((tok, f), BF), pltpu.VMEM((tok, f), BF),
+        pltpu.VMEM((dim, tok), BF), pltpu.VMEM((2, f, dim), BF),
+    )
+
+    def load_down(u, r0, h):
+        s = lax.rem(u, 2)
+        return [pltpu.make_async_copy(gdown6.at[:, :, :, :, pl.ds(r0, h), pl.ds(512 * a, 512)],
+                                      part.at[s, a, :, :, :, :, pl.ds(0, h)], vsem.at[2 + a]) for a in range(2)]
+
+    def load_mid(u):
+        return load_down(u, pl.multiple_of((u - n) * 32, 32), 32)
+
+    def mixer_backward(gp, turn, wout):
+        wcopy = pltpu.make_async_copy(wout_h, wout, vsem.at[0])
+        wcopy.start()
+        act_on(load_mid(n), "start")
+
+        def turned(i, _):
+            turn[:, cols(i, tt)] = nm[cols(i, tt), :].T
+            return 0
+
+        lax.fori_loop(0, nt_, turned, 0)
+        mcopy = pltpu.make_async_copy(mix_h, nm, vsem.at[1])
+        mcopy.start()
+        wcopy.wait()
+
+        def grad_in(k, s):
+            for i in range(2):
+                for a in range(2):
+                    t = dg(turn[512 * i : 512 * i + 512, :], gp[:, 1024 * k + 512 * a : 1024 * k + 512 * a + 512], 1, 0)
+                    part[s, a, i] = t.astype(BF).reshape(2, 2, 4, 32, 512)
+
+        def passes(ld, ost, tb):
+            def fetch(i, s):
+                r = cols(i, tt)
+                return [pltpu.make_async_copy(bcx_h.at[k, r], ld.at[s, k], lsem.at[s, k]) for k in range(3)] + [
+                    pltpu.make_async_copy(hid_h.at[r], ld.at[s, 3], lsem.at[s, 3])]
+
+            def put_out(i):
+                return pltpu.make_async_copy(ost, out_ref.at[cols(i, tt)], lsem.at[0, 4])
+
+            act_on(fetch(0, 0), "start")
+            tb[0:8, :] = halo_g[...]
+
+            def one(i, _):
+                u = n + i
+                su = lax.rem(u, 2)
+                s = lax.rem(i, 2)
+                r = cols(i, tt)
+                act_on(load_mid(u), "wait")
+                eng_mid.r0(u, su)
+                pl.when(i + 1 < nt_)(lambda: act_on(load_mid(u + 1), "start"))
+                pl.when(i + 1 < nt_)(lambda: act_on(fetch(i + 1, 1 - s), "start"))
+                eng_mid.r2(u - 1, 1 - su)
+                act_on(fetch(i, s), "wait")
+                pl.when(i >= 1)(lambda: put_out(i - 1).wait())
+                ost[...] = obuf[r, :] * msk_ref[r, 2:3]
+                put_out(i).start()
+                v = ld[s, 3]
+                g = gn[r, :]
+                inv = inverse_rms(v)
+                a = g * vec[1:2, :]
+                dot = jnp.sum(a * v, axis=1, keepdims=True) / dim
+                ghid = gf[r, :].astype(F32) + (inv * a - v * (inv * inv * inv) * dot)
+                sm[0, 1:2, :] += jnp.sum(g * v * inv, axis=0, keepdims=True)
+                gn[r, :] = ghid
+                low = ghid.astype(BF)
+                nf[r, :] = low
+                gm = dg(low, wout[...].reshape(dim, dim), 1, 1)
+                tb[8 : 8 + tt, :] = ld[s, 0] * ld[s, 2]
+                k1, k2 = msk_ref[r, 0:1], msk_ref[r, 1:2]
+                gated, lag1, lag2 = tb[8 : 8 + tt, :], k1 * tb[7 : 7 + tt, :], k2 * tb[6 : 6 + tt, :]
+                conv = vec[4:5, :] * gated + vec[3:4, :] * lag1 + vec[2:3, :] * lag2
+                gp[r, 1024:2048] = (gm * conv).astype(BF)
+                gc = gm * ld[s, 1]
+                obuf[r, :] = gc
+                sm[0, 2:3, :] += jnp.sum(gc * lag2, axis=0, keepdims=True)
+                sm[0, 3:4, :] += jnp.sum(gc * lag1, axis=0, keepdims=True)
+                sm[0, 4:5, :] += jnp.sum(gc * gated, axis=0, keepdims=True)
+                tb[0:8, :] = tb[tt : tt + 8, :]
+                eng_mid.r4(u - 2, su)
+                eng_mid.r1(u, su)
+                eng_mid.r3(u - 1, 1 - su)
+                eng_mid.drain(u - 2, su)
+                return 0
+
+            lax.fori_loop(0, nt_, one, 0)
+            u = ndn
+            act_on(load_down(u, 128, 16), "start")
+            put_out(nt_ - 1).wait()
+            first, second = obuf[0:1, :], obuf[1:2, :]
+            k1a, k2a, k2b = msk_ref[0:1, 0:1], msk_ref[0:1, 1:2], msk_ref[1:2, 1:2]
+            edge_s[6:7, :] = vec[2:3, :] * (k2a * first)
+            edge_s[7:8, :] = vec[3:4, :] * (k1a * first) + vec[2:3, :] * (k2b * second)
+            edge = remote(edge_s, edge_r, hsem.at[3], hsem.at[4], pc.zs[2])
+            edge.start()
+            act_on(load_down(u, 128, 16), "wait")
+            eng(u).r0(u, u % 2)
+            eng(u - 1).r2(u - 1, (u - 1) % 2)
+            mcopy.wait()
+            so = (u + 1) % 2
+            for i in range(4):
+                t = dg(nm[:, 256 * i : 256 * i + 256].T, nf[...], 1, 0).astype(BF)
+                for a in range(2):
+                    part[so, a, i // 2, i % 2] = t[:, 512 * a : 512 * a + 512].reshape(2, 4, 32, 512)
+            eng(u - 2).r4(u - 2, u % 2)
+            eng(u).r1(u, u % 2)
+            eng(u - 1).r3(u - 1, (u - 1) % 2)
+            eng(u - 2).drain(u - 2, u % 2)
+            u = ndn + 1
+            eng(u).r0(u, u % 2)
+            eng(u - 1).r2(u - 1, (u - 1) % 2)
+            grad_in(1, (u + 1) % 2)
+            eng(u - 2).r4(u - 2, u % 2)
+            eng(u).r1(u, u % 2)
+            eng(u - 1).r3(u - 1, (u - 1) % 2)
+            eng(u - 2).drain(u - 2, u % 2)
+            u = ndn + 2
+            eng(u).r0(u, u % 2)
+            eng(u - 1).r2(u - 1, (u - 1) % 2)
+            edge.wait()
+
+            def fetch2(i, s):
+                r = cols(i, tt)
+                return [pltpu.make_async_copy(bcx_h.at[k, r], ld.at[s, k], lsem.at[s, k]) for k in (0, 2)]
+
+            obuf[tok : tok + 8, :] = jnp.zeros((8, dim), F32)
+            act_on(fetch2(0, 0), "start")
+
+            def two(i, _):
+                s = lax.rem(i, 2)
+                r = cols(i, tt)
+                pl.when(i + 1 < nt_)(lambda: act_on(fetch2(i + 1, 1 - s), "start"))
+                act_on(fetch2(i, s), "wait")
+                tb[...] = obuf[pl.ds(pl.multiple_of(i * tt, tt), tt + 8), :]
+                k1, k2 = msk_ref[r, 3:4], msk_ref[r, 4:5]
+                ost[...] = (vec[4:5, :] * tb[0:tt, :] + vec[3:4, :] * (k1 * tb[1 : 1 + tt, :])
+                            + vec[2:3, :] * (k2 * tb[2 : 2 + tt, :]))
+
+                @pl.when(i == nt_ - 1)
+                def _():
+                    ost[tt - 8 : tt, :] += edge_r[...]
+
+                gg = ost[...]
+                gp[r, 0:1024] = (gg * ld[s, 2]).astype(BF)
+                gp[r, 2048:3072] = (gg * ld[s, 0]).astype(BF)
+                return 0
+
+            lax.fori_loop(0, nt_, two, 0)
+            grad_in(0, (u + 1) % 2)
+            eng(u - 2).r4(u - 2, u % 2)
+            eng(u).r1(u, u % 2)
+            eng(u - 1).r3(u - 1, (u - 1) % 2)
+            eng(u - 2).drain(u - 2, u % 2)
+
+        pl.run_scoped(passes, pltpu.VMEM((2, 4, tt, dim), F32), pltpu.VMEM((tt, dim), F32), pltpu.VMEM((tt + 8, dim), F32))
+
+        def ending(win, ost):
+            wl = [pltpu.make_async_copy(win_h.at[:, :, pl.ds(1024 * i, 1024)], win.at[i], lsem.at[0, i]) for i in range(3)]
+            act_on(wl, "start")
+            u = ndn + 3
+            eng(u).r0(u, u % 2)
+            eng(u - 1).r2(u - 1, (u - 1) % 2)
+            grad_in(2, (u + 1) % 2)
+            eng(u - 2).r4(u - 2, u % 2)
+            eng(u).r1(u, u % 2)
+            eng(u - 1).r3(u - 1, (u - 1) % 2)
+            eng(u - 2).drain(u - 2, u % 2)
+            u = ndn + 4
+            eng(u).r0(u, u % 2)
+            eng(u - 1).r2(u - 1, (u - 1) % 2)
+            act_on(wl, "wait")
+
+            def put_tok(i, s):
+                return pltpu.make_async_copy(ost.at[s], gtok_ref.at[cols(i, tt)], lsem.at[s, 4])
+
+            def grad_tok(i, _):
+                s = lax.rem(i, 2)
+                r = cols(i, tt)
+                g = dg(gp[r, 0:1024], win[0].reshape(dim, dim), 1, 1)
+                g = g + dg(gp[r, 1024:2048], win[1].reshape(dim, dim), 1, 1)
+                g = g + dg(gp[r, 2048:3072], win[2].reshape(dim, dim), 1, 1)
+                v = tok_ref[r, :].astype(F32)
+                inv = inverse_rms(v)
+                a = g * vec[0:1, :]
+                dot = jnp.sum(a * v, axis=1, keepdims=True) / dim
+                pl.when(i >= 2)(lambda: put_tok(i - 2, s).wait())
+                ost[s] = gn[r, :] + (inv * a - v * (inv * inv * inv) * dot)
+                put_tok(i, s).start()
+                sm[0, 0:1, :] += jnp.sum(g * v * inv, axis=0, keepdims=True)
+                return 0
+
+            lax.fori_loop(0, 2, grad_tok, 0)
+            eng(u - 2).r4(u - 2, u % 2)
+            eng(u).r1(u, u % 2)
+            eng(u - 1).r3(u - 1, (u - 1) % 2)
+            eng(u - 2).drain(u - 2, u % 2)
+            lax.fori_loop(2, nt_, grad_tok, 0)
+            small.s0()
+            eng(u).r2(u, u % 2)
+            eng(u - 1).r4(u - 1, (u - 1) % 2)
+            small.s1()
+            eng(u).r3(u, u % 2)
+            eng(u - 1).drain(u - 1, (u - 1) % 2)
+            small.s2()
+            small.s3()
+            eng(u).r4(u, u % 2)
+            small.s4()
+            eng(u).drain(u, u % 2)
+            for i in (nt_ - 2, nt_ - 1):
+                put_tok(i, i % 2).wait()
+
+        pl.run_scoped(ending, pltpu.VMEM((3, 32, 32, dim), BF), pltpu.VMEM((2, tt, dim), F32))
+
+    pl.run_scoped(mixer_backward, pltpu.VMEM((tok, 3 * dim), BF), pltpu.VMEM((dim, tok), BF), pltpu.VMEM((32, 32, dim), BF))
+
+    for u in range(9):
+        unit(u).fin()
+
+    def last(j, carry):
+        gu_unit(j).fin()
+        return carry
+
+    lax.fori_loop(0, n, last, 0)
+    small.fin()
+
+
+def block_call(tokens, cot, masks, vecs, w_in, w_out, w_gate, w_up, w_down):
+    tok, dim = tokens.shape
+    ff = w_gate.shape[1]
+    n = ff // 512
+    sd = jax.ShapeDtypeStruct
+    outs = [
+        sd((tok, dim), F32), sd((tok, dim), F32), sd((32, ff), F32), sd((32, ff), F32), sd((ff // 32, dim), F32),
+        sd((32, dim), F32), sd((32, 3 * dim), F32), sd((32, 8, dim), F32),
+        sd((32, 32, 3 * dim), BF), sd((32, 32, dim), BF), sd((ff, dim), BF), sd((32, 2, 32, ff), BF),
+        sd((32, 16, 128), BF), sd((3, tok, dim), F32), sd((tok, dim), F32), sd((tok, dim), BF), sd((ff, dim), BF),
+    ]
+    return pl.pallas_call(
+        block_kernel,
+        out_shape=outs,
+        in_specs=[VM, ANY, VM, ANY, ANY, ANY, ANY, ANY, ANY],
+        out_specs=[ANY] * len(outs),
+        scratch_shapes=[
+            pltpu.VMEM((tok + 8, dim), F32),
+            pltpu.VMEM((tok, dim), F32),
+            pltpu.VMEM((tok, dim), BF),
+            pltpu.VMEM((tok, dim), BF),
+            pltpu.VMEM((tok, dim), BF),
+            pltpu.VMEM((16, dim), F32),
+            pltpu.VMEM((1, 8, dim), F32),
+            pltpu.VMEM((16, dim), BF),
+            pltpu.VMEM((8, dim), F32),
+            pltpu.VMEM((8, dim), F32),
+            pltpu.VMEM((8, dim), F32),
+            pltpu.SemaphoreType.DMA((4,)),
+            pltpu.SemaphoreType.DMA((2, 5)),
+            pltpu.SemaphoreType.DMA((5,)),
+            pltpu.SemaphoreType.DMA((n + 10, NG)),
+            pltpu.SemaphoreType.DMA((n + 10, NG)),
+        ] + scatter_scratch(n + 9, 32, 512),
+        name="block",
+        compiler_params=pltpu.CompilerParams(collective_id=1, has_side_effects=True, vmem_limit_bytes=61 * 2**20),
+    )(tokens, cot, masks, vecs[None], w_in[None], w_out[None], w_gate[None], w_up[None], w_down)
 
 
 def passed_along(array, axis, by):
@@ -55,7 +836,7 @@
     return (keep_one[:, None], keep_two[:, None], live_mask[:, None])
 
 
-def shards(
+def shards_plain(
     tokens,
     cotangent,
     gain_mix,
@@ -189,36 +970,36 @@
     )
 
 
+def shards(
+    tokens, cotangent, gain_mix, in_weight, conv_taps, out_weight, gain_ffn,
+    gate_weight, up_weight, down_weight, doc_lengths, valid_count,
+):
+    tok_count = tokens.shape[0]
+    me = lax.axis_index(("wide", "narrow"))
+    keep_one, keep_two, live_mask = doc_masks(doc_lengths, valid_count, me * tok_count, tok_count)
+    later_one = jnp.pad(keep_one[1:], ((0, 1), (0, 0)))
+    later_two = jnp.pad(keep_two[2:], ((0, 2), (0, 0)))
+    masks = jnp.concatenate([keep_one, keep_two, live_mask, later_one, later_two], axis=1)
+    masks = jnp.pad(masks, ((0, 0), (0, 123)))
+    own = gain_mix.shape[0]
+    vecs = jnp.concatenate([gain_mix[None], gain_ffn[None], conv_taps, jnp.zeros((11, own), BF)], axis=0)
+    here = lax.broadcasted_iota(jnp.int32, (16, 128), 1) // own == lax.axis_index("narrow")
+    vecs = jnp.where(here, jnp.concatenate([vecs] * 4, axis=1), jnp.zeros((), BF))
+    output, grad_tokens, sum_gate, sum_up, sum_down, sum_out, sum_in, all_small = block_call(
+        tokens, cotangent, masks, vecs, in_weight, out_weight, gate_weight, up_weight, down_weight
+    )[:8]
+    mine = lax.dynamic_slice_in_dim(jnp.sum(all_small, axis=0), me * own, own, 1)
+    return (output, grad_tokens, mine[0], sum_in, mine[2:5], sum_out, mine[1], sum_gate, sum_up, sum_down)
+
+
 def solution(mesh):
-    placed = (
-        P(("wide", "narrow"), None),
-        P(("wide", "narrow"), None),
-        P(("wide", "narrow")),
-        P(("wide", "narrow"), None),
-        P(None, ("wide", "narrow")),
-        P(("wide", "narrow"), None),
-        P(("wide", "narrow")),
-        P(("wide", "narrow"), None),
-        P(("wide", "narrow"), None),
-        P(("wide", "narrow"), None),
-        P(),
-        P(),
-    )
+    both = ("wide", "narrow")
+    rows, vec, flat = P(both, None), P(both), P(None, both)
+    step = shards if (mesh.shape["wide"], mesh.shape["narrow"]) == (8, 4) else shards_plain
     return jax.shard_map(
-        shards,
+        step,
         mesh=mesh,
-        in_specs=placed,
-        out_specs=(
-            P(("wide", "narrow"), None),
-            P(("wide", "narrow"), None),
-            P(("wide", "narrow")),
-            P(("wide", "narrow"), None),
-            P(None, ("wide", "narrow")),
-            P(("wide", "narrow"), None),
-            P(("wide", "narrow")),
-            P(("wide", "narrow"), None),
-            P(("wide", "narrow"), None),
-            P(("wide", "narrow"), None),
-        ),
+        in_specs=(rows, rows, vec, rows, flat, rows, vec, rows, rows, rows, P(), P()),
+        out_specs=(rows, rows, vec, rows, flat, rows, vec, rows, rows, rows),
         check_vma=False,
     )

time: 1560 us -> 401 us (0.26)
  waiting for transfers between devices: 1100 us -> 0 us
  Pallas kernels: 0 us -> 380 us
  matrix products: 209 us -> 0 us
  blocking collectives: 148 us -> 0 us
  other arithmetic: 37.4 us -> 4.41 us
  local copies, waits for them, and re-layouts: 37.7 us -> 15.4 us
    reduce_scatter x5 -> x0, waiting for transfers between devices: 907 us -> none  [the longest x1 213 us: shards(): lax.psum_scatter(grad_gate, ('wide', 'narrow'), scatter_dimension=0, tile...]
    pallas_call x0 -> x1, Pallas kernels: none -> 380 us  [block_call(): pl.pallas_call(block_kernel, out_shape=outs, in_specs=[VM, ANY, VM, ANY,...]
    dot_general x15 -> x0, matrix products: 209 us -> none  [the longest x5 77.3 us: back_product(): lax.dot_general(grad_low, weight_mat, (((1,), (1,)), ((), ())), preferred...]
    all_gather x5 -> x0, waiting for transfers between devices: 191 us -> none  [the longest x1 67 us: shards(): lax.all_gather(up_weight, ('wide', 'narrow'), axis=0, tiled=True)]
    unnamed x2 -> x0, blocking collectives: 81.5 us -> none
    all_gather x1 -> x0, blocking collectives: 66.5 us -> none  [shards(): lax.all_gather(conv_taps, ('wide', 'narrow'), axis=1, tiled=True)]
    unnamed x72 -> x19, local copies, waits for them, and re-layouts: 35.8 us -> 10.9 us
  transfers between devices with their start and end apart: 13 -> 0, of which waited for: 9 -> 0; matrix products, arithmetic and copies ran while one was open for 13% -> 0% of each run, Pallas kernels for 0% -> 0%
where the time goes in v2:
time: 401 us; the launch traced here: 400 us
  Pallas kernels  380 us (95%)
  local copies, waits for them, and re-layouts  15.4 us (4%)
  other arithmetic  4.41 us (1%)
    pallas_call x1, Pallas kernels, block_call(): pl.pallas_call(block_kernel, out_shape=outs, in_specs=[VM, ANY, VM, ANY,...  380 us
    unnamed x19, local copies, waits for them, and re-layouts  10.9 us

profile of v2, /device:TPU:0, one launch (start us, length us, event | category | flops | bytes accessed | tf_op | source)
XLA Modules:
  0.0 400.5 jit_solution(6797562496094582266)
XLA Ops:
  0.7 1.2 dynamic_slice.12
  1.9 0.7 constant_dynamic-slice_fusion.1
  2.6 0.2 reduce-window_clone.1
  2.8 0.7 subtract_bitcast_fusion
  3.5 0.1 pad.22.clone
  3.6 0.8 maximum_bitcast_fusion
  4.4 0.7 fusion.vec_ref
  5.0 0.7 compare_select_fusion
  5.7 0.1 compare_reduce_fusion
  5.8 0.1 slice.23
  5.9 0.1 slice.21
  6.0 0.2 copy.27
  6.3 0.8 pad.14.msk_ref
  7.1 379.9 %block.1 = (f32[1024,1024]{1,0:T(8,128)}, f32[1024,1024]{1,0:T(8,128)}, f32[32,4608]{1,0:T(8,128)}, f32[32,4608]{1,0:T(8,128)}, f32[144,1024]{1,0:T(8,128)}, /*i...) custom-call(bf16[1024,1024]{1,0:T(8,128)(2,1)} %tok_ref.1, ...), custom_call_target="tpu_custom_call" | custom-call | tf_op jit(solution)/shard_map/block/pallas_call | solution.py:765
  387.0 1.3 reduce_sum.9
  388.3 0.1 constant_dynamic-slice_fusion
  388.4 0.5 slice_bitcast_fusion
  388.9 0.6 slice.26
  389.5 0.0 copy-start
  389.5 4.9 %copy.35 = f32[1024,1024]{1,0:T(8,128)} copy(f32[1024,1024]{1,0:T(8,128)} %get-tuple-element.46) | data formatting | bytes 8388608
  394.4 0.0 copy-done
  394.4 0.0 copy-start.4
  394.4 0.0 copy-start.5
  394.4 0.0 copy-start.3
  394.4 0.0 copy-start.2
  394.5 0.0 copy-start.1
  394.5 2.1 copy.36
  396.6 0.0 copy-done.4
  396.6 0.7 copy.37
  397.4 0.0 copy-done.5
  397.4 0.7 copy.38
  398.0 0.0 copy-done.3
  398.0 0.8 copy.39
  398.8 0.0 copy-done.2
  398.8 0.8 copy.40
  399.7 0.0 copy-done.1
  399.7 0.8 copy.41
  (8 shorter events, 0.1 us)
Async XLA Ops:
  389.5 4.9 %copy-start = (f32[1024,1024]{1,0:T(8,128)S(1)}, f32[1024,1024]{1,0:T(8,128)}, u32[]{:S(2)}) copy-start(f32[1024,1024]{1,0:T(8,128)} %get-tuple-element.47) | copy-start | bytes 12582916
  394.4 2.2 copy-start.4
  394.4 2.9 copy-start.5
  394.4 3.6 copy-start.3
  394.4 4.4 %copy-start.2 = (f32[32,4608]{1,0:T(8,128)S(1)}, f32[32,4608]{1,0:T(8,128)}, u32[]{:S(2)}) copy-start(f32[32,4608]{1,0:T(8,128)} %get-tuple-element.54) | copy-start | bytes 1769476
  394.5 5.2 %copy-start.1 = (f32[144,1024]{1,0:T(8,128)S(1)}, f32[144,1024]{1,0:T(8,128)}, u32[]{:S(2)}) copy-start(f32[144,1024]{1,0:T(8,128)} %get-tuple-element.55) | copy-start | bytes 1769476

commit v3 on v2

--- a/solution.py
+++ b/solution.py
@@ -129,6 +129,8 @@
 
 NG = 16
 NL = 4
+AHEAD = 2
+NS = 4
 
 
 class Scatter:
@@ -142,15 +144,15 @@
 
     def c0(self, j, s):
         p = self.pc
-        return remote(self.part.at[s, :, :, :, 1 - p.c, :, self.hr()], self.l0.at[lax.rem(j, NL), :, :, :, :, self.hr()],
+        return remote(self.part.at[lax.rem(j, 2), :, :, :, 1 - p.c, :, self.hr()], self.l0.at[lax.rem(j, 3), :, :, :, :, self.hr()],
                       self.ss.at[j, 0], self.rs.at[j, 0], p.core)
 
     def cdx(self, j, s):
-        return remote(self.sd.at[s, :, pl.ds(0, 2), self.hr()], self.ldx.at[lax.rem(j, NL), :, :, self.hr()],
+        return remote(self.sd.at[lax.rem(j, 2), :, pl.ds(0, 2), self.hr()], self.ldx.at[lax.rem(j, NL), :, :, self.hr()],
                       self.ss.at[j, 1], self.rs.at[j, 1], self.pc.xn)
 
     def cdy(self, j, s):
-        return remote(self.sd.at[s, :, pl.ds(2, 2), self.hr()], self.ldy.at[lax.rem(j, NL), :, :, self.hr()],
+        return remote(self.sd.at[lax.rem(j, 2), :, pl.ds(2, 2), self.hr()], self.ldy.at[lax.rem(j, NL), :, :, self.hr()],
                       self.ss.at[j, 2], self.rs.at[j, 2], self.pc.yn)
 
     def cx(self, j, s):
@@ -162,7 +164,7 @@
                       self.ss.at[j, 4], self.rs.at[j, 4], self.pc.yn)
 
     def cz(self, j, s, k):
-        return remote(self.sz.at[s, :, self.pc.zto[k], self.hr()], self.lz.at[lax.rem(j, NL), k, :, self.hr()],
+        return remote(self.sz.at[lax.rem(j, 2), :, self.pc.zto[k], self.hr()], self.lz.at[lax.rem(j, NL), k, :, self.hr()],
                       self.ss.at[j, 5 + k], self.rs.at[j, 5 + k], self.pc.zs[k])
 
     def r0(self, j, s):
@@ -170,14 +172,14 @@
 
     def q(self, j, s, a, yy, xx):
         hr = self.hr()
-        return (self.part[s, a, yy, xx, self.pc.c, :, hr].astype(F32)
-                + self.l0[lax.rem(j, NL), a, yy, xx, :, hr].astype(F32))
+        return (self.part[lax.rem(j, 2), a, yy, xx, self.pc.c, :, hr].astype(F32)
+                + self.l0[lax.rem(j, 3), a, yy, xx, :, hr].astype(F32))
 
     def r1(self, j, s):
         p, hr = self.pc, self.hr()
         self.c0(j, s).wait()
         for a in range(2):
-            self.sd[s, a, :, hr] = self.q(j, s, a, 1 - p.y, 1 - p.x).astype(BF)
+            self.sd[lax.rem(j, 2), a, :, hr] = self.q(j, s, a, 1 - p.y, 1 - p.x).astype(BF)
         self.cdx(j, s).start()
         self.cdy(j, s).start()
         for a in range(2):
@@ -204,7 +206,7 @@
         for a in range(2):
             t = self.so[s, a, :, hr] + self.lx[lax.rem(j, NL), a, :, hr].astype(F32) + self.ly[lax.rem(j, NL), a, :, hr].astype(F32)
             self.so[s, a, :, hr] = t
-            self.sz[s, a, :, hr] = t.astype(BF)
+            self.sz[lax.rem(j, 2), a, :, hr] = t.astype(BF)
         for k in range(3):
             self.cz(j, s, k).start()
 
@@ -219,6 +221,15 @@
             self.ob[s, a, hr] = t
         self.out(j, s, self.ob, self.os, "start")
 
+    def go(self, stage, j):
+        (self.r1, self.r2, self.r3, self.r4)[stage - 1](j, lax.rem(j, NS))
+
+    def begin(self, j):
+        self.r0(j, lax.rem(j, NS))
+
+    def end(self, j):
+        self.drain(j, lax.rem(j, NS))
+
     def drain(self, j, s):
         self.out(j, s, self.ob, self.os, "wait")
 
@@ -226,21 +237,21 @@
 def scatter_scratch(n, h, w):
     return [
         pltpu.VMEM((2, 2, 2, 2, 2, 4, h, w), BF),
-        pltpu.VMEM((NL, 2, 2, 2, 4, h, w), BF),
+        pltpu.VMEM((3, 2, 2, 2, 4, h, w), BF),
         pltpu.VMEM((NL, 2, 2, h, w), BF),
         pltpu.VMEM((NL, 2, 2, h, w), BF),
         pltpu.VMEM((NL, 2, 4, h, w), BF),
         pltpu.VMEM((NL, 2, 4, h, w), BF),
         pltpu.VMEM((NL, 3, 2, h, w), BF),
         pltpu.VMEM((2, 2, 4, h, w), BF),
+        pltpu.VMEM((NS, 2, 4, h, w), BF),
+        pltpu.VMEM((NS, 2, 4, h, w), BF),
+        pltpu.VMEM((NS, 2, 4, h, w), F32),
         pltpu.VMEM((2, 2, 4, h, w), BF),
-        pltpu.VMEM((2, 2, 4, h, w), BF),
-        pltpu.VMEM((2, 2, 4, h, w), F32),
-        pltpu.VMEM((2, 2, 4, h, w), BF),
-        pltpu.VMEM((2, 2, h, w), F32),
+        pltpu.VMEM((NS, 2, h, w), F32),
         pltpu.SemaphoreType.DMA((n, 8)),
         pltpu.SemaphoreType.DMA((n, 8)),
-        pltpu.SemaphoreType.DMA((2, 2)),
+        pltpu.SemaphoreType.DMA((NS, 2)),
     ]
 
 
@@ -249,11 +260,11 @@
 
 
 def block_kernel(
-    tok_ref, cot_ref, msk_ref, vec_ref, win_s, wout_s, wgate_s, wup_s, wdown_s,
+    tok_ref, cot_ref, doc_ref, count_ref, vec_ref, win_s, wout_s, wgate_s, wup_s, wdown_s,
     out_ref, gtok_ref, ggate_o, gup_o, gdown_o, gout_o, gin_o, small_o,
     win_h, wout_h, wd_h, wgu_h, vec_h, bcx_h, hid_h, mix_h, gdown_h,
-    obuf, gn, nf, gf, nm, vec, sm, halo_t, halo_g, edge_s, edge_r,
-    vsem, lsem, hsem, gss, grs, *sc,
+    obuf, gn, nf, gf, nm, msk_ref, vec, vown, sm, sml, halo_t, halo_g, edge_s, edge_r,
+    vsem, lsem, hsem, esem, gss, grs, *sc,
 ):
     pc = Place()
     tok, dim = tok_ref.shape
@@ -283,7 +294,7 @@
 
     def unit(u):
         if u == 0:
-            return simple(0, vec_ref, vec_h, 0, 128)
+            return simple(0, vown, vec_h, 0, 128)
         if u < 4:
             return simple(u, win_s, win_h, 1024 * (u - 1), 1024)
         if u == 4:
@@ -292,18 +303,31 @@
             return down_unit(u - 5)
         return gu_unit(u - 9)
 
-    small = Gather(pc, [lambda: sm], [lambda b, m: small_o.at[pl.ds(b, m)]], lambda b, m: small_o.at[pl.ds(b, m)],
-                   gss.at[9 + n], grs.at[9 + n])
+    def small_copies(k):
+        peers = [pc.core, pc.xn, pc.yn] + pc.zs
+        return [remote(sm, sml.at[q], esem.at[q], esem.at[6 + q], peers[q]) for q in ((0,), (1,), (2,), (3, 4, 5))[k]]
+
+    def small_begin(k):
+        for c in small_copies(k):
+            c.start()
+
+    def small_end(k):
+        for c in small_copies(k):
+            c.wait()
+        t = sm[...]
+        for q in ((0,), (1,), (2,), (3, 4, 5))[k]:
+            t = t + sml[q]
+        sm[...] = t
 
     def step(t):
-        if t + 4 < 9 + n:
-            unit(t + 4).s0()
         unit(t).s1()
-        if t >= 1:
+        if t + AHEAD < 9 + n:
+            unit(t + AHEAD).s0()
+        if t >= 2:
             unit(t - 1).s2()
-        if t >= 2:
+        if t >= 3:
             unit(t - 2).s3()
-        if t >= 3:
+        if t >= 4:
             unit(t - 3).s4()
 
     ndn = n + 4
@@ -339,47 +363,65 @@
         if u < ndn:
             return Scatter(pc, sc, 32, out_down)
         if u == ndn:
-            return Scatter(pc, sc, 16, out_rows(gdown_o, 128, 0, 16))
-        if u == ndn + 1:
             return Scatter(pc, sc, 32, out_rows(gout_o, 0, 0, 32))
-        return Scatter(pc, sc, 32, out_rows(gin_o, 0, 1024 * order[u - ndn - 2], 32))
+        if u < ndn + 4:
+            return Scatter(pc, sc, 32, out_rows(gin_o, 0, 1024 * order[u - ndn - 1], 32))
+        return Scatter(pc, sc, 16, out_rows(gdown_o, 128, 0, 16))
 
     pc.greet()
+    vown[0] = pltpu.roll(vec_ref[...], 32 * pc.z, 1)
+    unit(0).s0()
+    unit(1).s0()
     cot_copy = pltpu.make_async_copy(cot_ref, gf, hsem.at[0])
     cot_copy.start()
-    for u in range(5):
-        unit(u).s0()
     tail = remote(tok_ref.at[pl.ds(tok - 16, 16)], halo_t, hsem.at[1], hsem.at[2], pc.zs[0])
     tail.start()
     sm[...] = jnp.zeros_like(sm)
     edge_s[...] = jnp.zeros_like(edge_s)
     gn[...] = jnp.zeros_like(gn)
+    row_devs = ROW_LEN // tok
+    row = pc.me // row_devs
+    lens = jnp.broadcast_to(doc_ref[pl.ds(row, 1), :], (8, 128))
+    lane = lax.broadcasted_iota(jnp.int32, (8, 128), 1)
+    sums = lens
+    for k in (1, 2, 4, 8):
+        sums = sums + jnp.where(lane >= k, pltpu.roll(sums, k, 1), 0)
+    starts = jnp.where(lane < 16, sums - lens, -8)[0:1, :]
+    limit = count_ref[row]
     cot_copy.wait()
 
     def live_rows(i, _):
         r = cols(i, tt)
+        t = i * tt + lax.broadcasted_iota(jnp.int32, (tt, 128), 0)
+        place = lax.rem(pc.me, row_devs) * tok + t
+
+        def begins(by):
+            return jnp.max(jnp.where(starts == place + by, 1.0, 0.0), axis=1, keepdims=True)
+
+        b0, b1, b2, bm = begins(0), begins(1), begins(2), begins(-1)
+        ln = lax.broadcasted_iota(jnp.int32, (tt, 128), 1)
+        m = jnp.where(ln == 0, 1.0 - b0, 1.0 - jnp.maximum(b0, bm))
+        m = jnp.where(ln == 2, jnp.where(place < limit, 1.0, 0.0), m)
+        m = jnp.where(ln == 3, jnp.where(t + 1 < tok, 1.0 - b1, 0.0), m)
+        msk_ref[r, :] = jnp.where(ln == 4, jnp.where(t + 2 < tok, 1.0 - jnp.maximum(b2, b1), 0.0), m)
         gf[r, :] = (gf[r, :].astype(F32) * msk_ref[r, 2:3]).astype(BF)
         return 0
 
     lax.fori_loop(0, nt_, live_rows, 0)
     unit(0).s1()
+    unit(2).s0()
+    unit(0).s2()
+    unit(0).s3()
     unit(1).s1()
-    unit(0).s2()
-    unit(2).s1()
-    unit(0).s3()
-    unit(1).s2()
+    unit(3).s0()
     unit(0).s4()
 
     def mixer_forward(vbuf, win, wout, st, mst, tb):
         vcopy = pltpu.make_async_copy(vec_h, vbuf, vsem.at[0])
         vcopy.start()
-        for u in (5, 6, 7):
-            unit(u).s0()
         vcopy.wait()
         for q in range(8):
-            v = vbuf[4 * q].astype(F32)
-            for k in range(1, 4):
-                v = v + vbuf[4 * q + k].astype(F32)
+            v = vbuf[4 * q] + vbuf[4 * q + 1] + vbuf[4 * q + 2] + vbuf[4 * q + 3]
             vec[:, 128 * q : 128 * q + 128] = v
         gain = vec[0:1, :]
 
@@ -390,9 +432,8 @@
             return 0
 
         lax.fori_loop(0, nt_, normed, 0)
-        unit(3).s1()
-        unit(2).s2()
-        unit(1).s3()
+        step(2)
+        step(3)
         wl = [pltpu.make_async_copy(win_h.at[:, :, pl.ds(1024 * i, 1024)], win.at[i], vsem.at[i]) for i in range(3)]
         wl.append(pltpu.make_async_copy(wout_h, wout, vsem.at[3]))
         for t in (4, 5, 6, 7):
@@ -444,7 +485,7 @@
             act_on(stash(i, i % 2), "wait")
 
     pl.run_scoped(
-        mixer_forward, pltpu.VMEM((32, 16, 128), BF), pltpu.VMEM((3, 32, 32, dim), BF), pltpu.VMEM((32, 32, dim), BF),
+        mixer_forward, pltpu.VMEM((32, 8, 128), F32), pltpu.VMEM((3, 32, 32, dim), BF), pltpu.VMEM((32, 32, dim), BF),
         pltpu.VMEM((2, 3, tt, dim), F32), pltpu.VMEM((2, tt, dim), BF), pltpu.VMEM((tt + 8, dim), F32),
     )
     step(12)
@@ -495,17 +536,17 @@
                 gn[r, :] += dg(ggv, g_w, 1, 1) + dg(guv, u_w, 1, 1)
 
             tile(0)
-            stage(lambda u: eng_gu.r2(u, 1 - s), -1)
+            stage(lambda u: eng_gu.go(2, u), -1)
             stage(lambda u: gu_unit(u).s2(), 2, 3)
             tile(1)
-            stage(lambda u: eng_gu.r4(u, s), -2)
+            stage(lambda u: eng_gu.go(4, u), -2)
             stage(lambda u: gu_unit(u).s1(), 3, 4)
-            stage(lambda u: gu_unit(u).s0(), 8, 8)
+            stage(lambda u: gu_unit(u).s0(), 4 + AHEAD, 4 + AHEAD)
             for i in range(dim // td):
                 x = nt[i * td : (i + 1) * td, :]
                 part[s, 0, i] = dg(x, gg[...], 1, 0).astype(BF).reshape(2, 2, 4, 32, f)
                 part[s, 1, i] = dg(x, gu[...], 1, 0).astype(BF).reshape(2, 2, 4, 32, f)
-            eng_gu.r0(j, s)
+            eng_gu.begin(j)
             stage(lambda u: gu_unit(u).s3(), 2, 2)
             stage(lambda u: gu_unit(u).s4(), 1, 1)
             stage(lambda u: act_on(fetch(u, 1 - s), "start"), 1)
@@ -513,9 +554,9 @@
             for i in range(f // 256):
                 b3[s, i * 256 : (i + 1) * 256, :] = dg(act[:, i * 256 : (i + 1) * 256].T, gf[...], 1, 0).astype(BF)
             put(b3, j, s).start()
-            eng_gu.r1(j, s)
-            stage(lambda u: eng_gu.r3(u, 1 - s), -1)
-            stage(lambda u: eng_gu.drain(u, s), -2)
+            eng_gu.go(1, j)
+            stage(lambda u: eng_gu.go(3, u), -1)
+            stage(lambda u: eng_gu.end(u), -2)
             return carry
 
         lax.fori_loop(0, n, body, 0)
@@ -538,8 +579,10 @@
 
     def mixer_backward(gp, turn, wout):
         wcopy = pltpu.make_async_copy(wout_h, wout, vsem.at[0])
+        act_on(load_mid(n), "start")
         wcopy.start()
-        act_on(load_mid(n), "start")
+        act_on(load_mid(n), "wait")
+        eng_mid.begin(n)
 
         def turned(i, _):
             turn[:, cols(i, tt)] = nm[cols(i, tt), :].T
@@ -549,6 +592,11 @@
         mcopy = pltpu.make_async_copy(mix_h, nm, vsem.at[1])
         mcopy.start()
         wcopy.wait()
+
+        def advance(u):
+            for k, stage in ((0, 1), (1, 2), (2, 3), (3, 4)):
+                if u - k < ndn + 5:
+                    eng(u - k).go(stage, u - k)
 
         def grad_in(k, s):
             for i in range(2):
@@ -556,7 +604,19 @@
                     t = dg(turn[512 * i : 512 * i + 512, :], gp[:, 1024 * k + 512 * a : 1024 * k + 512 * a + 512], 1, 0)
                     part[s, a, i] = t.astype(BF).reshape(2, 2, 4, 32, 512)
 
-        def passes(ld, ost, tb):
+        def part_of(u):
+            if u == ndn:
+                for i in range(4):
+                    t = dg(nm[:, 256 * i : 256 * i + 256].T, nf[...], 1, 0).astype(BF)
+                    for a in range(2):
+                        part[u % 2, a, i // 2, i % 2] = t[:, 512 * a : 512 * a + 512].reshape(2, 4, 32, 512)
+            elif u < ndn + 4:
+                grad_in(order[u - ndn - 1], u % 2)
+            else:
+                act_on(load_down(u, 128, 16), "start")
+                act_on(load_down(u, 128, 16), "wait")
+
+        def passes(ld, ost, tb, tb2):
             def fetch(i, s):
                 r = cols(i, tt)
                 return [pltpu.make_async_copy(bcx_h.at[k, r], ld.at[s, k], lsem.at[s, k]) for k in range(3)] + [
@@ -567,17 +627,32 @@
 
             act_on(fetch(0, 0), "start")
             tb[0:8, :] = halo_g[...]
+            obuf[tok : tok + 8, :] = jnp.zeros((8, dim), F32)
+
+            def two(i, s):
+                r = cols(i, tt)
+                tb2[...] = obuf[pl.ds(pl.multiple_of(i * tt, tt), tt + 8), :]
+                k1, k2 = msk_ref[r, 3:4], msk_ref[r, 4:5]
+                tb2[0:tt, :] = (vec[4:5, :] * tb2[0:tt, :] + vec[3:4, :] * (k1 * tb2[1 : 1 + tt, :])
+                                + vec[2:3, :] * (k2 * tb2[2 : 2 + tt, :]))
+
+                @pl.when(i == nt_ - 1)
+                def _():
+                    tb2[tt - 8 : tt, :] += edge_r[...]
+
+                gg = tb2[0:tt, :]
+                gp[r, 0:1024] = (gg * ld[s, 2]).astype(BF)
+                gp[r, 2048:3072] = (gg * ld[s, 0]).astype(BF)
 
             def one(i, _):
                 u = n + i
-                su = lax.rem(u, 2)
                 s = lax.rem(i, 2)
                 r = cols(i, tt)
-                act_on(load_mid(u), "wait")
-                eng_mid.r0(u, su)
+                eng_mid.go(1, u)
+                eng_mid.go(2, u - 1)
+                pl.when(i >= 1)(lambda: eng_mid.go(3, u - 2))
+                pl.when(i != 1)(lambda: eng_mid.go(4, jnp.where(i == 0, n - 2, u - 3)))
                 pl.when(i + 1 < nt_)(lambda: act_on(load_mid(u + 1), "start"))
-                pl.when(i + 1 < nt_)(lambda: act_on(fetch(i + 1, 1 - s), "start"))
-                eng_mid.r2(u - 1, 1 - su)
                 act_on(fetch(i, s), "wait")
                 pl.when(i >= 1)(lambda: put_out(i - 1).wait())
                 ost[...] = obuf[r, :] * msk_ref[r, 2:3]
@@ -588,7 +663,7 @@
                 a = g * vec[1:2, :]
                 dot = jnp.sum(a * v, axis=1, keepdims=True) / dim
                 ghid = gf[r, :].astype(F32) + (inv * a - v * (inv * inv * inv) * dot)
-                sm[0, 1:2, :] += jnp.sum(g * v * inv, axis=0, keepdims=True)
+                sm[1:2, :] += jnp.sum(g * v * inv, axis=0, keepdims=True)
                 gn[r, :] = ghid
                 low = ghid.astype(BF)
                 nf[r, :] = low
@@ -600,102 +675,45 @@
                 gp[r, 1024:2048] = (gm * conv).astype(BF)
                 gc = gm * ld[s, 1]
                 obuf[r, :] = gc
-                sm[0, 2:3, :] += jnp.sum(gc * lag2, axis=0, keepdims=True)
-                sm[0, 3:4, :] += jnp.sum(gc * lag1, axis=0, keepdims=True)
-                sm[0, 4:5, :] += jnp.sum(gc * gated, axis=0, keepdims=True)
+                sm[2:3, :] += jnp.sum(gc * lag2, axis=0, keepdims=True)
+                sm[3:4, :] += jnp.sum(gc * lag1, axis=0, keepdims=True)
+                sm[4:5, :] += jnp.sum(gc * gated, axis=0, keepdims=True)
                 tb[0:8, :] = tb[tt : tt + 8, :]
-                eng_mid.r4(u - 2, su)
-                eng_mid.r1(u, su)
-                eng_mid.r3(u - 1, 1 - su)
-                eng_mid.drain(u - 2, su)
+
+                @pl.when(i == 0)
+                def _():
+                    first, second = obuf[0:1, :], obuf[1:2, :]
+                    k1a, k2a, k2b = msk_ref[0:1, 0:1], msk_ref[0:1, 1:2], msk_ref[1:2, 1:2]
+                    edge_s[6:7, :] = vec[2:3, :] * (k2a * first)
+                    edge_s[7:8, :] = vec[3:4, :] * (k1a * first) + vec[2:3, :] * (k2b * second)
+                    edge.start()
+
+                pl.when(i >= 1)(lambda: two(i - 1, 1 - s))
+
+                @pl.when(i + 1 < nt_)
+                def _():
+                    act_on(fetch(i + 1, 1 - s), "start")
+                    act_on(load_mid(u + 1), "wait")
+                    eng_mid.begin(u + 1)
+
+                pl.when(i != 1)(lambda: eng_mid.end(jnp.where(i == 0, n - 2, u - 3)))
                 return 0
 
             lax.fori_loop(0, nt_, one, 0)
-            u = ndn
-            act_on(load_down(u, 128, 16), "start")
+            mcopy.wait()
+            part_of(ndn)
+            eng(ndn).begin(ndn)
             put_out(nt_ - 1).wait()
-            first, second = obuf[0:1, :], obuf[1:2, :]
-            k1a, k2a, k2b = msk_ref[0:1, 0:1], msk_ref[0:1, 1:2], msk_ref[1:2, 1:2]
-            edge_s[6:7, :] = vec[2:3, :] * (k2a * first)
-            edge_s[7:8, :] = vec[3:4, :] * (k1a * first) + vec[2:3, :] * (k2b * second)
-            edge = remote(edge_s, edge_r, hsem.at[3], hsem.at[4], pc.zs[2])
-            edge.start()
-            act_on(load_down(u, 128, 16), "wait")
-            eng(u).r0(u, u % 2)
-            eng(u - 1).r2(u - 1, (u - 1) % 2)
-            mcopy.wait()
-            so = (u + 1) % 2
-            for i in range(4):
-                t = dg(nm[:, 256 * i : 256 * i + 256].T, nf[...], 1, 0).astype(BF)
-                for a in range(2):
-                    part[so, a, i // 2, i % 2] = t[:, 512 * a : 512 * a + 512].reshape(2, 4, 32, 512)
-            eng(u - 2).r4(u - 2, u % 2)
-            eng(u).r1(u, u % 2)
-            eng(u - 1).r3(u - 1, (u - 1) % 2)
-            eng(u - 2).drain(u - 2, u % 2)
-            u = ndn + 1
-            eng(u).r0(u, u % 2)
-            eng(u - 1).r2(u - 1, (u - 1) % 2)
-            grad_in(1, (u + 1) % 2)
-            eng(u - 2).r4(u - 2, u % 2)
-            eng(u).r1(u, u % 2)
-            eng(u - 1).r3(u - 1, (u - 1) % 2)
-            eng(u - 2).drain(u - 2, u % 2)
-            u = ndn + 2
-            eng(u).r0(u, u % 2)
-            eng(u - 1).r2(u - 1, (u - 1) % 2)
             edge.wait()
-
-            def fetch2(i, s):
-                r = cols(i, tt)
-                return [pltpu.make_async_copy(bcx_h.at[k, r], ld.at[s, k], lsem.at[s, k]) for k in (0, 2)]
-
-            obuf[tok : tok + 8, :] = jnp.zeros((8, dim), F32)
-            act_on(fetch2(0, 0), "start")
-
-            def two(i, _):
-                s = lax.rem(i, 2)
-                r = cols(i, tt)
-                pl.when(i + 1 < nt_)(lambda: act_on(fetch2(i + 1, 1 - s), "start"))
-                act_on(fetch2(i, s), "wait")
-                tb[...] = obuf[pl.ds(pl.multiple_of(i * tt, tt), tt + 8), :]
-                k1, k2 = msk_ref[r, 3:4], msk_ref[r, 4:5]
-                ost[...] = (vec[4:5, :] * tb[0:tt, :] + vec[3:4, :] * (k1 * tb[1 : 1 + tt, :])
-                            + vec[2:3, :] * (k2 * tb[2 : 2 + tt, :]))
-
-                @pl.when(i == nt_ - 1)
-                def _():
-                    ost[tt - 8 : tt, :] += edge_r[...]
-
-                gg = ost[...]
-                gp[r, 0:1024] = (gg * ld[s, 2]).astype(BF)
-                gp[r, 2048:3072] = (gg * ld[s, 0]).astype(BF)
-                return 0
-
-            lax.fori_loop(0, nt_, two, 0)
-            grad_in(0, (u + 1) % 2)
-            eng(u - 2).r4(u - 2, u % 2)
-            eng(u).r1(u, u % 2)
-            eng(u - 1).r3(u - 1, (u - 1) % 2)
-            eng(u - 2).drain(u - 2, u % 2)
-
-        pl.run_scoped(passes, pltpu.VMEM((2, 4, tt, dim), F32), pltpu.VMEM((tt, dim), F32), pltpu.VMEM((tt + 8, dim), F32))
+            two(nt_ - 1, (nt_ - 1) % 2)
+
+        edge = remote(edge_s, edge_r, hsem.at[3], hsem.at[4], pc.zs[2])
+        pl.run_scoped(passes, pltpu.VMEM((2, 4, tt, dim), F32), pltpu.VMEM((tt, dim), F32),
+                      pltpu.VMEM((tt + 8, dim), F32), pltpu.VMEM((tt + 8, dim), F32))
 
         def ending(win, ost):
             wl = [pltpu.make_async_copy(win_h.at[:, :, pl.ds(1024 * i, 1024)], win.at[i], lsem.at[0, i]) for i in range(3)]
             act_on(wl, "start")
-            u = ndn + 3
-            eng(u).r0(u, u % 2)
-            eng(u - 1).r2(u - 1, (u - 1) % 2)
-            grad_in(2, (u + 1) % 2)
-            eng(u - 2).r4(u - 2, u % 2)
-            eng(u).r1(u, u % 2)
-            eng(u - 1).r3(u - 1, (u - 1) % 2)
-            eng(u - 2).drain(u - 2, u % 2)
-            u = ndn + 4
-            eng(u).r0(u, u % 2)
-            eng(u - 1).r2(u - 1, (u - 1) % 2)
-            act_on(wl, "wait")
 
             def put_tok(i, s):
                 return pltpu.make_async_copy(ost.at[s], gtok_ref.at[cols(i, tt)], lsem.at[s, 4])
@@ -713,26 +731,29 @@
                 pl.when(i >= 2)(lambda: put_tok(i - 2, s).wait())
                 ost[s] = gn[r, :] + (inv * a - v * (inv * inv * inv) * dot)
                 put_tok(i, s).start()
-                sm[0, 0:1, :] += jnp.sum(g * v * inv, axis=0, keepdims=True)
+                sm[0:1, :] += jnp.sum(g * v * inv, axis=0, keepdims=True)
                 return 0
 
-            lax.fori_loop(0, 2, grad_tok, 0)
-            eng(u - 2).r4(u - 2, u % 2)
-            eng(u).r1(u, u % 2)
-            eng(u - 1).r3(u - 1, (u - 1) % 2)
-            eng(u - 2).drain(u - 2, u % 2)
-            lax.fori_loop(2, nt_, grad_tok, 0)
-            small.s0()
-            eng(u).r2(u, u % 2)
-            eng(u - 1).r4(u - 1, (u - 1) % 2)
-            small.s1()
-            eng(u).r3(u, u % 2)
-            eng(u - 1).drain(u - 1, (u - 1) % 2)
-            small.s2()
-            small.s3()
-            eng(u).r4(u, u % 2)
-            small.s4()
-            eng(u).drain(u, u % 2)
+            for u in range(ndn, ndn + 8):
+                advance(u)
+                if u < ndn + 4:
+                    part_of(u + 1)
+                    eng(u + 1).begin(u + 1)
+                if u == ndn:
+                    act_on(wl, "wait")
+                if u in (ndn + 1, ndn + 2):
+                    lax.fori_loop(2 * (u - ndn - 1), 2 * (u - ndn), grad_tok, 0)
+                if u == ndn + 2:
+                    small_begin(0)
+                elif u > ndn + 2 and u < ndn + 6:
+                    small_end(u - ndn - 3)
+                    small_begin(u - ndn - 2)
+                elif u == ndn + 6:
+                    small_end(3)
+                    outs = pltpu.make_async_copy(sm, small_o, hsem.at[0])
+                    outs.start()
+                eng(u - 3).end(u - 3)
+            outs.wait()
             for i in (nt_ - 2, nt_ - 1):
                 put_tok(i, i % 2).wait()
 
@@ -748,24 +769,23 @@
         return carry
 
     lax.fori_loop(0, n, last, 0)
-    small.fin()
-
-
-def block_call(tokens, cot, masks, vecs, w_in, w_out, w_gate, w_up, w_down):
+
+
+def block_call(tokens, cot, lengths, counts, vecs, w_in, w_out, w_gate, w_up, w_down):
     tok, dim = tokens.shape
     ff = w_gate.shape[1]
     n = ff // 512
     sd = jax.ShapeDtypeStruct
     outs = [
         sd((tok, dim), F32), sd((tok, dim), F32), sd((32, ff), F32), sd((32, ff), F32), sd((ff // 32, dim), F32),
-        sd((32, dim), F32), sd((32, 3 * dim), F32), sd((32, 8, dim), F32),
+        sd((32, dim), F32), sd((32, 3 * dim), F32), sd((8, dim), F32),
         sd((32, 32, 3 * dim), BF), sd((32, 32, dim), BF), sd((ff, dim), BF), sd((32, 2, 32, ff), BF),
-        sd((32, 16, 128), BF), sd((3, tok, dim), F32), sd((tok, dim), F32), sd((tok, dim), BF), sd((ff, dim), BF),
+        sd((32, 8, 128), F32), sd((3, tok, dim), F32), sd((tok, dim), F32), sd((tok, dim), BF), sd((ff, dim), BF),
     ]
     return pl.pallas_call(
         block_kernel,
         out_shape=outs,
-        in_specs=[VM, ANY, VM, ANY, ANY, ANY, ANY, ANY, ANY],
+        in_specs=[VM, ANY, VM, pl.BlockSpec(memory_space=pltpu.SMEM), VM, ANY, ANY, ANY, ANY, ANY],
         out_specs=[ANY] * len(outs),
         scratch_shapes=[
             pltpu.VMEM((tok + 8, dim), F32),
@@ -773,8 +793,11 @@
             pltpu.VMEM((tok, dim), BF),
             pltpu.VMEM((tok, dim), BF),
             pltpu.VMEM((tok, dim), BF),
-            pltpu.VMEM((16, dim), F32),
-            pltpu.VMEM((1, 8, dim), F32),
+            pltpu.VMEM((tok, 128), F32),
+            pltpu.VMEM((8, dim), F32),
+            pltpu.VMEM((1, 8, 128), F32),
+            pltpu.VMEM((8, dim), F32),
+            pltpu.VMEM((6, 8, dim), F32),
             pltpu.VMEM((16, dim), BF),
             pltpu.VMEM((8, dim), F32),
             pltpu.VMEM((8, dim), F32),
@@ -782,12 +805,13 @@
             pltpu.SemaphoreType.DMA((4,)),
             pltpu.SemaphoreType.DMA((2, 5)),
             pltpu.SemaphoreType.DMA((5,)),
-            pltpu.SemaphoreType.DMA((n + 10, NG)),
-            pltpu.SemaphoreType.DMA((n + 10, NG)),
+            pltpu.SemaphoreType.DMA((12,)),
+            pltpu.SemaphoreType.DMA((n + 9, NG)),
+            pltpu.SemaphoreType.DMA((n + 9, NG)),
         ] + scatter_scratch(n + 9, 32, 512),
         name="block",
-        compiler_params=pltpu.CompilerParams(collective_id=1, has_side_effects=True, vmem_limit_bytes=61 * 2**20),
-    )(tokens, cot, masks, vecs[None], w_in[None], w_out[None], w_gate[None], w_up[None], w_down)
+        compiler_params=pltpu.CompilerParams(collective_id=1, has_side_effects=True, vmem_limit_bytes=62 * 2**20 + 2**19),
+    )(tokens, cot, lengths, counts, vecs, w_in[None], w_out[None], w_gate[None], w_up[None], w_down)
 
 
 def passed_along(array, axis, by):
@@ -974,21 +998,15 @@
     tokens, cotangent, gain_mix, in_weight, conv_taps, out_weight, gain_ffn,
     gate_weight, up_weight, down_weight, doc_lengths, valid_count,
 ):
-    tok_count = tokens.shape[0]
     me = lax.axis_index(("wide", "narrow"))
-    keep_one, keep_two, live_mask = doc_masks(doc_lengths, valid_count, me * tok_count, tok_count)
-    later_one = jnp.pad(keep_one[1:], ((0, 1), (0, 0)))
-    later_two = jnp.pad(keep_two[2:], ((0, 2), (0, 0)))
-    masks = jnp.concatenate([keep_one, keep_two, live_mask, later_one, later_two], axis=1)
-    masks = jnp.pad(masks, ((0, 0), (0, 123)))
     own = gain_mix.shape[0]
-    vecs = jnp.concatenate([gain_mix[None], gain_ffn[None], conv_taps, jnp.zeros((11, own), BF)], axis=0)
-    here = lax.broadcasted_iota(jnp.int32, (16, 128), 1) // own == lax.axis_index("narrow")
-    vecs = jnp.where(here, jnp.concatenate([vecs] * 4, axis=1), jnp.zeros((), BF))
+    vecs = jnp.concatenate([gain_mix[None], gain_ffn[None], conv_taps], axis=0).astype(F32)
+    vecs = jnp.pad(vecs, ((0, 3), (0, 128 - own)))
+    lengths = jnp.pad(doc_lengths, ((0, 0), (0, 128 - doc_lengths.shape[1])))
     output, grad_tokens, sum_gate, sum_up, sum_down, sum_out, sum_in, all_small = block_call(
-        tokens, cotangent, masks, vecs, in_weight, out_weight, gate_weight, up_weight, down_weight
+        tokens, cotangent, lengths, valid_count, vecs, in_weight, out_weight, gate_weight, up_weight, down_weight
     )[:8]
-    mine = lax.dynamic_slice_in_dim(jnp.sum(all_small, axis=0), me * own, own, 1)
+    mine = lax.dynamic_slice_in_dim(all_small, me * own, own, 1)
     return (output, grad_tokens, mine[0], sum_in, mine[2:5], sum_out, mine[1], sum_gate, sum_up, sum_down)
 
 

time: 401 us -> 383 us (0.955)
  Pallas kernels: 380 us -> 367 us
    pallas_call x1, Pallas kernels: 380 us -> 367 us  [block_call(): pl.pallas_call(block_kernel, out_shape=outs, in_specs=[VM, ANY, VM, pl.Bl...]
where the time goes in v3:
time: 383 us
  Pallas kernels  367 us (96%)
  local copies, waits for them, and re-layouts  14.1 us (4%)
    pallas_call x1, Pallas kernels, block_call(): pl.pallas_call(block_kernel, out_shape=outs, in_specs=[VM, ANY, VM, pl.Bl...  367 us
    unnamed x19, local copies, waits for them, and re-layouts  10.9 us

profile of v3, /device:TPU:0, one launch (start us, length us, event | category | flops | bytes accessed | tf_op | source)
XLA Modules:
  0.0 383.0 jit_solution(9973363189145523403)
XLA Ops:
  0.6 1.3 pad.10.doc_ref
  1.9 1.3 fusion.9.vec_ref
  3.2 366.9 %block.1 = (f32[1024,1024]{1,0:T(8,128)}, f32[1024,1024]{1,0:T(8,128)}, f32[32,4608]{1,0:T(8,128)}, f32[32,4608]{1,0:T(8,128)}, f32[144,1024]{1,0:T(8,128)}, /*i...) custom-call(bf16[1024,1024]{1,0:T(8,128)(2,1)} %tok_ref.1, ...), custom_call_target="tpu_custom_call" | custom-call | tf_op jit(solution)/shard_map/block/pallas_call | solution.py:785
  370.2 0.8 constant_dynamic-slice_fusion
  370.9 0.5 slice_bitcast_fusion
  371.4 0.6 slice.10
  372.0 0.0 copy-start
  372.0 4.9 %copy.29 = f32[1024,1024]{1,0:T(8,128)} copy(f32[1024,1024]{1,0:T(8,128)} %get-tuple-element.38) | data formatting | bytes 8388608
  377.0 0.0 copy-done
  377.0 0.0 copy-start.4
  377.0 0.0 copy-start.5
  377.0 0.0 copy-start.3
  377.0 0.0 copy-start.2
  377.0 0.0 copy-start.1
  377.0 2.1 copy.30
  379.1 0.0 copy-done.4
  379.1 0.7 copy.31
  379.9 0.0 copy-done.5
  379.9 0.7 copy.32
  380.5 0.0 copy-done.3
  380.5 0.8 copy.33
  381.4 0.0 copy-done.2
  381.4 0.8 copy.34
  382.2 0.0 copy-done.1
  382.2 0.8 copy.35
Async XLA Ops:
  372.0 4.9 %copy-start = (f32[1024,1024]{1,0:T(8,128)S(1)}, f32[1024,1024]{1,0:T(8,128)}, u32[]{:S(2)}) copy-start(f32[1024,1024]{1,0:T(8,128)} %get-tuple-element.39) | copy-start | bytes 12582916
  377.0 2.2 copy-start.4
  377.0 2.9 copy-start.5
  377.0 3.6 copy-start.3
  377.0 4.4 %copy-start.2 = (f32[32,4608]{1,0:T(8,128)S(1)}, f32[32,4608]{1,0:T(8,128)}, u32[]{:S(2)}) copy-start(f32[32,4608]{1,0:T(8,128)} %get-tuple-element.46) | copy-start | bytes 1769476
  377.0 5.2 %copy-start.1 = (f32[144,1024]{1,0:T(8,128)S(1)}, f32[144,1024]{1,0:T(8,128)}, u32[]{:S(2)}) copy-start(f32[144,1024]{1,0:T(8,128)} %get-tuple-element.47) | copy-start | bytes 1769476

commit v4 on v3

--- a/solution.py
+++ b/solution.py
@@ -320,12 +320,12 @@
         sm[...] = t
 
     def step(t):
-        unit(t).s1()
-        if t + AHEAD < 9 + n:
+        if t < 11:
+            unit(t).s1()
             unit(t + AHEAD).s0()
-        if t >= 2:
+        if t >= 2 and t < 11:
             unit(t - 1).s2()
-        if t >= 3:
+        if t >= 3 and t < 12:
             unit(t - 2).s3()
         if t >= 4:
             unit(t - 3).s4()
@@ -536,18 +536,18 @@
                 gn[r, :] += dg(ggv, g_w, 1, 1) + dg(guv, u_w, 1, 1)
 
             tile(0)
+            stage(lambda u: gu_unit(u).s2(), 1, 1)
             stage(lambda u: eng_gu.go(2, u), -1)
-            stage(lambda u: gu_unit(u).s2(), 2, 3)
             tile(1)
             stage(lambda u: eng_gu.go(4, u), -2)
-            stage(lambda u: gu_unit(u).s1(), 3, 4)
-            stage(lambda u: gu_unit(u).s0(), 4 + AHEAD, 4 + AHEAD)
+            stage(lambda u: gu_unit(u).s1(), 2, 2)
+            stage(lambda u: gu_unit(u).s0(), 2 + AHEAD, 2 + AHEAD)
             for i in range(dim // td):
                 x = nt[i * td : (i + 1) * td, :]
                 part[s, 0, i] = dg(x, gg[...], 1, 0).astype(BF).reshape(2, 2, 4, 32, f)
                 part[s, 1, i] = dg(x, gu[...], 1, 0).astype(BF).reshape(2, 2, 4, 32, f)
             eng_gu.begin(j)
-            stage(lambda u: gu_unit(u).s3(), 2, 2)
+            stage(lambda u: gu_unit(u).s3(), 1, 1)
             stage(lambda u: gu_unit(u).s4(), 1, 1)
             stage(lambda u: act_on(fetch(u, 1 - s), "start"), 1)
             pl.when(j >= 2)(lambda: put(b3, j - 2, s).wait())

time: 383 us -> 374 us (0.977)
  Pallas kernels: 367 us -> 357 us
    pallas_call x1, Pallas kernels: 367 us -> 357 us  [block_call(): pl.pallas_call(block_kernel, out_shape=outs, in_specs=[VM, ANY, VM, pl.Bl...]
where the time goes in v4:
time: 374 us
  Pallas kernels  357 us (95%)
  local copies, waits for them, and re-layouts  14.1 us (4%)
    pallas_call x1, Pallas kernels, block_call(): pl.pallas_call(block_kernel, out_shape=outs, in_specs=[VM, ANY, VM, pl.Bl...  357 us
    unnamed x19, local copies, waits for them, and re-layouts  10.9 us

profile of v4, /device:TPU:0, one launch (start us, length us, event | category | flops | bytes accessed | tf_op | source)
XLA Modules:
  0.0 373.5 jit_solution(4173010989598415383)
XLA Ops:
  0.6 1.3 pad.10.doc_ref
  1.9 1.3 fusion.9.vec_ref
  3.2 357.5 %block.1 = (f32[1024,1024]{1,0:T(8,128)}, f32[1024,1024]{1,0:T(8,128)}, f32[32,4608]{1,0:T(8,128)}, f32[32,4608]{1,0:T(8,128)}, f32[144,1024]{1,0:T(8,128)}, /*i...) custom-call(bf16[1024,1024]{1,0:T(8,128)(2,1)} %tok_ref.1, ...), custom_call_target="tpu_custom_call" | custom-call | tf_op jit(solution)/shard_map/block/pallas_call | solution.py:785
  360.7 0.8 constant_dynamic-slice_fusion
  361.5 0.5 slice_bitcast_fusion
  362.0 0.6 slice.10
  362.6 0.0 copy-start
  362.6 4.9 %copy.29 = f32[1024,1024]{1,0:T(8,128)} copy(f32[1024,1024]{1,0:T(8,128)} %get-tuple-element.38) | data formatting | bytes 8388608
  367.5 0.0 copy-done
  367.5 0.0 copy-start.4
  367.5 0.0 copy-start.5
  367.5 0.0 copy-start.3
  367.5 0.0 copy-start.2
  367.5 0.0 copy-start.1
  367.5 2.1 copy.30
  369.7 0.0 copy-done.4
  369.7 0.7 copy.31
  370.4 0.0 copy-done.5
  370.4 0.7 copy.32
  371.1 0.0 copy-done.3
  371.1 0.8 copy.33
  371.9 0.0 copy-done.2
  371.9 0.8 copy.34
  372.7 0.0 copy-done.1
  372.7 0.8 copy.35
Async XLA Ops:
  362.6 4.9 %copy-start = (f32[1024,1024]{1,0:T(8,128)S(1)}, f32[1024,1024]{1,0:T(8,128)}, u32[]{:S(2)}) copy-start(f32[1024,1024]{1,0:T(8,128)} %get-tuple-element.39) | copy-start | bytes 12582916
  367.5 2.2 copy-start.4
  367.5 2.9 copy-start.5
  367.5 3.6 copy-start.3
  367.5 4.4 %copy-start.2 = (f32[32,4608]{1,0:T(8,128)S(1)}, f32[32,4608]{1,0:T(8,128)}, u32[]{:S(2)}) copy-start(f32[32,4608]{1,0:T(8,128)} %get-tuple-element.46) | copy-start | bytes 1769476
  367.5 5.2 %copy-start.1 = (f32[144,1024]{1,0:T(8,128)S(1)}, f32[144,1024]{1,0:T(8,128)}, u32[]{:S(2)}) copy-start(f32[144,1024]{1,0:T(8,128)} %get-tuple-element.47) | copy-start | bytes 1769476

commit v5 on v4

--- a/solution.py
+++ b/solution.py
@@ -125,6 +125,82 @@
             (10, p.xb, 4), (11, p.yb + 2, 2), (12, p.yb, 4), (13, p.db, 4),
         ):
             self.cp(k, b, n, p.core).wait_send()
+
+
+class GatherLate:
+    def __init__(self, pc, src, view, ss, rs):
+        self.pc, self.src, self.view, self.ss, self.rs = pc, src, view, ss, rs
+
+    def at(self, flip_y=0, flip_x=0, p=None):
+        pc = self.pc
+        return self.view(1 - pc.y if flip_y else pc.y, 1 - pc.x if flip_x else pc.x, pc.z, pc.c, p)
+
+    def four(self, z, c=None):
+        both = slice(None)
+        return self.view(both, both, z, self.pc.c if c is None else c, None)
+
+    def r(self, k, v, dev, src=None):
+        return remote(v if src is None else src, v, self.ss.at[k], self.rs.at[k], dev)
+
+    def loc(self, p):
+        return pltpu.make_async_copy(self.src[p](), self.at(p=p), self.ss.at[14 + p])
+
+    def own(self, p):
+        v, src = self.at(p=p), self.src[p]()
+        return [self.r(p, v, self.pc.xn, src), self.r(2 + p, v, self.pc.yn, src)]
+
+    def s0(self):
+        for p in (0, 1):
+            self.loc(p).start()
+            for c in self.own(p):
+                c.start()
+
+    def s1(self):
+        pc = self.pc
+        self.r(0, self.at(0, 1, 0), pc.xn).wait_recv()
+        self.r(4, self.at(0, 1, 0), pc.yn).start()
+        self.r(3, self.at(1, 0, 1), pc.yn).wait_recv()
+        self.r(5, self.at(1, 0, 1), pc.xn).start()
+
+    def s2(self):
+        pc = self.pc
+        for p in (0, 1):
+            self.loc(p).wait()
+        self.r(1, self.at(0, 1, 1), pc.xn).wait_recv()
+        self.r(2, self.at(1, 0, 0), pc.yn).wait_recv()
+        self.r(4, self.at(1, 1, 0), pc.yn).wait_recv()
+        self.r(5, self.at(1, 1, 1), pc.xn).wait_recv()
+        self.r(9, self.four(pc.z), pc.core).start()
+
+    def piece(self, q):
+        pc = self.pc
+        k, i = lax.rem(q, 3), q // 3
+        v = self.view(i // 2, lax.rem(i, 2), pc.z, pc.c, None)
+        self.r(6 + k, v, (pc.w, lax.rem(pc.z + 1 + k, 4))).start()
+
+    def s3(self):
+        pc = self.pc
+        for k in range(3):
+            self.r(6 + k, self.four(pc.zfrom[k]), pc.zs[k]).wait_recv()
+            self.r(10 + k, self.four(pc.zfrom[k]), pc.core).start()
+
+    def s4(self):
+        pc = self.pc
+        self.r(9, self.four(pc.z, 1 - pc.c), pc.core).wait_recv()
+        for k in range(3):
+            self.r(10 + k, self.four(pc.zfrom[k], 1 - pc.c), pc.core).wait_recv()
+
+    def fin(self):
+        pc = self.pc
+        for p in (0, 1):
+            for c in self.own(p):
+                c.wait_send()
+        self.r(4, self.at(0, 1, 0), pc.yn).wait_send()
+        self.r(5, self.at(1, 0, 1), pc.xn).wait_send()
+        for k in range(3):
+            self.r(6 + k, self.four(pc.z), pc.zs[k]).wait_send()
+            self.r(10 + k, self.four(pc.zfrom[k]), pc.core).wait_send()
+        self.r(9, self.four(pc.z), pc.core).wait_send()
 
 
 NG = 16
@@ -263,7 +339,7 @@
     tok_ref, cot_ref, doc_ref, count_ref, vec_ref, win_s, wout_s, wgate_s, wup_s, wdown_s,
     out_ref, gtok_ref, ggate_o, gup_o, gdown_o, gout_o, gin_o, small_o,
     win_h, wout_h, wd_h, wgu_h, vec_h, bcx_h, hid_h, mix_h, gdown_h,
-    obuf, gn, nf, gf, nm, msk_ref, vec, vown, sm, sml, halo_t, halo_g, edge_s, edge_r,
+    obuf, gn, nf, gf, nm, msk_ref, dlen, vec, vown, sm, sml, halo_t, halo_g, edge_s, edge_r,
     vsem, lsem, hsem, esem, gss, grs, *sc,
 ):
     pc = Place()
@@ -303,6 +379,20 @@
             return down_unit(u - 5)
         return gu_unit(u - 9)
 
+    wd6 = wd_h.reshape(2, 2, 2, 4, ff // 32, dim)
+    wgu7 = wgu_h.reshape(2, 2, 2, 4, 2, 32, ff)
+
+    def down_view(y, x, z, c, p):
+        return wd6.at[y, x, c, z, :, pl.ds(768, 256) if p is None else pl.ds(768 + 128 * p, 128)]
+
+    def gu_view(y, x, z, c, p):
+        return wgu7.at[y, x, c, z, slice(None) if p is None else p, :, pl.ds(ff - f, f)]
+
+    late_down = GatherLate(pc, [lambda: wdown_s.at[:, pl.ds(768, 128)], lambda: wdown_s.at[:, pl.ds(896, 128)]],
+                           down_view, gss.at[8], grs.at[8])
+    late_gu = GatherLate(pc, [lambda: wgate_s.at[0, :, pl.ds(ff - f, f)], lambda: wup_s.at[0, :, pl.ds(ff - f, f)]],
+                         gu_view, gss.at[8 + n], grs.at[8 + n])
+
     def small_copies(k):
         peers = [pc.core, pc.xn, pc.yn] + pc.zs
         return [remote(sm, sml.at[q], esem.at[q], esem.at[6 + q], peers[q]) for q in ((0,), (1,), (2,), (3, 4, 5))[k]]
@@ -319,16 +409,18 @@
             t = t + sml[q]
         sm[...] = t
 
+    turn_of = [0, 1, 2, 3, 4, 5, 6, 7, 9, 10, 11, 12]
+
     def step(t):
-        if t < 11:
-            unit(t).s1()
-            unit(t + AHEAD).s0()
-        if t >= 2 and t < 11:
-            unit(t - 1).s2()
-        if t >= 3 and t < 12:
-            unit(t - 2).s3()
+        if t < 10:
+            unit(turn_of[t]).s1()
+            unit(turn_of[t + AHEAD]).s0()
+        if t >= 2 and t < 10:
+            unit(turn_of[t - 1]).s2()
+        if t >= 3 and t < 11:
+            unit(turn_of[t - 2]).s3()
         if t >= 4:
-            unit(t - 3).s4()
+            unit(turn_of[t - 3]).s4()
 
     ndn = n + 4
     gdown6 = gdown_h.reshape(2, 2, 2, 4, ff // 32, dim)
@@ -381,7 +473,9 @@
     gn[...] = jnp.zeros_like(gn)
     row_devs = ROW_LEN // tok
     row = pc.me // row_devs
-    lens = jnp.broadcast_to(doc_ref[pl.ds(row, 1), :], (8, 128))
+    dlen[...] = jnp.zeros_like(dlen)
+    dlen[0:1, 0:16] = doc_ref[pl.ds(row, 1), :]
+    lens = dlen[...]
     lane = lax.broadcasted_iota(jnp.int32, (8, 128), 1)
     sums = lens
     for k in (1, 2, 4, 8):
@@ -410,10 +504,18 @@
     lax.fori_loop(0, nt_, live_rows, 0)
     unit(0).s1()
     unit(2).s0()
-    unit(0).s2()
-    unit(0).s3()
+    late_down.s0()
+    late_gu.s0()
     unit(1).s1()
     unit(3).s0()
+    unit(0).s2()
+    step(2)
+    unit(0).s3()
+    late_down.s1()
+    late_gu.s1()
+    step(3)
+    late_down.s2()
+    late_down.piece(0)
     unit(0).s4()
 
     def mixer_forward(vbuf, win, wout, st, mst, tb):
@@ -432,12 +534,12 @@
             return 0
 
         lax.fori_loop(0, nt_, normed, 0)
-        step(2)
-        step(3)
         wl = [pltpu.make_async_copy(win_h.at[:, :, pl.ds(1024 * i, 1024)], win.at[i], vsem.at[i]) for i in range(3)]
         wl.append(pltpu.make_async_copy(wout_h, wout, vsem.at[3]))
         for t in (4, 5, 6, 7):
             step(t)
+            late_down.piece(2 * t - 7)
+            late_down.piece(2 * t - 6)
             wl[t - 4].start()
         tail.wait()
         th = halo_t[...].astype(F32)
@@ -476,8 +578,10 @@
             obuf[r, :] = h
             nf[r, :] = (h * inverse_rms(h) * vec[1:2, :]).astype(BF)
             act_on(stash(i, s), "start")
-            for k in range(4):
+            for k in range(3):
                 pl.when(i == k)(functools.partial(step, 8 + k))
+            pl.when(i < 3)(lambda: late_down.piece(9 + i))
+            pl.when(i == 3)(late_down.s3)
             return 0
 
         lax.fori_loop(0, nt_, tile, 0)
@@ -488,7 +592,8 @@
         mixer_forward, pltpu.VMEM((32, 8, 128), F32), pltpu.VMEM((3, 32, 32, dim), BF), pltpu.VMEM((32, 32, dim), BF),
         pltpu.VMEM((2, 3, tt, dim), F32), pltpu.VMEM((2, tt, dim), BF), pltpu.VMEM((tt + 8, dim), F32),
     )
-    step(12)
+    step(11)
+    late_down.s4()
 
     def put(b3, j, s):
         return pltpu.make_async_copy(b3.at[s], gdown_h.at[cols(j), :], vsem.at[s])
@@ -512,8 +617,8 @@
         def body(j, carry):
             s = lax.rem(j, 2)
 
-            def stage(fn, k, lo=0):
-                pl.when(jnp.logical_and(j + k >= lo, j + k < n))(lambda: fn(j + k))
+            def stage(fn, k, lo=0, hi=n):
+                pl.when(jnp.logical_and(j + k >= lo, j + k < hi))(lambda: fn(j + k))
 
             act_on(fetch(j, s), "wait")
 
@@ -536,19 +641,24 @@
                 gn[r, :] += dg(ggv, g_w, 1, 1) + dg(guv, u_w, 1, 1)
 
             tile(0)
-            stage(lambda u: gu_unit(u).s2(), 1, 1)
+            pl.when(jnp.logical_and(j >= 1, j < 7))(lambda: late_gu.piece(2 * j - 2))
+            pl.when(j == n - 2)(late_gu.s3)
+            stage(lambda u: gu_unit(u).s2(), 1, 1, n - 1)
             stage(lambda u: eng_gu.go(2, u), -1)
             tile(1)
             stage(lambda u: eng_gu.go(4, u), -2)
-            stage(lambda u: gu_unit(u).s1(), 2, 2)
-            stage(lambda u: gu_unit(u).s0(), 2 + AHEAD, 2 + AHEAD)
+            stage(lambda u: gu_unit(u).s1(), 2, 2, n - 1)
+            stage(lambda u: gu_unit(u).s0(), 2 + AHEAD, 2 + AHEAD, n - 1)
+            pl.when(j == 0)(late_gu.s2)
+            pl.when(jnp.logical_and(j >= 1, j < 7))(lambda: late_gu.piece(2 * j - 1))
             for i in range(dim // td):
                 x = nt[i * td : (i + 1) * td, :]
                 part[s, 0, i] = dg(x, gg[...], 1, 0).astype(BF).reshape(2, 2, 4, 32, f)
                 part[s, 1, i] = dg(x, gu[...], 1, 0).astype(BF).reshape(2, 2, 4, 32, f)
             eng_gu.begin(j)
-            stage(lambda u: gu_unit(u).s3(), 1, 1)
-            stage(lambda u: gu_unit(u).s4(), 1, 1)
+            stage(lambda u: gu_unit(u).s3(), 1, 1, n - 1)
+            stage(lambda u: gu_unit(u).s4(), 1, 1, n - 1)
+            pl.when(j == n - 2)(late_gu.s4)
             stage(lambda u: act_on(fetch(u, 1 - s), "start"), 1)
             pl.when(j >= 2)(lambda: put(b3, j - 2, s).wait())
             for i in range(f // 256):
@@ -761,14 +871,16 @@
 
     pl.run_scoped(mixer_backward, pltpu.VMEM((tok, 3 * dim), BF), pltpu.VMEM((dim, tok), BF), pltpu.VMEM((32, 32, dim), BF))
 
-    for u in range(9):
+    for u in range(8):
         unit(u).fin()
+    late_down.fin()
+    late_gu.fin()
 
     def last(j, carry):
         gu_unit(j).fin()
         return carry
 
-    lax.fori_loop(0, n, last, 0)
+    lax.fori_loop(0, n - 1, last, 0)
 
 
 def block_call(tokens, cot, lengths, counts, vecs, w_in, w_out, w_gate, w_up, w_down):
@@ -794,6 +906,7 @@
             pltpu.VMEM((tok, dim), BF),
             pltpu.VMEM((tok, dim), BF),
             pltpu.VMEM((tok, 128), F32),
+            pltpu.VMEM((8, 128), jnp.int32),
             pltpu.VMEM((8, dim), F32),
             pltpu.VMEM((1, 8, 128), F32),
             pltpu.VMEM((8, dim), F32),
@@ -1002,9 +1115,8 @@
     own = gain_mix.shape[0]
     vecs = jnp.concatenate([gain_mix[None], gain_ffn[None], conv_taps], axis=0).astype(F32)
     vecs = jnp.pad(vecs, ((0, 3), (0, 128 - own)))
-    lengths = jnp.pad(doc_lengths, ((0, 0), (0, 128 - doc_lengths.shape[1])))
     output, grad_tokens, sum_gate, sum_up, sum_down, sum_out, sum_in, all_small = block_call(
-        tokens, cotangent, lengths, valid_count, vecs, in_weight, out_weight, gate_weight, up_weight, down_weight
+        tokens, cotangent, doc_lengths, valid_count, vecs, in_weight, out_weight, gate_weight, up_weight, down_weight
     )[:8]
     mine = lax.dynamic_slice_in_dim(all_small, me * own, own, 1)
     return (output, grad_tokens, mine[0], sum_in, mine[2:5], sum_out, mine[1], sum_gate, sum_up, sum_down)

time: 374 us -> 366 us (0.979)
  Pallas kernels: 357 us -> 351 us
    pallas_call x1, Pallas kernels: 357 us -> 351 us  [block_call(): pl.pallas_call(block_kernel, out_shape=outs, in_specs=[VM, ANY, VM, pl.Bl...]
where the time goes in v5:
time: 366 us
  Pallas kernels  351 us (96%)
  local copies, waits for them, and re-layouts  12.8 us (3%)
    pallas_call x1, Pallas kernels, block_call(): pl.pallas_call(block_kernel, out_shape=outs, in_specs=[VM, ANY, VM, pl.Bl...  351 us
    unnamed x19, local copies, waits for them, and re-layouts  10.9 us

profile of v5, /device:TPU:0, one launch (start us, length us, event | category | flops | bytes accessed | tf_op | source)
XLA Modules:
  0.0 365.6 jit_solution(8570655973723395614)
XLA Ops:
  0.6 1.3 fusion.9.vec_ref
  1.9 350.8 %block.1 = (f32[1024,1024]{1,0:T(8,128)}, f32[1024,1024]{1,0:T(8,128)}, f32[32,4608]{1,0:T(8,128)}, f32[32,4608]{1,0:T(8,128)}, f32[144,1024]{1,0:T(8,128)}, /*i...) custom-call(bf16[1024,1024]{1,0:T(8,128)(2,1)} %tok_ref.1, ...), custom_call_target="tpu_custom_call" | custom-call | tf_op jit(solution)/shard_map/block/pallas_call | solution.py:897
  352.8 0.8 constant_dynamic-slice_fusion
  353.5 0.5 slice_bitcast_fusion
  354.1 0.6 slice.10
  354.6 0.0 copy-start
  354.7 4.9 %copy.29 = f32[1024,1024]{1,0:T(8,128)} copy(f32[1024,1024]{1,0:T(8,128)} %get-tuple-element.38) | data formatting | bytes 8388608
  359.6 0.0 copy-done
  359.6 0.0 copy-start.4
  359.6 0.0 copy-start.5
  359.6 0.0 copy-start.3
  359.6 0.0 copy-start.2
  359.6 0.0 copy-start.1
  359.6 2.1 copy.30
  361.8 0.0 copy-done.4
  361.8 0.7 copy.31
  362.5 0.0 copy-done.5
  362.5 0.7 copy.32
  363.2 0.0 copy-done.3
  363.2 0.8 copy.33
  364.0 0.0 copy-done.2
  364.0 0.8 copy.34
  364.8 0.0 copy-done.1
  364.8 0.8 copy.35
Async XLA Ops:
  354.6 4.9 %copy-start = (f32[1024,1024]{1,0:T(8,128)S(1)}, f32[1024,1024]{1,0:T(8,128)}, u32[]{:S(2)}) copy-start(f32[1024,1024]{1,0:T(8,128)} %get-tuple-element.39) | copy-start | bytes 12582916
  359.6 2.2 copy-start.4
  359.6 2.9 copy-start.5
  359.6 3.6 copy-start.3
  359.6 4.4 %copy-start.2 = (f32[32,4608]{1,0:T(8,128)S(1)}, f32[32,4608]{1,0:T(8,128)}, u32[]{:S(2)}) copy-start(f32[32,4608]{1,0:T(8,128)} %get-tuple-element.46) | copy-start | bytes 1769476
  359.6 5.2 %copy-start.1 = (f32[144,1024]{1,0:T(8,128)S(1)}, f32[144,1024]{1,0:T(8,128)}, u32[]{:S(2)}) copy-start(f32[144,1024]{1,0:T(8,128)} %get-tuple-element.47) | copy-start | bytes 1769476

commit v6 on v5

--- a/solution.py
+++ b/solution.py
@@ -578,8 +578,8 @@
             obuf[r, :] = h
             nf[r, :] = (h * inverse_rms(h) * vec[1:2, :]).astype(BF)
             act_on(stash(i, s), "start")
-            for k in range(3):
-                pl.when(i == k)(functools.partial(step, 8 + k))
+            for k, t in ((0, 8), (1, 9), (3, 10)):
+                pl.when(i == k)(functools.partial(step, t))
             pl.when(i < 3)(lambda: late_down.piece(9 + i))
             pl.when(i == 3)(late_down.s3)
             return 0
@@ -881,6 +881,38 @@
         return carry
 
     lax.fori_loop(0, n - 1, last, 0)
+
+
+def deliver_kernel(pieces, n, *refs):
+    ins, outs, bufs, sems = refs[:n], refs[n : 2 * n], refs[2 * n : 3 * n], refs[3 * n]
+    every = [(i, r) for i in range(n) for r in pieces[i]]
+    load = [pltpu.make_async_copy(ins[i].at[pl.ds(*r)], bufs[i].at[pl.ds(*r)], sems.at[0, q]) for q, (i, r) in enumerate(every)]
+    store = [pltpu.make_async_copy(bufs[i].at[pl.ds(*r)], outs[i].at[pl.ds(*r)], sems.at[1, q]) for q, (i, r) in enumerate(every)]
+    for c in load:
+        c.start()
+    for c, d in zip(load, store):
+        c.wait()
+        d.start()
+    for d in store:
+        d.wait()
+
+
+def deliver(arrays):
+    n = len(arrays)
+    pieces = []
+    for a in arrays:
+        rows = a.shape[0] // 8 if a.shape[0] % 64 == 0 else a.shape[0]
+        pieces.append([(r, rows) for r in range(0, a.shape[0], rows)])
+    return pl.pallas_call(
+        functools.partial(deliver_kernel, pieces, n),
+        out_shape=[jax.ShapeDtypeStruct(a.shape, a.dtype) for a in arrays],
+        in_specs=[ANY] * n,
+        out_specs=[ANY] * n,
+        scratch_shapes=[pltpu.VMEM(a.shape, a.dtype) for a in arrays]
+        + [pltpu.SemaphoreType.DMA((2, sum(map(len, pieces))))],
+        name="deliver",
+        compiler_params=pltpu.CompilerParams(vmem_limit_bytes=60 * 2**20),
+    )(*arrays)
 
 
 def block_call(tokens, cot, lengths, counts, vecs, w_in, w_out, w_gate, w_up, w_down):
@@ -1118,6 +1150,9 @@
     output, grad_tokens, sum_gate, sum_up, sum_down, sum_out, sum_in, all_small = block_call(
         tokens, cotangent, doc_lengths, valid_count, vecs, in_weight, out_weight, gate_weight, up_weight, down_weight
     )[:8]
+    output, grad_tokens, sum_gate, sum_up, sum_down, sum_out, sum_in = deliver(
+        [output, grad_tokens, sum_gate, sum_up, sum_down, sum_out, sum_in]
+    )
     mine = lax.dynamic_slice_in_dim(all_small, me * own, own, 1)
     return (output, grad_tokens, mine[0], sum_in, mine[2:5], sum_out, mine[1], sum_gate, sum_up, sum_down)
 

time: 366 us -> 361 us (0.986)
  local copies, waits for them, and re-layouts: 12.8 us -> 1.86 us
  Pallas kernels: 351 us -> 357 us
    unnamed x19 -> x0, local copies, waits for them, and re-layouts: 10.9 us -> none
    pallas_call x0 -> x1, Pallas kernels: none -> 8.12 us  [deliver(): pl.pallas_call(functools.partial(deliver_kernel, pieces, n), out_shape=[j...]
where the time goes in v6:
time: 361 us
  Pallas kernels  357 us (99%)
    pallas_call x1, Pallas kernels, block_call(): pl.pallas_call(block_kernel, out_shape=outs, in_specs=[VM, ANY, VM, pl.Bl...  349 us
    pallas_call x1, Pallas kernels, deliver(): pl.pallas_call(functools.partial(deliver_kernel, pieces, n), out_shape=[j...  8.12 us

profile of v6, /device:TPU:0, one launch (start us, length us, event | category | flops | bytes accessed | tf_op | source)
XLA Modules:
  0.0 360.6 jit_solution(18171575814922337531)
XLA Ops:
  0.6 1.3 fusion.9.vec_ref
  1.9 348.7 %block.1 = (f32[1024,1024]{1,0:T(8,128)}, f32[1024,1024]{1,0:T(8,128)}, f32[32,4608]{1,0:T(8,128)}, f32[32,4608]{1,0:T(8,128)}, f32[144,1024]{1,0:T(8,128)}, /*i...) custom-call(bf16[1024,1024]{1,0:T(8,128)(2,1)} %tok_ref.1, ...), custom_call_target="tpu_custom_call" | custom-call | tf_op jit(solution)/shard_map/block/pallas_call | solution.py:929
  350.6 8.1 %deliver.1 = (f32[1024,1024]{1,0:T(8,128)}, f32[1024,1024]{1,0:T(8,128)}, f32[32,4608]{1,0:T(8,128)}, f32[32,4608]{1,0:T(8,128)}, f32[144,1024]{1,0:T(8,128)}, /*index=5*/f32[32,1024]{1,0:T(8,128)}, f32[32,3072]{1,0:T(8,128)}) custom-call(f32[1024,1024]{1,0:T(8,128)} %get-tuple-element.25.refs_0_, f32[1024,1024]{1,0:T(8,128)} %get-tuple-element.26.refs_1_, ...), custom_call_target="tpu_custom_call" | custom-call | tf_op jit(solution)/shard_map/deliver/pallas_call | solution.py:906
  358.8 0.8 constant_dynamic-slice_fusion
  359.5 0.5 slice_bitcast_fusion
  360.0 0.6 slice.10

commit v7 on v6

--- a/solution.py
+++ b/solution.py
@@ -645,9 +645,9 @@
             pl.when(j == n - 2)(late_gu.s3)
             stage(lambda u: gu_unit(u).s2(), 1, 1, n - 1)
             stage(lambda u: eng_gu.go(2, u), -1)
+            stage(lambda u: gu_unit(u).s1(), 2, 2, n - 1)
             tile(1)
             stage(lambda u: eng_gu.go(4, u), -2)
-            stage(lambda u: gu_unit(u).s1(), 2, 2, n - 1)
             stage(lambda u: gu_unit(u).s0(), 2 + AHEAD, 2 + AHEAD, n - 1)
             pl.when(j == 0)(late_gu.s2)
             pl.when(jnp.logical_and(j >= 1, j < 7))(lambda: late_gu.piece(2 * j - 1))
@@ -664,8 +664,8 @@
             for i in range(f // 256):
                 b3[s, i * 256 : (i + 1) * 256, :] = dg(act[:, i * 256 : (i + 1) * 256].T, gf[...], 1, 0).astype(BF)
             put(b3, j, s).start()
+            stage(lambda u: eng_gu.go(3, u), -1)
             eng_gu.go(1, j)
-            stage(lambda u: eng_gu.go(3, u), -1)
             stage(lambda u: eng_gu.end(u), -2)
             return carry
 
@@ -704,7 +704,7 @@
         wcopy.wait()
 
         def advance(u):
-            for k, stage in ((0, 1), (1, 2), (2, 3), (3, 4)):
+            for k, stage in ((1, 2), (0, 1), (2, 3), (3, 4)):
                 if u - k < ndn + 5:
                     eng(u - k).go(stage, u - k)
 
@@ -758,8 +758,8 @@
                 u = n + i
                 s = lax.rem(i, 2)
                 r = cols(i, tt)
+                eng_mid.go(2, u - 1)
                 eng_mid.go(1, u)
-                eng_mid.go(2, u - 1)
                 pl.when(i >= 1)(lambda: eng_mid.go(3, u - 2))
                 pl.when(i != 1)(lambda: eng_mid.go(4, jnp.where(i == 0, n - 2, u - 3)))
                 pl.when(i + 1 < nt_)(lambda: act_on(load_mid(u + 1), "start"))

time: 361 us -> 360 us (level)
  no operation moved by 1% of the time
where the time goes in v7:
time: 360 us
  Pallas kernels  356 us (99%)
    pallas_call x1, Pallas kernels, block_call(): pl.pallas_call(block_kernel, out_shape=outs, in_specs=[VM, ANY, VM, pl.Bl...  348 us
    pallas_call x1, Pallas kernels, deliver(): pl.pallas_call(functools.partial(deliver_kernel, pieces, n), out_shape=[j...  8.12 us

profile of v7, /device:TPU:0, one launch (start us, length us, event | category | flops | bytes accessed | tf_op | source)
XLA Modules:
  0.0 359.9 jit_solution(3638324188378807272)
XLA Ops:
  0.6 1.3 fusion.9.vec_ref
  1.9 348.0 %block.1 = (f32[1024,1024]{1,0:T(8,128)}, f32[1024,1024]{1,0:T(8,128)}, f32[32,4608]{1,0:T(8,128)}, f32[32,4608]{1,0:T(8,128)}, f32[144,1024]{1,0:T(8,128)}, /*i...) custom-call(bf16[1024,1024]{1,0:T(8,128)(2,1)} %tok_ref.1, ...), custom_call_target="tpu_custom_call" | custom-call | tf_op jit(solution)/shard_map/block/pallas_call | solution.py:929
  349.9 8.1 %deliver.1 = (f32[1024,1024]{1,0:T(8,128)}, f32[1024,1024]{1,0:T(8,128)}, f32[32,4608]{1,0:T(8,128)}, f32[32,4608]{1,0:T(8,128)}, f32[144,1024]{1,0:T(8,128)}, /*index=5*/f32[32,1024]{1,0:T(8,128)}, f32[32,3072]{1,0:T(8,128)}) custom-call(f32[1024,1024]{1,0:T(8,128)} %get-tuple-element.25.refs_0_, f32[1024,1024]{1,0:T(8,128)} %get-tuple-element.26.refs_1_, ...), custom_call_target="tpu_custom_call" | custom-call | tf_op jit(solution)/shard_map/deliver/pallas_call | solution.py:906
  358.1 0.8 constant_dynamic-slice_fusion
  358.8 0.5 slice_bitcast_fusion
  359.4 0.6 slice.10
